TPU v7x, 128 devices: a whole 4x4x4 slice. The times are simulated.
128 devices in a mesh: pts: 8 (over x, core), shk: 16 (over z, y).
Axes of the slice: x: 4, y: 4, z: 4, core: 2. Of those that a mesh axis runs over, the one named last changes fastest.
Arguments:
- savings: float32 [16, 59, 1024], P('shk', None, 'pts'), may hold values from 0.05 to 0.95
- wealth: float32 [16, 59, 1024], P('shk', None, 'pts'), may hold values from 0.5 to 2
- surplus: bfloat16 [16, 118, 2048], P('shk', None, 'pts'), may hold values from -0.12 to 0.12
- point_dims: int32 [16, 3, 2048], P('shk', None, 'pts'), may hold values from 0 to 58
- point_levels: int32 [16, 3, 2048], P('shk', None, 'pts'), may hold values from 0 to 3
- point_index: int32 [16, 3, 2048], P('shk', None, 'pts'), may hold values from 1 to 7, as said below
- live_count: int32 [16, 8], P('shk', 'pts'), may hold values from 64 to 256
- trans_counts: int32 [16, 16], replicated, may hold values from 1 to 99
Outputs:
- savings_out: float32 [16, 59, 1024], P('shk', None, 'pts')
- consumption: float32 [16, 59, 1024], P('shk', None, 'pts')
Inputs may be any that keep to these rules, and one draw needn't show every extreme that they name: `point_index`: odd, below 2 ** level where the level is positive, 1 where it is 0. Points at positions from live_count on in a shard are padding.
All inputs are finite; a program needn't handle non-finite values.
Results may differ from a plain program's by a relative error of at most 0.0011.
Values may be sent and summed in bfloat16 or wider, within the bound.
No kernel may reach another device: no remote copies, remote signals or barrier semaphores. Data moves between devices by JAX's collectives and lax.ppermute only.
A program may use at most 192 MiB of HBM per device.

v0:
```python
import jax
import jax.numpy as jnp
from jax import lax
from jax.sharding import PartitionSpec as P

ITERS = 2


GAMMA = 2.0
BETA = 0.96
damping = 0.5
query_block = 2048


def hat_tables(levels, indices):
    scaled = jnp.exp2(levels.astype(jnp.float32))
    inverse = jnp.where(levels > 0, scaled, jnp.zeros_like(scaled))
    centre = indices.astype(jnp.float32) / scaled
    return (centre, inverse)


def basis_block(coords, dims, centre, inverse):
    chosen = jnp.take(coords, dims, axis=0)
    factor = jnp.maximum(0.0, 1.0 - jnp.abs(chosen - centre[:, :, None]) * inverse[:, :, None])
    product = factor[0]
    for slot in range(1, factor.shape[0]):
        product = product * factor[slot]
    return product.astype(jnp.bfloat16)


def make_evaluate(weights, dims, centre, inverse):

    def block_eval(coords):
        basis = basis_block(coords, dims, centre, inverse)
        return jnp.dot(weights, basis, preferred_element_type=jnp.float32)

    def evaluate(piece, start):
        coords = piece.astype(jnp.float32)
        breadth = coords.shape[1]
        stacked = coords.reshape(coords.shape[0], breadth // query_block, query_block).transpose(
            1, 0, 2
        )
        results = lax.map(block_eval, stacked)
        return results.transpose(1, 0, 2).reshape(results.shape[1], breadth)

    return evaluate


def per_device(
    savings, wealth, surplus, point_dims, point_levels, point_index, live_count, trans_counts
):
    npoints = surplus.shape[2]
    live = live_count[0, 0]
    position = lax.iota(jnp.int32, npoints)
    live_surplus = jnp.where(position[None, :] < live, surplus[0], jnp.zeros_like(surplus[0]))
    counts = trans_counts.astype(jnp.float32)
    prob = counts / jnp.sum(counts, axis=1, keepdims=True)
    shock = lax.axis_index("shk")
    shk_count = lax.axis_size("shk")
    current = savings[0]
    income = wealth[0]
    dimension = current.shape[0]
    nquery = current.shape[1]
    centre, inverse = hat_tables(point_levels[0], point_index[0])
    evaluate = make_evaluate(live_surplus, point_dims[0], centre, inverse)
    consumption = current
    for sweep in range(ITERS):
        query = current.astype(jnp.bfloat16)
        partial_value = evaluate(
            lax.all_gather(query, ("pts", "shk"), axis=1, tiled=True), jnp.int32(0)
        )
        mine = lax.psum_scatter(partial_value, "pts", scatter_dimension=1, tiled=True)
        marginal = jnp.exp(-GAMMA * mine[:dimension] + mine[dimension:]).reshape(
            dimension, shk_count, nquery
        )
        column = lax.dynamic_index_in_dim(prob, shock, 1, keepdims=False)
        terms = marginal * column[None, :, None]
        expect = lax.psum_scatter(terms, "shk", scatter_dimension=1, tiled=True)[:, 0, :]
        consumption = (BETA * expect) ** (-1.0 / GAMMA)
        current = (1.0 - damping) * current + damping * jax.nn.sigmoid(income - consumption)
    return (current[None], consumption[None])


def solution(mesh):
    return jax.shard_map(
        per_device,
        mesh=mesh,
        in_specs=(
            P("shk", None, "pts"),
            P("shk", None, "pts"),
            P("shk", None, "pts"),
            P("shk", None, "pts"),
            P("shk", None, "pts"),
            P("shk", None, "pts"),
            P("shk", "pts"),
            P(),
        ),
        out_specs=(P("shk", None, "pts"), P("shk", None, "pts")),
        check_vma=False,
    )
```

profile of v0, /device:TPU:0, one launch (start us, length us, event | category | flops | bytes accessed | tf_op | source)
XLA Modules:
  0.0 647.0 jit_solution(12382082039239027195)
XLA Ops:
  11.5 66.2 %all-gather.3.cloned.1.call-done = bf16[59,16384]{1,0:T(8,128)(2,1)} async-done(((bf16[59,128]{1,0:T(8,128)(2,1)}), bf16[59,16384]{1,0:T(8,128)(2,1)}) %all-gather.3.cloned.1.call-update) | async-done | bytes 1933328 | tf_op jit(solution)/shard_map/all_gather | solution.py:70
  90.8 89.7 %while.20 = (s32[]{:T(128)}, f32[8,118,2048]{2,1,0:T(8,128)}, f32[8,59,2048]{2,1,0:T(8,128)}, s32[3,256]{1,0:T(4,128)S(1)}, f32[3,256]{1,0:T(4,128)S(1)}, /*inde...) while((s32[]{:T(128)}, f32[8,118,2048]{2,1,0:T(8,128)}, f32[8,59,2048]{2,1,0:T(8,128)}, ...), condition=%wide.region_1.3_spmd, body=%wide.region_0.0_spmd.sunk | while | flops 134749952 | bytes 33501272 | solution.py:43
  91.9 5.0 gather_fusion
  103.1 5.0 gather_fusion
  114.3 5.0 gather_fusion
  125.5 5.0 gather_fusion
  136.7 5.0 gather_fusion
  147.9 5.0 gather_fusion
  159.1 5.0 gather_fusion
  170.3 5.0 gather_fusion
  180.5 7.7 %copy.26 = f32[118,8,2048]{2,1,0:T(8,128)S(1)} copy(f32[118,8,2048]{2,0,1:T(8,128)} %bitcast.15) | data formatting | bytes 15466496 | tf_op jit(solution)/shard_map/transpose | solution.py:44
  189.2 9.0 %copy.40 = f32[15,8,8,2048]{3,1,2,0:T(8,128)} copy(f32[15,8,8,2048]{3,2,1,0:T(8,128)S(1)} %bitcast.133) | data formatting | bytes 15728640
  199.2 48.4 %reduce-scatter.9.cloned.1.call-done = f32[118,2048]{1,0:T(8,128)} async-done(((f32[118,16384]{1,0:T(8,128)}), f32[118,2048]{1,0:T(8,128)}) %reduce-scatter.9.cloned.1.call-update) | async-done | bytes 966672 | tf_op jit(solution)/shard_map/reduce_scatter | solution.py:72
  250.2 74.0 %reduce-scatter.13.cloned.1.call-done = f32[59,1,128]{2,0,1:T(8,128)} async-done(((f32[59,16,128]{2,0,1:T(8,128)}), f32[59,1,128]{2,0,1:T(8,128)}) %reduce-scatter.13.cloned.1.call-update) | async-done | bytes 30224
  325.7 64.9 %all-gather.5.cloned.1.call-done = bf16[59,16384]{1,0:T(8,128)(2,1)} async-done(((bf16[59,128]{1,0:T(8,128)(2,1)}), bf16[59,16384]{1,0:T(8,128)(2,1)}) %all-gather.5.cloned.1.call-update) | async-done | bytes 1933328 | tf_op jit(solution)/shard_map/all_gather | solution.py:70
  403.6 89.8 %while.21 = (s32[]{:T(128)}, f32[8,118,2048]{2,1,0:T(8,128)}, f32[8,59,2048]{2,1,0:T(8,128)}, s32[3,256]{1,0:T(4,128)S(1)}, f32[3,256]{1,0:T(4,128)S(1)}, /*inde...) while((s32[]{:T(128)}, f32[8,118,2048]{2,1,0:T(8,128)}, f32[8,59,2048]{2,1,0:T(8,128)}, ...), condition=%wide.region_6.8_spmd, body=%wide.region_5.7_spmd.sunk | while | flops 134749952 | bytes 33501272 | solution.py:43
  404.7 5.0 gather_fusion.1
  415.9 5.0 gather_fusion.1
  438.3 5.0 gather_fusion.1
  483.1 5.0 gather_fusion.1
  493.4 7.7 %copy.31 = f32[118,8,2048]{2,1,0:T(8,128)S(1)} copy(f32[118,8,2048]{2,0,1:T(8,128)} %bitcast.19) | data formatting | bytes 15466496 | tf_op jit(solution)/shard_map/transpose | solution.py:44
  502.1 9.0 %copy.43 = f32[15,8,8,2048]{3,1,2,0:T(8,128)} copy(f32[15,8,8,2048]{3,2,1,0:T(8,128)S(1)} %bitcast.132) | data formatting | bytes 15728640
  511.2 49.4 %reduce-scatter.11.cloned.1.call-done = f32[118,2048]{1,0:T(8,128)} async-done(((f32[118,16384]{1,0:T(8,128)}), f32[118,2048]{1,0:T(8,128)}) %reduce-scatter.11.cloned.1.call-update) | async-done | bytes 966672 | tf_op jit(solution)/shard_map/reduce_scatter | solution.py:72
  563.0 73.9 %reduce-scatter.15.cloned.1.call-done = f32[59,1,128]{2,0,1:T(8,128)} async-done(((f32[59,16,128]{2,0,1:T(8,128)}), f32[59,1,128]{2,0,1:T(8,128)}) %reduce-scatter.15.cloned.1.call-update) | async-done | bytes 30224
  (169 shorter events, 160.4 us)
Async XLA Ops:
  7.2 70.6 %all-gather.3.cloned.1.call-start = ((), (), s32[]{:S(2)}) async-start(), calls=%async_computation.4 | async-start | bytes 2113536 | tf_op jit(solution)/shard_map/all_gather | solution.py:70
  8.6 239.1 %reduce-scatter.9.cloned.1.call-start = ((), (), s32[]{:S(2)}) async-start(), calls=%async_computation.5 | async-start | bytes 8847360 | tf_op jit(solution)/shard_map/reduce_scatter | solution.py:72
  198.2 0.7 copy-start.3
  198.2 126.0 %copy-start = (f32[1,59,128]{2,0,1:T(1,128)S(1)}, f32[1,59,128]{2,0,1:T(1,128)}, u32[]{:S(2)}) copy-start(f32[1,59,128]{2,0,1:T(1,128)} %param.14) | copy-start | bytes 90628
  198.2 126.0 %copy-start.2 = (f32[1,59,128]{2,0,1:T(1,128)S(1)}, f32[1,59,128]{2,0,1:T(1,128)}, u32[]{:S(2)}) copy-start(f32[1,59,128]{2,0,1:T(1,128)} %param.15) | copy-start | bytes 90628
  198.3 125.9 %reduce-scatter.13.cloned.1.call-start = ((), (), s32[]{:S(2)}) async-start(), calls=%async_computation.8 | async-start | bytes 557056
  250.1 140.4 %all-gather.5.cloned.1.call-start = ((), (), s32[]{:S(2)}) async-start(), calls=%async_computation.6 | async-start | bytes 2113536 | tf_op jit(solution)/shard_map/all_gather | solution.py:70
  325.6 234.9 %reduce-scatter.11.cloned.1.call-start = ((), (), s32[]{:S(2)}) async-start(), calls=%async_computation.7 | async-start | bytes 8847360 | tf_op jit(solution)/shard_map/reduce_scatter | solution.py:72
  511.1 125.8 %copy-start.1 = (f32[59,1,128]{2,0,1:T(8,128)S(1)}, f32[59,1,128]{2,0,1:T(8,128)}, u32[]{:S(2)}) copy-start(f32[59,1,128]{2,0,1:T(8,128)} %reduce-scatter.13.cloned.1.call-done) | copy-start | bytes 90628
  511.1 125.8 %reduce-scatter.15.cloned.1.call-start = ((), (), s32[]{:S(2)}) async-start(), calls=%async_computation.9 | async-start | bytes 557056
Sparse Core Ops, SparseCore 0:
  11.3 66.3 all-gather.2
  198.4 49.2 reduce-scatter.8
  250.8 73.2 reduce-scatter.12
  327.4 63.0 all-gather.4
  511.2 49.2 reduce-scatter.10
  563.6 73.2 reduce-scatter.14
where the time goes:
time: 655 us; the launch traced here: 647 us
  waiting for transfers between devices  377 us (58%)
  local copies, waits for them, and re-layouts  160 us (24%)
  other arithmetic  71.1 us (11%)
  matrix products  22.8 us (3%)
  between operations  15.3 us (2%)
    unnamed x8, waiting for transfers between devices  148 us
    all_gather x2, waiting for transfers between devices, per_device(): lax.all_gather(query, ('pts', 'shk'), axis=1, tiled=True)  131 us
    reduce_scatter x2, waiting for transfers between devices, per_device(): lax.psum_scatter(partial_value, 'pts', scatter_dimension=1, tiled=True)  97.8 us
    gather x16, local copies, waits for them, and re-layouts, basis_block(): chosen = jnp.take(coords, dims, axis=0)  80.3 us
    max x16, other arithmetic, basis_block(): jnp.maximum(0.0, 1.0 - jnp.abs(chosen - centre[:, :, None]) * inverse[:,...  57.7 us
    unnamed x20, local copies, waits for them, and re-layouts  29 us
    dot_general x16, matrix products, block_eval(): return jnp.dot(weights, basis, preferred_element_type=jnp.float32)  22.8 us
    squeeze x16, local copies, waits for them, and re-layouts, evaluate(): results = lax.map(block_eval, stacked)  17.2 us
  transfers between devices with their start and end apart: 6, of which 6 were waited for; matrix products, arithmetic and copies ran while one was open for 0% of the time, Pallas kernels for 0%

commit v1 on v0

v1 whole, which is shorter than its diff:
```python
import functools

import jax
import jax.numpy as jnp
from jax import lax
from jax.experimental import pallas as pl
from jax.experimental.pallas import tpu as pltpu
from jax.sharding import PartitionSpec as P

ITERS = 2
GAMMA = 2.0
BETA = 0.96
damping = 0.5
DIM = 59
HALF = 64
RING = 4
BF = jnp.bfloat16
F32 = jnp.float32


def pack(surplus, dims, levels, index, live):
    npoints = surplus.shape[1]
    position = lax.iota(jnp.int32, npoints)
    kept = jnp.where(position[None, :] < live, surplus, jnp.zeros_like(surplus))
    refined = levels > 0
    scale = jnp.where(refined, jnp.exp2(levels.astype(F32)), 0.0).astype(BF)
    bias = jnp.where(refined, 1 - index, 1).astype(BF)
    which = dims.astype(BF)
    return jnp.concatenate(
        [kept[:DIM], which, scale[:2], kept[DIM:], scale[2:], bias, jnp.zeros((1, npoints), BF)], axis=0
    )


def kernel(where_ref, counts_ref, tab_ref, q0, q1, q2, q3, o0, o1, o2, o3, qt_ref, acc_ref, sum_ref):
    z, y = where_ref[0], where_ref[1]
    for j, q in enumerate((q0, q1, q2, q3)):
        qt_ref[pl.ds(j * 128, 128), :] = q[...].astype(F32).T.astype(BF)
    row = lax.broadcasted_iota(jnp.int32, (HALF, 256), 0)
    for yy in range(RING):
        acc_ref[...] = jnp.zeros_like(acc_ref)

        @pl.loop(0, 8)
        def _(p):
            blk = tab_ref[p * RING + yy]
            par = jnp.concatenate([blk[56:64], blk[120:128]], axis=0).astype(F32)
            basis = None
            for k in range(3):
                dim = par[3 + k : 4 + k].astype(jnp.int32)
                scale = par[6 + k : 7 + k] if k < 2 else par[11:12]
                bias = par[12 + k : 13 + k]
                table = jnp.where(row == dim, scale, jnp.where(row == DIM, bias, 0.0)).astype(BF)
                left = jnp.dot(qt_ref[...], table, preferred_element_type=F32)
                factor = jnp.maximum(jnp.minimum(left, 2.0 - left), 0.0)
                basis = factor if basis is None else basis * factor
            acc_ref[...] += lax.dot_general(
                basis.astype(BF), blk, (((1,), (1,)), ((), ())), preferred_element_type=F32
            )

        value = acc_ref[...]
        marginal = jnp.exp(-GAMMA * value[:, :HALF] + value[:, HALF:])
        for j in range(RING):
            s = lax.rem(z + j, RING) * RING + y
            count = counts_ref[s, z * RING + yy].astype(F32)
            term = count * marginal[j * 128 : (j + 1) * 128]
            if yy == 0:
                sum_ref[j] = term
            else:
                sum_ref[j] += term
    for j, o in enumerate((o0, o1, o2, o3)):
        o[...] = sum_ref[j].T


def partial_sums(where, counts, tables, queries):
    vm = pl.BlockSpec(memory_space=pltpu.VMEM)
    sm = pl.BlockSpec(memory_space=pltpu.SMEM)
    return pl.pallas_call(
        kernel,
        out_shape=[jax.ShapeDtypeStruct((HALF, 128), F32)] * RING,
        in_specs=[sm, sm, vm, vm, vm, vm, vm],
        out_specs=[vm] * RING,
        scratch_shapes=[
            pltpu.VMEM((512, HALF), BF),
            pltpu.VMEM((512, 128), F32),
            pltpu.VMEM((RING, 128, HALF), F32),
        ],
        compiler_params=pltpu.CompilerParams(vmem_limit_bytes=40 << 20),
        name="euler_basis",
    )(where, counts, tables, *queries)


def shift(dz):
    return [(z * RING + y, (z + dz) % RING * RING + y) for z in range(RING) for y in range(RING)]


def per_device(savings, wealth, surplus, point_dims, point_levels, point_index, live_count, trans_counts):
    block = pack(surplus[0], point_dims[0], point_levels[0], point_index[0], live_count[0, 0])
    groups = [
        [p * 16 + z * RING + y for p in range(8) for y in range(RING)] for z in range(RING)
    ]
    tables = lax.all_to_all(
        jnp.broadcast_to(block[None], (32,) + block.shape), ("pts", "shk"), 0, 0, tiled=True, axis_index_groups=groups
    )
    shock = lax.axis_index("shk")
    where = jnp.stack([shock // RING, shock % RING]).astype(jnp.int32)
    rowsum = jnp.sum(lax.dynamic_index_in_dim(trans_counts, shock, 0, keepdims=False).astype(F32))
    current = savings[0]
    income = wealth[0]
    nq = current.shape[1]
    consumption = current
    for sweep in range(ITERS):
        own = jnp.concatenate(
            [current.astype(BF), jnp.ones((1, nq), BF), jnp.zeros((HALF - DIM - 1, nq), BF)], axis=0
        )
        queries = [own] + [lax.ppermute(own, "shk", shift(-j)) for j in range(1, RING)]
        parts = partial_sums(where, trans_counts, tables, queries)
        got = [parts[0]] + [lax.ppermute(parts[j], "shk", shift(j)) for j in range(1, RING)]
        expect = ((got[0] + got[1]) + (got[2] + got[3]))[:DIM] / rowsum
        consumption = (BETA * expect) ** (-1.0 / GAMMA)
        current = (1.0 - damping) * current + damping * jax.nn.sigmoid(income - consumption)
    return (current[None], consumption[None])


def solution(mesh):
    return jax.shard_map(
        per_device,
        mesh=mesh,
        in_specs=(
            P("shk", None, "pts"),
            P("shk", None, "pts"),
            P("shk", None, "pts"),
            P("shk", None, "pts"),
            P("shk", None, "pts"),
            P("shk", None, "pts"),
            P("shk", "pts"),
            P(),
        ),
        out_specs=(P("shk", None, "pts"), P("shk", None, "pts")),
        check_vma=False,
    )
```

time: 655 us -> 106 us (0.16); the launches traced: 647 us -> 106 us
  waiting for transfers between devices: 377 us -> 34.7 us
  local copies, waits for them, and re-layouts: 160 us -> 3.11 us
  other arithmetic: 71.1 us -> 5.24 us
  Pallas kernels: 0 us -> 37.2 us
  starting transfers between devices: 0.46 us -> 24.3 us
  matrix products: 22.8 us -> 0 us
  between operations: 15.3 us -> 1.42 us
    unnamed x8 -> x0, waiting for transfers between devices: 148 us -> none
    all_gather x2 -> x0, waiting for transfers between devices: 131 us -> none  [per_device(): lax.all_gather(query, ('pts', 'shk'), axis=1, tiled=True)]
    reduce_scatter x2 -> x0, waiting for transfers between devices: 97.8 us -> none  [per_device(): lax.psum_scatter(partial_value, 'pts', scatter_dimension=1, tiled=True)]
    gather x16 -> x0, local copies, waits for them, and re-layouts: 80.3 us -> none  [basis_block(): chosen = jnp.take(coords, dims, axis=0)]
    max x16 -> x0, other arithmetic: 57.7 us -> none  [basis_block(): jnp.maximum(0.0, 1.0 - jnp.abs(chosen - centre[:, :, None]) * inverse[:,...]
    pallas_call x0 -> x2, Pallas kernels: none -> 37.2 us  [partial_sums(): pl.pallas_call(kernel, out_shape=[jax.ShapeDtypeStruct((HALF, 128), F32)]...]
    unnamed x20 -> x11, local copies, waits for them, and re-layouts: 29 us -> 1.31 us
    transpose x6 -> x0, local copies, waits for them, and re-layouts: 24.7 us -> none  [the longest x2 15.4 us: evaluate(): return results.transpose(1, 0, 2).reshape(results.shape[1], breadth)]
  transfers between devices with their start and end apart: 6 -> 13, of which waited for: 6 -> 10; matrix products, arithmetic and copies ran while one was open for 0% -> 1% of each run, Pallas kernels for 0% -> 0%
where the time goes in v1:
time: 106 us
  Pallas kernels  37.2 us (35%)
  waiting for transfers between devices  34.7 us (33%)
  starting transfers between devices  24.3 us (23%)
  other arithmetic  5.24 us (5%)
  local copies, waits for them, and re-layouts  3.11 us (3%)
  between operations  1.42 us (1%)
    pallas_call x2, Pallas kernels, partial_sums(): pl.pallas_call(kernel, out_shape=[jax.ShapeDtypeStruct((HALF, 128), F32)]...  37.2 us
    all_to_all x1, waiting for transfers between devices, per_device(): lax.all_to_all(jnp.broadcast_to(block[None], (32,) + block.shape), ('pts'...  18.7 us
    ppermute x6, starting transfers between devices, per_device(): lax.ppermute(own, 'shk', shift(-j))  8.82 us
    ppermute x6, waiting for transfers between devices, per_device(): lax.ppermute(parts[j], 'shk', shift(j))  8.54 us
    ppermute x6, starting transfers between devices, per_device(): lax.ppermute(parts[j], 'shk', shift(j))  7.97 us
    all_to_all x1, starting transfers between devices, per_device(): lax.all_to_all(jnp.broadcast_to(block[None], (32,) + block.shape), ('pts'...  7.56 us
    ppermute x6, waiting for transfers between devices, per_device(): lax.ppermute(own, 'shk', shift(-j))  7.53 us
  transfers between devices with their start and end apart: 13, of which 10 were waited for; matrix products, arithmetic and copies ran while one was open for 1% of the time, Pallas kernels for 0%

profile of v1, /device:TPU:0, one launch (start us, length us, event | category | flops | bytes accessed | tf_op | source)
XLA Modules:
  0.0 106.1 jit_solution(704770774306614091)
XLA Ops:
  0.6 0.8 fusion.17
  2.1 0.8 bitcast_select_fusion
  3.0 0.7 fusion.18
  4.4 1.6 %broadcast_in_dim.37 = bf16[32,128,256]{2,1,0:T(8,128)(2,1)} broadcast(bf16[128,256]{1,0:T(8,128)(2,1)S(1)} %concatenate.9), dimensions={1,2} | broadcast | bytes 2162688 | tf_op jit(solution)/shard_map/broadcast_in_dim | solution.py:101
  6.0 7.6 %all-to-all-start = ((bf16[32,128,256]{2,1,0:T(8,128)(2,1)}), bf16[32,128,256]{2,1,0:T(8,128)(2,1)S(1)}, u32[]{:S(2)}, u32[]{:S(2)}) async-start(bf16[32,128,256]{2,1,0:T(8,128)(2,1)} %broadcast_in_dim.37), calls=%async_computation | async-start | bytes 4194304 | tf_op jit(solution)/shard_map/all_to_all | solution.py:100
  13.9 4.1 %collective-permute-start = (bf16[64,128]{1,0:T(8,128)(2,1)S(1)}, bf16[64,128]{1,0:T(8,128)(2,1)S(1)}, u32[]{:S(2)}, u32[]{:S(2)}) collective-permute-start(bf16[64,128]{1,0:T(8,128)(2,1)S(1)} %maximum_maximum_fusion.q0), channel_id=1, source_target_pairs={{0,12},{1,13},{2,14},{3,15},{4,0},{5,1},{6,2},{7,3},{8,4},{9,5},{1... | collective-permute-start | bytes 49160 | tf_op jit(solution)/shard_map/ppermute | solution.py:114
  18.0 1.3 %collective-permute-start.2 = (bf16[64,128]{1,0:T(8,128)(2,1)S(1)}, bf16[64,128]{1,0:T(8,128)(2,1)S(1)}, u32[]{:S(2)}, u32[]{:S(2)}) collective-permute-start(bf16[64,128]{1,0:T(8,128)(2,1)S(1)} %maximum_maximum_fusion.q0), channel_id=1, source_target_pairs={{0,4},{1,5},{2,6},{3,7},{4,8},{5,9},{6,10},{7,11},{8,12},{9,13},{1... | collective-permute-start | bytes 49160 | tf_op jit(solution)/shard_map/ppermute | solution.py:114
  19.4 3.8 %collective-permute-done.1.q2 = bf16[64,128]{1,0:T(8,128)(2,1)S(1)} collective-permute-done((bf16[64,128]{1,0:T(8,128)(2,1)S(1)}, bf16[64,128]{1,0:T(8,128)(2,1)S(1)}, u32[]{:S(2)}, u32[]{:S(2)}) %collective-permute-start.1) | collective-permute-done | bytes 16416 | tf_op jit(solution)/shard_map/ppermute | solution.py:114
  23.2 18.7 %all-to-all-done.tab_ref = bf16[32,128,256]{2,1,0:T(8,128)(2,1)S(1)} async-done(((bf16[32,128,256]{2,1,0:T(8,128)(2,1)}), bf16[32,128,256]{2,1,0:T(8,128)(2,1)S(1)}, u32[]{:S(2)}, u32[]{:S(2)}) %all-to-all-start) | async-done | bytes 2097184 | tf_op jit(solution)/shard_map/all_to_all | solution.py:100
  41.9 18.6 %euler_basis.2 = (f32[64,128]{1,0:T(8,128)S(1)}, f32[64,128]{1,0:T(8,128)S(1)}, f32[64,128]{1,0:T(8,128)S(1)}, f32[64,128]{1,0:T(8,128)S(1)}) custom-call(s32[2]{0:T(128)S(1)} %pad_add_fusion.where_ref, s32[16,16]{1,0:T(8,128)S(1)} %copy-done, bf16[32,128,256]{2,1,0:T(8,128)(2,1)S(1)} %all-to-all-done.tab_ref, bf16[64,128]{1,0:T(8,128)(2,1)S(1)} %maximum_maximum_fusion.q0, ...), custom_call_target="tpu_custom_call" | custom-call | tf_op jit(solution)/shard_map/euler_basis/pallas_call | solution.py:76
  60.5 4.1 %collective-permute-start.5 = (f32[64,128]{1,0:T(8,128)S(1)}, f32[64,128]{1,0:T(8,128)S(1)}, u32[]{:S(2)}, u32[]{:S(2)}) collective-permute-start(f32[64,128]{1,0:T(8,128)S(1)} %get-tuple-element.13), channel_id=1, source_target_pairs={{0,12},{1,13},{2,14},{3,15},{4,0},{5,1},{6,2},{7,3},{8,4},{9,5},{1... | collective-permute-start | bytes 98312 | tf_op jit(solution)/shard_map/ppermute | solution.py:116
  64.6 1.3 %collective-permute-start.3 = (f32[64,128]{1,0:T(8,128)S(1)}, f32[64,128]{1,0:T(8,128)S(1)}, u32[]{:S(2)}, u32[]{:S(2)}) collective-permute-start(f32[64,128]{1,0:T(8,128)S(1)} %get-tuple-element.11), channel_id=1, source_target_pairs={{0,4},{1,5},{2,6},{3,7},{4,8},{5,9},{6,10},{7,11},{8,12},{9,13},{1... | collective-permute-start | bytes 98312 | tf_op jit(solution)/shard_map/ppermute | solution.py:116
  66.5 3.6 %collective-permute-done.4 = f32[64,128]{1,0:T(8,128)S(1)} collective-permute-done((f32[64,128]{1,0:T(8,128)S(1)}, f32[64,128]{1,0:T(8,128)S(1)}, u32[]{:S(2)}, u32[]{:S(2)}) %collective-permute-start.4) | collective-permute-done | bytes 32800 | tf_op jit(solution)/shard_map/ppermute | solution.py:116
  70.1 0.7 multiply_convert_fusion
  70.9 0.9 collective-permute-start.6
  71.8 1.2 %collective-permute-start.7 = (bf16[64,128]{1,0:T(8,128)(2,1)S(1)}, bf16[64,128]{1,0:T(8,128)(2,1)S(1)}, u32[]{:S(2)}, u32[]{:S(2)}) collective-permute-start(bf16[64,128]{1,0:T(8,128)(2,1)S(1)} %maximum_maximum_fusion.1.q0), channel_id=1, source_target_pairs={{0,8},{1,9},{2,10},{3,11},{4,12},{5,13},{6,14},{7,15},{8,0},{9,1},... | collective-permute-start | bytes 49160 | tf_op jit(solution)/shard_map/ppermute | solution.py:114
  73.0 1.3 %collective-permute-start.8 = (bf16[64,128]{1,0:T(8,128)(2,1)S(1)}, bf16[64,128]{1,0:T(8,128)(2,1)S(1)}, u32[]{:S(2)}, u32[]{:S(2)}) collective-permute-start(bf16[64,128]{1,0:T(8,128)(2,1)S(1)} %maximum_maximum_fusion.1.q0), channel_id=1, source_target_pairs={{0,4},{1,5},{2,6},{3,7},{4,8},{5,9},{6,10},{7,11},{8,12},{9,13},{1... | collective-permute-start | bytes 49160 | tf_op jit(solution)/shard_map/ppermute | solution.py:114
  74.7 2.4 %collective-permute-done.7.q2 = bf16[64,128]{1,0:T(8,128)(2,1)S(1)} collective-permute-done((bf16[64,128]{1,0:T(8,128)(2,1)S(1)}, bf16[64,128]{1,0:T(8,128)(2,1)S(1)}, u32[]{:S(2)}, u32[]{:S(2)}) %collective-permute-start.7) | collective-permute-done | bytes 16416 | tf_op jit(solution)/shard_map/ppermute | solution.py:114
  77.0 0.9 collective-permute-done.8.q3
  78.0 18.6 %euler_basis.3 = (f32[64,128]{1,0:T(8,128)S(1)}, f32[64,128]{1,0:T(8,128)S(1)}, f32[64,128]{1,0:T(8,128)S(1)}, f32[64,128]{1,0:T(8,128)S(1)}) custom-call(s32[2]{0:T(128)S(1)} %pad_add_fusion.where_ref, s32[16,16]{1,0:T(8,128)S(1)} %copy-done, bf16[32,128,256]{2,1,0:T(8,128)(2,1)S(1)} %all-to-all-done.tab_ref, bf16[64,128]{1,0:T(8,128)(2,1)S(1)} %maximum_maximum_fusion.1.q0, ...), custom_call_target="tpu_custom_call" | custom-call | tf_op jit(solution)/shard_map/euler_basis/pallas_call | solution.py:76
  96.6 1.5 %collective-permute-start.11 = (f32[64,128]{1,0:T(8,128)S(1)}, f32[64,128]{1,0:T(8,128)S(1)}, u32[]{:S(2)}, u32[]{:S(2)}) collective-permute-start(f32[64,128]{1,0:T(8,128)S(1)} %get-tuple-element.17), channel_id=1, source_target_pairs={{0,12},{1,13},{2,14},{3,15},{4,0},{5,1},{6,2},{7,3},{8,4},{9,5},{1... | collective-permute-start | bytes 98312 | tf_op jit(solution)/shard_map/ppermute | solution.py:116
  98.1 0.9 collective-permute-start.10
  99.2 1.4 %collective-permute-done.11 = f32[64,128]{1,0:T(8,128)S(1)} collective-permute-done((f32[64,128]{1,0:T(8,128)S(1)}, f32[64,128]{1,0:T(8,128)S(1)}, u32[]{:S(2)}, u32[]{:S(2)}) %collective-permute-start.11) | collective-permute-done | bytes 32800 | tf_op jit(solution)/shard_map/ppermute | solution.py:116
  100.5 2.9 %collective-permute-done.10 = f32[64,128]{1,0:T(8,128)S(1)} collective-permute-done((f32[64,128]{1,0:T(8,128)S(1)}, f32[64,128]{1,0:T(8,128)S(1)}, u32[]{:S(2)}, u32[]{:S(2)}) %collective-permute-start.10) | collective-permute-done | bytes 32800 | tf_op jit(solution)/shard_map/ppermute | solution.py:116
  (35 shorter events, 5.0 us)
Async XLA Ops:
  6.0 7.6 %copy-start.1 = (f32[1,59,128]{2,0,1:T(1,128)S(1)}, f32[1,59,128]{2,0,1:T(1,128)}, u32[]{:S(2)}) copy-start(f32[1,59,128]{2,0,1:T(1,128)} %param.8) | copy-start | bytes 90628
  6.0 35.9 %copy-start = (s32[16,16]{1,0:T(8,128)S(1)}, s32[16,16]{1,0:T(8,128)}, u32[]{:S(2)}) copy-start(s32[16,16]{1,0:T(8,128)} %counts_ref.3) | copy-start | bytes 3076
  6.0 35.9 %all-to-all-start = ((bf16[32,128,256]{2,1,0:T(8,128)(2,1)}), bf16[32,128,256]{2,1,0:T(8,128)(2,1)S(1)}, u32[]{:S(2)}, u32[]{:S(2)}) async-start(bf16[32,128,256]{2,1,0:T(8,128)(2,1)} %broadcast_in_dim.37), calls=%async_computation | async-start | bytes 4194304 | tf_op jit(solution)/shard_map/all_to_all | solution.py:100
  13.6 56.5 %copy-start.2 = (f32[1,59,128]{2,0,1:T(1,128)S(1)}, f32[1,59,128]{2,0,1:T(1,128)}, u32[]{:S(2)}) copy-start(f32[1,59,128]{2,0,1:T(1,128)} %param.9) | copy-start | bytes 90628
  13.9 5.5 %collective-permute-start = (bf16[64,128]{1,0:T(8,128)(2,1)S(1)}, bf16[64,128]{1,0:T(8,128)(2,1)S(1)}, u32[]{:S(2)}, u32[]{:S(2)}) collective-permute-start(bf16[64,128]{1,0:T(8,128)(2,1)S(1)} %maximum_maximum_fusion.q0), channel_id=1, source_target_pairs={{0,12},{1,13},{2,14},{3,15},{4,0},{5,1},{6,2},{7,3},{8,4},{9,5},{1... | collective-permute-start | bytes 49160 | tf_op jit(solution)/shard_map/ppermute | solution.py:114
  18.0 5.2 %collective-permute-start.1 = (bf16[64,128]{1,0:T(8,128)(2,1)S(1)}, bf16[64,128]{1,0:T(8,128)(2,1)S(1)}, u32[]{:S(2)}, u32[]{:S(2)}) collective-permute-start(bf16[64,128]{1,0:T(8,128)(2,1)S(1)} %maximum_maximum_fusion.q0), channel_id=1, source_target_pairs={{0,8},{1,9},{2,10},{3,11},{4,12},{5,13},{6,14},{7,15},{8,0},{9,1},... | collective-permute-start | bytes 49160 | tf_op jit(solution)/shard_map/ppermute | solution.py:114
  18.0 5.2 %collective-permute-start.2 = (bf16[64,128]{1,0:T(8,128)(2,1)S(1)}, bf16[64,128]{1,0:T(8,128)(2,1)S(1)}, u32[]{:S(2)}, u32[]{:S(2)}) collective-permute-start(bf16[64,128]{1,0:T(8,128)(2,1)S(1)} %maximum_maximum_fusion.q0), channel_id=1, source_target_pairs={{0,4},{1,5},{2,6},{3,7},{4,8},{5,9},{6,10},{7,11},{8,12},{9,13},{1... | collective-permute-start | bytes 49160 | tf_op jit(solution)/shard_map/ppermute | solution.py:114
  60.5 6.0 %collective-permute-start.5 = (f32[64,128]{1,0:T(8,128)S(1)}, f32[64,128]{1,0:T(8,128)S(1)}, u32[]{:S(2)}, u32[]{:S(2)}) collective-permute-start(f32[64,128]{1,0:T(8,128)S(1)} %get-tuple-element.13), channel_id=1, source_target_pairs={{0,12},{1,13},{2,14},{3,15},{4,0},{5,1},{6,2},{7,3},{8,4},{9,5},{1... | collective-permute-start | bytes 98312 | tf_op jit(solution)/shard_map/ppermute | solution.py:116
  64.6 5.5 %collective-permute-start.4 = (f32[64,128]{1,0:T(8,128)S(1)}, f32[64,128]{1,0:T(8,128)S(1)}, u32[]{:S(2)}, u32[]{:S(2)}) collective-permute-start(f32[64,128]{1,0:T(8,128)S(1)} %get-tuple-element.12), channel_id=1, source_target_pairs={{0,8},{1,9},{2,10},{3,11},{4,12},{5,13},{6,14},{7,15},{8,0},{9,1},... | collective-permute-start | bytes 98312 | tf_op jit(solution)/shard_map/ppermute | solution.py:116
  64.6 5.5 %collective-permute-start.3 = (f32[64,128]{1,0:T(8,128)S(1)}, f32[64,128]{1,0:T(8,128)S(1)}, u32[]{:S(2)}, u32[]{:S(2)}) collective-permute-start(f32[64,128]{1,0:T(8,128)S(1)} %get-tuple-element.11), channel_id=1, source_target_pairs={{0,4},{1,5},{2,6},{3,7},{4,8},{5,9},{6,10},{7,11},{8,12},{9,13},{1... | collective-permute-start | bytes 98312 | tf_op jit(solution)/shard_map/ppermute | solution.py:116
  70.9 3.8 %collective-permute-start.6 = (bf16[64,128]{1,0:T(8,128)(2,1)S(1)}, bf16[64,128]{1,0:T(8,128)(2,1)S(1)}, u32[]{:S(2)}, u32[]{:S(2)}) collective-permute-start(bf16[64,128]{1,0:T(8,128)(2,1)S(1)} %maximum_maximum_fusion.1.q0), channel_id=1, source_target_pairs={{0,12},{1,13},{2,14},{3,15},{4,0},{5,1},{6,2},{7,3},{8,4},{9,5},{1... | collective-permute-start | bytes 49160 | tf_op jit(solution)/shard_map/ppermute | solution.py:114
  71.8 5.2 %collective-permute-start.7 = (bf16[64,128]{1,0:T(8,128)(2,1)S(1)}, bf16[64,128]{1,0:T(8,128)(2,1)S(1)}, u32[]{:S(2)}, u32[]{:S(2)}) collective-permute-start(bf16[64,128]{1,0:T(8,128)(2,1)S(1)} %maximum_maximum_fusion.1.q0), channel_id=1, source_target_pairs={{0,8},{1,9},{2,10},{3,11},{4,12},{5,13},{6,14},{7,15},{8,0},{9,1},... | collective-permute-start | bytes 49160 | tf_op jit(solution)/shard_map/ppermute | solution.py:114
  73.0 4.9 %collective-permute-start.8 = (bf16[64,128]{1,0:T(8,128)(2,1)S(1)}, bf16[64,128]{1,0:T(8,128)(2,1)S(1)}, u32[]{:S(2)}, u32[]{:S(2)}) collective-permute-start(bf16[64,128]{1,0:T(8,128)(2,1)S(1)} %maximum_maximum_fusion.1.q0), channel_id=1, source_target_pairs={{0,4},{1,5},{2,6},{3,7},{4,8},{5,9},{6,10},{7,11},{8,12},{9,13},{1... | collective-permute-start | bytes 49160 | tf_op jit(solution)/shard_map/ppermute | solution.py:114
  96.6 4.0 %collective-permute-start.11 = (f32[64,128]{1,0:T(8,128)S(1)}, f32[64,128]{1,0:T(8,128)S(1)}, u32[]{:S(2)}, u32[]{:S(2)}) collective-permute-start(f32[64,128]{1,0:T(8,128)S(1)} %get-tuple-element.17), channel_id=1, source_target_pairs={{0,12},{1,13},{2,14},{3,15},{4,0},{5,1},{6,2},{7,3},{8,4},{9,5},{1... | collective-permute-start | bytes 98312 | tf_op jit(solution)/shard_map/ppermute | solution.py:116
  98.1 5.4 %collective-permute-start.10 = (f32[64,128]{1,0:T(8,128)S(1)}, f32[64,128]{1,0:T(8,128)S(1)}, u32[]{:S(2)}, u32[]{:S(2)}) collective-permute-start(f32[64,128]{1,0:T(8,128)S(1)} %get-tuple-element.16), channel_id=1, source_target_pairs={{0,8},{1,9},{2,10},{3,11},{4,12},{5,13},{6,14},{7,15},{8,0},{9,1},... | collective-permute-start | bytes 98312 | tf_op jit(solution)/shard_map/ppermute | solution.py:116
  99.0 5.1 %collective-permute-start.9 = (f32[64,128]{1,0:T(8,128)S(1)}, f32[64,128]{1,0:T(8,128)S(1)}, u32[]{:S(2)}, u32[]{:S(2)}) collective-permute-start(f32[64,128]{1,0:T(8,128)S(1)} %get-tuple-element.15), channel_id=1, source_target_pairs={{0,4},{1,5},{2,6},{3,7},{4,8},{5,9},{6,10},{7,11},{8,12},{9,13},{1... | collective-permute-start | bytes 98312 | tf_op jit(solution)/shard_map/ppermute | solution.py:116

commit v2 on v1

--- a/solution.py
+++ b/solution.py
@@ -14,6 +14,7 @@
 DIM = 59
 HALF = 64
 RING = 4
+UNIT = 2
 BF = jnp.bfloat16
 F32 = jnp.float32
 
@@ -31,43 +32,73 @@
     )
 
 
-def kernel(where_ref, counts_ref, tab_ref, q0, q1, q2, q3, o0, o1, o2, o3, qt_ref, acc_ref, sum_ref):
+def kernel(
+    where_ref, counts_ref, tab_ref, q0, q1, q2, q3, o0, o1, o2, o3, qt_ref, sel_a, sel_b, basis_a, basis_b, acc_ref
+):
     z, y = where_ref[0], where_ref[1]
     for j, q in enumerate((q0, q1, q2, q3)):
         qt_ref[pl.ds(j * 128, 128), :] = q[...].astype(F32).T.astype(BF)
     row = lax.broadcasted_iota(jnp.int32, (HALF, 256), 0)
-    for yy in range(RING):
-        acc_ref[...] = jnp.zeros_like(acc_ref)
+    units = 8 * RING // UNIT
 
-        @pl.loop(0, 8)
-        def _(p):
-            blk = tab_ref[p * RING + yy]
+    def block(i):
+        return tab_ref[(i % 8) * RING + i // 8]
+
+    def select(u, sel_ref):
+        for b in range(UNIT):
+            blk = block(jnp.minimum(u, units - 1) * UNIT + b)
             par = jnp.concatenate([blk[56:64], blk[120:128]], axis=0).astype(F32)
-            basis = None
             for k in range(3):
                 dim = par[3 + k : 4 + k].astype(jnp.int32)
                 scale = par[6 + k : 7 + k] if k < 2 else par[11:12]
                 bias = par[12 + k : 13 + k]
-                table = jnp.where(row == dim, scale, jnp.where(row == DIM, bias, 0.0)).astype(BF)
-                left = jnp.dot(qt_ref[...], table, preferred_element_type=F32)
+                table = jnp.where(row == dim, scale, jnp.where(row == DIM, bias, 0.0))
+                sel_ref[b, k] = table.astype(BF)
+
+    def hats(sel_ref, basis_ref):
+        for b in range(UNIT):
+            basis = None
+            for k in range(3):
+                left = jnp.dot(qt_ref[...], sel_ref[b, k], preferred_element_type=F32)
                 factor = jnp.maximum(jnp.minimum(left, 2.0 - left), 0.0)
                 basis = factor if basis is None else basis * factor
-            acc_ref[...] += lax.dot_general(
-                basis.astype(BF), blk, (((1,), (1,)), ((), ())), preferred_element_type=F32
-            )
+            basis_ref[:, pl.ds(b * 256, 256)] = basis.astype(BF)
 
-        value = acc_ref[...]
-        marginal = jnp.exp(-GAMMA * value[:, :HALF] + value[:, HALF:])
-        for j in range(RING):
-            s = lax.rem(z + j, RING) * RING + y
-            count = counts_ref[s, z * RING + yy].astype(F32)
-            term = count * marginal[j * 128 : (j + 1) * 128]
-            if yy == 0:
-                sum_ref[j] = term
-            else:
-                sum_ref[j] += term
+    def sums(u, basis_ref):
+        weights = jnp.concatenate([block(u * UNIT + b) for b in range(UNIT)], axis=1)
+        acc_ref[u * UNIT // 8] += lax.dot_general(
+            basis_ref[...], weights, (((1,), (1,)), ((), ())), preferred_element_type=F32
+        )
+
+    acc_ref[...] = jnp.zeros_like(acc_ref)
+    select(0, sel_a)
+    select(1, sel_b)
+    hats(sel_a, basis_a)
+    select(2, sel_a)
+
+    @pl.loop(0, units // 2 - 1)
+    def _(it):
+        u = 2 * it + 1
+        hats(sel_b, basis_b)
+        sums(u - 1, basis_a)
+        select(u + 2, sel_b)
+        hats(sel_a, basis_a)
+        sums(u, basis_b)
+        select(u + 3, sel_a)
+
+    hats(sel_b, basis_b)
+    sums(units - 2, basis_a)
+    sums(units - 1, basis_b)
+
     for j, o in enumerate((o0, o1, o2, o3)):
-        o[...] = sum_ref[j].T
+        s = lax.rem(z + j, RING) * RING + y
+        total = None
+        for t in range(RING):
+            value = acc_ref[t, pl.ds(j * 128, 128), :]
+            count = counts_ref[s, z * RING + t].astype(F32)
+            term = count * jnp.exp(-GAMMA * value[:, :HALF] + value[:, HALF:])
+            total = term if total is None else total + term
+        o[...] = total.T
 
 
 def partial_sums(where, counts, tables, queries):
@@ -80,8 +111,11 @@
         out_specs=[vm] * RING,
         scratch_shapes=[
             pltpu.VMEM((512, HALF), BF),
-            pltpu.VMEM((512, 128), F32),
-            pltpu.VMEM((RING, 128, HALF), F32),
+            pltpu.VMEM((UNIT, 3, HALF, 256), BF),
+            pltpu.VMEM((UNIT, 3, HALF, 256), BF),
+            pltpu.VMEM((512, UNIT * 256), BF),
+            pltpu.VMEM((512, UNIT * 256), BF),
+            pltpu.VMEM((RING, 512, 128), F32),
         ],
         compiler_params=pltpu.CompilerParams(vmem_limit_bytes=40 << 20),
         name="euler_basis",

time: 106 us -> 92.3 us (0.87)
  Pallas kernels: 37.2 us -> 23.1 us
    pallas_call x2, Pallas kernels: 37.2 us -> 23.1 us  [partial_sums(): pl.pallas_call(kernel, out_shape=[jax.ShapeDtypeStruct((HALF, 128), F32)]...]
where the time goes in v2:
time: 92.3 us; the launch traced here: 91.9 us
  waiting for transfers between devices  34.7 us (38%)
  starting transfers between devices  24.3 us (26%)
  Pallas kernels  23.1 us (25%)
  other arithmetic  5.24 us (6%)
  local copies, waits for them, and re-layouts  3.11 us (3%)
  between operations  1.41 us (2%)
    pallas_call x2, Pallas kernels, partial_sums(): pl.pallas_call(kernel, out_shape=[jax.ShapeDtypeStruct((HALF, 128), F32)]...  23.1 us
    all_to_all x1, waiting for transfers between devices, per_device(): lax.all_to_all(jnp.broadcast_to(block[None], (32,) + block.shape), ('pts'...  18.7 us
    ppermute x6, starting transfers between devices, per_device(): lax.ppermute(own, 'shk', shift(-j))  8.82 us
    ppermute x6, waiting for transfers between devices, per_device(): lax.ppermute(parts[j], 'shk', shift(j))  8.54 us
    ppermute x6, starting transfers between devices, per_device(): lax.ppermute(parts[j], 'shk', shift(j))  7.96 us
    all_to_all x1, starting transfers between devices, per_device(): lax.all_to_all(jnp.broadcast_to(block[None], (32,) + block.shape), ('pts'...  7.56 us
    ppermute x6, waiting for transfers between devices, per_device(): lax.ppermute(own, 'shk', shift(-j))  7.53 us
  transfers between devices with their start and end apart: 13, of which 10 were waited for; matrix products, arithmetic and copies ran while one was open for 1% of the time, Pallas kernels for 0%

profile of v2, /device:TPU:0, one launch (start us, length us, event | category | flops | bytes accessed | tf_op | source)
XLA Modules:
  0.0 91.9 jit_solution(14861453287159474950)
XLA Ops:
  0.6 0.8 fusion.17
  2.1 0.8 bitcast_select_fusion
  3.0 0.7 fusion.18
  4.4 1.6 %broadcast_in_dim.37 = bf16[32,128,256]{2,1,0:T(8,128)(2,1)} broadcast(bf16[128,256]{1,0:T(8,128)(2,1)S(1)} %concatenate.9), dimensions={1,2} | broadcast | bytes 2162688 | tf_op jit(solution)/shard_map/broadcast_in_dim | solution.py:135
  6.0 7.6 %all-to-all-start = ((bf16[32,128,256]{2,1,0:T(8,128)(2,1)}), bf16[32,128,256]{2,1,0:T(8,128)(2,1)S(1)}, u32[]{:S(2)}, u32[]{:S(2)}) async-start(bf16[32,128,256]{2,1,0:T(8,128)(2,1)} %broadcast_in_dim.37), calls=%async_computation | async-start | bytes 4194304 | tf_op jit(solution)/shard_map/all_to_all | solution.py:134
  13.9 4.1 %collective-permute-start = (bf16[64,128]{1,0:T(8,128)(2,1)S(1)}, bf16[64,128]{1,0:T(8,128)(2,1)S(1)}, u32[]{:S(2)}, u32[]{:S(2)}) collective-permute-start(bf16[64,128]{1,0:T(8,128)(2,1)S(1)} %maximum_maximum_fusion.q0), channel_id=1, source_target_pairs={{0,12},{1,13},{2,14},{3,15},{4,0},{5,1},{6,2},{7,3},{8,4},{9,5},{1... | collective-permute-start | bytes 49160 | tf_op jit(solution)/shard_map/ppermute | solution.py:148
  18.0 1.3 %collective-permute-start.2 = (bf16[64,128]{1,0:T(8,128)(2,1)S(1)}, bf16[64,128]{1,0:T(8,128)(2,1)S(1)}, u32[]{:S(2)}, u32[]{:S(2)}) collective-permute-start(bf16[64,128]{1,0:T(8,128)(2,1)S(1)} %maximum_maximum_fusion.q0), channel_id=1, source_target_pairs={{0,4},{1,5},{2,6},{3,7},{4,8},{5,9},{6,10},{7,11},{8,12},{9,13},{1... | collective-permute-start | bytes 49160 | tf_op jit(solution)/shard_map/ppermute | solution.py:148
  19.4 3.8 %collective-permute-done.1.q2 = bf16[64,128]{1,0:T(8,128)(2,1)S(1)} collective-permute-done((bf16[64,128]{1,0:T(8,128)(2,1)S(1)}, bf16[64,128]{1,0:T(8,128)(2,1)S(1)}, u32[]{:S(2)}, u32[]{:S(2)}) %collective-permute-start.1) | collective-permute-done | bytes 16416 | tf_op jit(solution)/shard_map/ppermute | solution.py:148
  23.2 18.7 %all-to-all-done.tab_ref = bf16[32,128,256]{2,1,0:T(8,128)(2,1)S(1)} async-done(((bf16[32,128,256]{2,1,0:T(8,128)(2,1)}), bf16[32,128,256]{2,1,0:T(8,128)(2,1)S(1)}, u32[]{:S(2)}, u32[]{:S(2)}) %all-to-all-start) | async-done | bytes 2097184 | tf_op jit(solution)/shard_map/all_to_all | solution.py:134
  41.9 11.5 %euler_basis.2 = (f32[64,128]{1,0:T(8,128)S(1)}, f32[64,128]{1,0:T(8,128)S(1)}, f32[64,128]{1,0:T(8,128)S(1)}, f32[64,128]{1,0:T(8,128)S(1)}) custom-call(s32[2]{0:T(128)S(1)} %pad_add_fusion.where_ref, s32[16,16]{1,0:T(8,128)S(1)} %copy-done, bf16[32,128,256]{2,1,0:T(8,128)(2,1)S(1)} %all-to-all-done.tab_ref, bf16[64,128]{1,0:T(8,128)(2,1)S(1)} %maximum_maximum_fusion.q0, ...), custom_call_target="tpu_custom_call" | custom-call | tf_op jit(solution)/shard_map/euler_basis/pallas_call | solution.py:107
  53.4 4.1 %collective-permute-start.5 = (f32[64,128]{1,0:T(8,128)S(1)}, f32[64,128]{1,0:T(8,128)S(1)}, u32[]{:S(2)}, u32[]{:S(2)}) collective-permute-start(f32[64,128]{1,0:T(8,128)S(1)} %get-tuple-element.13), channel_id=1, source_target_pairs={{0,12},{1,13},{2,14},{3,15},{4,0},{5,1},{6,2},{7,3},{8,4},{9,5},{1... | collective-permute-start | bytes 98312 | tf_op jit(solution)/shard_map/ppermute | solution.py:150
  57.5 1.3 %collective-permute-start.3 = (f32[64,128]{1,0:T(8,128)S(1)}, f32[64,128]{1,0:T(8,128)S(1)}, u32[]{:S(2)}, u32[]{:S(2)}) collective-permute-start(f32[64,128]{1,0:T(8,128)S(1)} %get-tuple-element.11), channel_id=1, source_target_pairs={{0,4},{1,5},{2,6},{3,7},{4,8},{5,9},{6,10},{7,11},{8,12},{9,13},{1... | collective-permute-start | bytes 98312 | tf_op jit(solution)/shard_map/ppermute | solution.py:150
  59.4 3.6 %collective-permute-done.4 = f32[64,128]{1,0:T(8,128)S(1)} collective-permute-done((f32[64,128]{1,0:T(8,128)S(1)}, f32[64,128]{1,0:T(8,128)S(1)}, u32[]{:S(2)}, u32[]{:S(2)}) %collective-permute-start.4) | collective-permute-done | bytes 32800 | tf_op jit(solution)/shard_map/ppermute | solution.py:150
  63.0 0.7 multiply_convert_fusion
  63.8 0.9 collective-permute-start.6
  64.7 1.2 %collective-permute-start.7 = (bf16[64,128]{1,0:T(8,128)(2,1)S(1)}, bf16[64,128]{1,0:T(8,128)(2,1)S(1)}, u32[]{:S(2)}, u32[]{:S(2)}) collective-permute-start(bf16[64,128]{1,0:T(8,128)(2,1)S(1)} %maximum_maximum_fusion.1.q0), channel_id=1, source_target_pairs={{0,8},{1,9},{2,10},{3,11},{4,12},{5,13},{6,14},{7,15},{8,0},{9,1},... | collective-permute-start | bytes 49160 | tf_op jit(solution)/shard_map/ppermute | solution.py:148
  65.9 1.3 %collective-permute-start.8 = (bf16[64,128]{1,0:T(8,128)(2,1)S(1)}, bf16[64,128]{1,0:T(8,128)(2,1)S(1)}, u32[]{:S(2)}, u32[]{:S(2)}) collective-permute-start(bf16[64,128]{1,0:T(8,128)(2,1)S(1)} %maximum_maximum_fusion.1.q0), channel_id=1, source_target_pairs={{0,4},{1,5},{2,6},{3,7},{4,8},{5,9},{6,10},{7,11},{8,12},{9,13},{1... | collective-permute-start | bytes 49160 | tf_op jit(solution)/shard_map/ppermute | solution.py:148
  67.6 2.4 %collective-permute-done.7.q2 = bf16[64,128]{1,0:T(8,128)(2,1)S(1)} collective-permute-done((bf16[64,128]{1,0:T(8,128)(2,1)S(1)}, bf16[64,128]{1,0:T(8,128)(2,1)S(1)}, u32[]{:S(2)}, u32[]{:S(2)}) %collective-permute-start.7) | collective-permute-done | bytes 16416 | tf_op jit(solution)/shard_map/ppermute | solution.py:148
  70.0 0.9 collective-permute-done.8.q3
  70.9 11.5 %euler_basis.3 = (f32[64,128]{1,0:T(8,128)S(1)}, f32[64,128]{1,0:T(8,128)S(1)}, f32[64,128]{1,0:T(8,128)S(1)}, f32[64,128]{1,0:T(8,128)S(1)}) custom-call(s32[2]{0:T(128)S(1)} %pad_add_fusion.where_ref, s32[16,16]{1,0:T(8,128)S(1)} %copy-done, bf16[32,128,256]{2,1,0:T(8,128)(2,1)S(1)} %all-to-all-done.tab_ref, bf16[64,128]{1,0:T(8,128)(2,1)S(1)} %maximum_maximum_fusion.1.q0, ...), custom_call_target="tpu_custom_call" | custom-call | tf_op jit(solution)/shard_map/euler_basis/pallas_call | solution.py:107
  82.4 1.5 %collective-permute-start.11 = (f32[64,128]{1,0:T(8,128)S(1)}, f32[64,128]{1,0:T(8,128)S(1)}, u32[]{:S(2)}, u32[]{:S(2)}) collective-permute-start(f32[64,128]{1,0:T(8,128)S(1)} %get-tuple-element.17), channel_id=1, source_target_pairs={{0,12},{1,13},{2,14},{3,15},{4,0},{5,1},{6,2},{7,3},{8,4},{9,5},{1... | collective-permute-start | bytes 98312 | tf_op jit(solution)/shard_map/ppermute | solution.py:150
  83.9 0.9 collective-permute-start.10
  85.0 1.4 %collective-permute-done.11 = f32[64,128]{1,0:T(8,128)S(1)} collective-permute-done((f32[64,128]{1,0:T(8,128)S(1)}, f32[64,128]{1,0:T(8,128)S(1)}, u32[]{:S(2)}, u32[]{:S(2)}) %collective-permute-start.11) | collective-permute-done | bytes 32800 | tf_op jit(solution)/shard_map/ppermute | solution.py:150
  86.4 2.9 %collective-permute-done.10 = f32[64,128]{1,0:T(8,128)S(1)} collective-permute-done((f32[64,128]{1,0:T(8,128)S(1)}, f32[64,128]{1,0:T(8,128)S(1)}, u32[]{:S(2)}, u32[]{:S(2)}) %collective-permute-start.10) | collective-permute-done | bytes 32800 | tf_op jit(solution)/shard_map/ppermute | solution.py:150
  (35 shorter events, 5.0 us)
Async XLA Ops:
  6.0 7.6 %copy-start.1 = (f32[1,59,128]{2,0,1:T(1,128)S(1)}, f32[1,59,128]{2,0,1:T(1,128)}, u32[]{:S(2)}) copy-start(f32[1,59,128]{2,0,1:T(1,128)} %param.8) | copy-start | bytes 90628
  6.0 35.9 %copy-start = (s32[16,16]{1,0:T(8,128)S(1)}, s32[16,16]{1,0:T(8,128)}, u32[]{:S(2)}) copy-start(s32[16,16]{1,0:T(8,128)} %counts_ref.3) | copy-start | bytes 3076
  6.0 35.9 %all-to-all-start = ((bf16[32,128,256]{2,1,0:T(8,128)(2,1)}), bf16[32,128,256]{2,1,0:T(8,128)(2,1)S(1)}, u32[]{:S(2)}, u32[]{:S(2)}) async-start(bf16[32,128,256]{2,1,0:T(8,128)(2,1)} %broadcast_in_dim.37), calls=%async_computation | async-start | bytes 4194304 | tf_op jit(solution)/shard_map/all_to_all | solution.py:134
  13.6 49.4 %copy-start.2 = (f32[1,59,128]{2,0,1:T(1,128)S(1)}, f32[1,59,128]{2,0,1:T(1,128)}, u32[]{:S(2)}) copy-start(f32[1,59,128]{2,0,1:T(1,128)} %param.9) | copy-start | bytes 90628
  13.9 5.5 %collective-permute-start = (bf16[64,128]{1,0:T(8,128)(2,1)S(1)}, bf16[64,128]{1,0:T(8,128)(2,1)S(1)}, u32[]{:S(2)}, u32[]{:S(2)}) collective-permute-start(bf16[64,128]{1,0:T(8,128)(2,1)S(1)} %maximum_maximum_fusion.q0), channel_id=1, source_target_pairs={{0,12},{1,13},{2,14},{3,15},{4,0},{5,1},{6,2},{7,3},{8,4},{9,5},{1... | collective-permute-start | bytes 49160 | tf_op jit(solution)/shard_map/ppermute | solution.py:148
  18.0 5.2 %collective-permute-start.1 = (bf16[64,128]{1,0:T(8,128)(2,1)S(1)}, bf16[64,128]{1,0:T(8,128)(2,1)S(1)}, u32[]{:S(2)}, u32[]{:S(2)}) collective-permute-start(bf16[64,128]{1,0:T(8,128)(2,1)S(1)} %maximum_maximum_fusion.q0), channel_id=1, source_target_pairs={{0,8},{1,9},{2,10},{3,11},{4,12},{5,13},{6,14},{7,15},{8,0},{9,1},... | collective-permute-start | bytes 49160 | tf_op jit(solution)/shard_map/ppermute | solution.py:148
  18.0 5.2 %collective-permute-start.2 = (bf16[64,128]{1,0:T(8,128)(2,1)S(1)}, bf16[64,128]{1,0:T(8,128)(2,1)S(1)}, u32[]{:S(2)}, u32[]{:S(2)}) collective-permute-start(bf16[64,128]{1,0:T(8,128)(2,1)S(1)} %maximum_maximum_fusion.q0), channel_id=1, source_target_pairs={{0,4},{1,5},{2,6},{3,7},{4,8},{5,9},{6,10},{7,11},{8,12},{9,13},{1... | collective-permute-start | bytes 49160 | tf_op jit(solution)/shard_map/ppermute | solution.py:148
  53.4 6.0 %collective-permute-start.5 = (f32[64,128]{1,0:T(8,128)S(1)}, f32[64,128]{1,0:T(8,128)S(1)}, u32[]{:S(2)}, u32[]{:S(2)}) collective-permute-start(f32[64,128]{1,0:T(8,128)S(1)} %get-tuple-element.13), channel_id=1, source_target_pairs={{0,12},{1,13},{2,14},{3,15},{4,0},{5,1},{6,2},{7,3},{8,4},{9,5},{1... | collective-permute-start | bytes 98312 | tf_op jit(solution)/shard_map/ppermute | solution.py:150
  57.5 5.5 %collective-permute-start.4 = (f32[64,128]{1,0:T(8,128)S(1)}, f32[64,128]{1,0:T(8,128)S(1)}, u32[]{:S(2)}, u32[]{:S(2)}) collective-permute-start(f32[64,128]{1,0:T(8,128)S(1)} %get-tuple-element.12), channel_id=1, source_target_pairs={{0,8},{1,9},{2,10},{3,11},{4,12},{5,13},{6,14},{7,15},{8,0},{9,1},... | collective-permute-start | bytes 98312 | tf_op jit(solution)/shard_map/ppermute | solution.py:150
  57.5 5.5 %collective-permute-start.3 = (f32[64,128]{1,0:T(8,128)S(1)}, f32[64,128]{1,0:T(8,128)S(1)}, u32[]{:S(2)}, u32[]{:S(2)}) collective-permute-start(f32[64,128]{1,0:T(8,128)S(1)} %get-tuple-element.11), channel_id=1, source_target_pairs={{0,4},{1,5},{2,6},{3,7},{4,8},{5,9},{6,10},{7,11},{8,12},{9,13},{1... | collective-permute-start | bytes 98312 | tf_op jit(solution)/shard_map/ppermute | solution.py:150
  63.8 3.8 %collective-permute-start.6 = (bf16[64,128]{1,0:T(8,128)(2,1)S(1)}, bf16[64,128]{1,0:T(8,128)(2,1)S(1)}, u32[]{:S(2)}, u32[]{:S(2)}) collective-permute-start(bf16[64,128]{1,0:T(8,128)(2,1)S(1)} %maximum_maximum_fusion.1.q0), channel_id=1, source_target_pairs={{0,12},{1,13},{2,14},{3,15},{4,0},{5,1},{6,2},{7,3},{8,4},{9,5},{1... | collective-permute-start | bytes 49160 | tf_op jit(solution)/shard_map/ppermute | solution.py:148
  64.7 5.2 %collective-permute-start.7 = (bf16[64,128]{1,0:T(8,128)(2,1)S(1)}, bf16[64,128]{1,0:T(8,128)(2,1)S(1)}, u32[]{:S(2)}, u32[]{:S(2)}) collective-permute-start(bf16[64,128]{1,0:T(8,128)(2,1)S(1)} %maximum_maximum_fusion.1.q0), channel_id=1, source_target_pairs={{0,8},{1,9},{2,10},{3,11},{4,12},{5,13},{6,14},{7,15},{8,0},{9,1},... | collective-permute-start | bytes 49160 | tf_op jit(solution)/shard_map/ppermute | solution.py:148
  65.9 4.9 %collective-permute-start.8 = (bf16[64,128]{1,0:T(8,128)(2,1)S(1)}, bf16[64,128]{1,0:T(8,128)(2,1)S(1)}, u32[]{:S(2)}, u32[]{:S(2)}) collective-permute-start(bf16[64,128]{1,0:T(8,128)(2,1)S(1)} %maximum_maximum_fusion.1.q0), channel_id=1, source_target_pairs={{0,4},{1,5},{2,6},{3,7},{4,8},{5,9},{6,10},{7,11},{8,12},{9,13},{1... | collective-permute-start | bytes 49160 | tf_op jit(solution)/shard_map/ppermute | solution.py:148
  82.4 4.0 %collective-permute-start.11 = (f32[64,128]{1,0:T(8,128)S(1)}, f32[64,128]{1,0:T(8,128)S(1)}, u32[]{:S(2)}, u32[]{:S(2)}) collective-permute-start(f32[64,128]{1,0:T(8,128)S(1)} %get-tuple-element.17), channel_id=1, source_target_pairs={{0,12},{1,13},{2,14},{3,15},{4,0},{5,1},{6,2},{7,3},{8,4},{9,5},{1... | collective-permute-start | bytes 98312 | tf_op jit(solution)/shard_map/ppermute | solution.py:150
  83.9 5.4 %collective-permute-start.10 = (f32[64,128]{1,0:T(8,128)S(1)}, f32[64,128]{1,0:T(8,128)S(1)}, u32[]{:S(2)}, u32[]{:S(2)}) collective-permute-start(f32[64,128]{1,0:T(8,128)S(1)} %get-tuple-element.16), channel_id=1, source_target_pairs={{0,8},{1,9},{2,10},{3,11},{4,12},{5,13},{6,14},{7,15},{8,0},{9,1},... | collective-permute-start | bytes 98312 | tf_op jit(solution)/shard_map/ppermute | solution.py:150
  84.8 5.1 %collective-permute-start.9 = (f32[64,128]{1,0:T(8,128)S(1)}, f32[64,128]{1,0:T(8,128)S(1)}, u32[]{:S(2)}, u32[]{:S(2)}) collective-permute-start(f32[64,128]{1,0:T(8,128)S(1)} %get-tuple-element.15), channel_id=1, source_target_pairs={{0,4},{1,5},{2,6},{3,7},{4,8},{5,9},{6,10},{7,11},{8,12},{9,13},{1... | collective-permute-start | bytes 98312 | tf_op jit(solution)/shard_map/ppermute | solution.py:150

commit v3 on v2

v3 whole, which is shorter than its diff:
```python
import jax
import jax.numpy as jnp
from jax import lax
from jax.experimental import pallas as pl
from jax.experimental.pallas import tpu as pltpu
from jax.sharding import PartitionSpec as P

ITERS = 2
GAMMA = 2.0
BETA = 0.96
damping = 0.5
DIM = 59
HALF = 64
RING = 4
UNIT = 2
BF = jnp.bfloat16
F32 = jnp.float32


def pack_kernel(live_ref, surplus_ref, dims_ref, levels_ref, index_ref, o_ref):
    npoints = surplus_ref.shape[1]
    position = lax.broadcasted_iota(jnp.int32, (1, npoints), 1)
    kept = position < live_ref[0, 0]
    body = jnp.where(kept, surplus_ref[0:112, :].astype(F32), 0.0).astype(BF)
    row = lax.broadcasted_iota(jnp.int32, (16, npoints), 0)
    tail = jnp.where(kept, surplus_ref[112:118, :].astype(F32), 0.0)
    tail = jnp.concatenate([tail, jnp.zeros((10, npoints), F32)], axis=0)
    for k in range(3):
        level = levels_ref[k]
        refined = level > 0
        scale = jnp.where(refined, jnp.left_shift(jnp.ones_like(level), level), 0).astype(F32)
        bias = jnp.where(refined, 1 - index_ref[k], 1).astype(F32)
        for place, value in ((6 + k, dims_ref[k].astype(F32)), (9 + k, scale), (12 + k, bias)):
            tail = jnp.where(row == place, value, tail)
    tail = tail.astype(BF)
    for g in range(o_ref.shape[0]):
        o_ref[g, 0:112, :] = body
        o_ref[g, 112:128, :] = tail


def pack(surplus, dims, levels, index, live):
    vm = pl.BlockSpec(memory_space=pltpu.VMEM)
    sm = pl.BlockSpec(memory_space=pltpu.SMEM)
    return pl.pallas_call(
        pack_kernel,
        out_shape=jax.ShapeDtypeStruct((16, 128, surplus.shape[1]), BF),
        in_specs=[sm, vm, vm, vm, vm],
        out_specs=vm,
        compiler_params=pltpu.CompilerParams(vmem_limit_bytes=8 << 20),
        name="pack_tables",
    )(live, surplus, *(jnp.transpose(v, (1, 0, 2)) for v in (dims, levels, index)))


def finish_kernel(rowsum_ref, now_ref, income_ref, g0, g1, g2, g3, cur_ref, con_ref):
    total = ((g0[...] + g1[...]) + (g2[...] + g3[...]))[:DIM]
    expect = total / rowsum_ref[0].astype(F32)
    consumption = (BETA * expect) ** (-1.0 / GAMMA)
    value = income_ref[:, 0, :] - consumption
    share = 1.0 / (1.0 + jnp.exp(-value))
    con_ref[:, 0, :] = consumption
    cur_ref[:, 0, :] = (1.0 - damping) * now_ref[...] + damping * share


def finish(rowsum, current, income, got):
    vm = pl.BlockSpec(memory_space=pltpu.VMEM)
    sm = pl.BlockSpec(memory_space=pltpu.SMEM)
    flat = jax.ShapeDtypeStruct((DIM, 1, current.shape[1]), F32)
    new, consumption = pl.pallas_call(
        finish_kernel,
        out_shape=[flat, flat],
        in_specs=[sm, vm, vm, vm, vm, vm, vm],
        out_specs=[vm, vm],
        compiler_params=pltpu.CompilerParams(vmem_limit_bytes=4 << 20),
        name="finish",
    )(rowsum, current, income, *got)
    return jnp.transpose(new, (1, 0, 2)), jnp.transpose(consumption, (1, 0, 2))


def kernel(
    where_ref, counts_ref, tab_a, tab_b, q0, q1, q2, q3, o0, o1, o2, o3, qt_ref, sel_a, sel_b, basis_a, basis_b, acc_ref
):
    z, y = where_ref[0], where_ref[1]
    for j, q in enumerate((q0, q1, q2, q3)):
        qt_ref[pl.ds(j * 128, 128), :] = q[...].astype(F32).T.astype(BF)
    row = lax.broadcasted_iota(jnp.int32, (HALF, 256), 0)
    units = 8 * RING // UNIT

    def block(u, b):
        return (tab_a, tab_b)[b][(u % RING) * RING + u // RING]

    def select(u, sel_ref):
        for b in range(UNIT):
            par = block(jnp.minimum(u, units - 1), b)[112:128].astype(F32)
            for k in range(3):
                dim = par[6 + k : 7 + k].astype(jnp.int32)
                scale = par[9 + k : 10 + k]
                bias = par[12 + k : 13 + k]
                table = jnp.where(row == dim, scale, jnp.where(row == DIM, bias, 0.0))
                sel_ref[b, k] = table.astype(BF)

    def hats(sel_ref, basis_ref):
        for b in range(UNIT):
            basis = None
            for k in range(3):
                left = jnp.dot(qt_ref[...], sel_ref[b, k], preferred_element_type=F32)
                factor = jnp.maximum(jnp.minimum(left, 2.0 - left), 0.0)
                basis = factor if basis is None else basis * factor
            basis_ref[:, pl.ds(b * 256, 256)] = basis.astype(BF)

    def sums(u, basis_ref):
        weights = jnp.concatenate([block(u, b) for b in range(UNIT)], axis=1)
        acc_ref[u // RING] += lax.dot_general(
            basis_ref[...], weights, (((1,), (1,)), ((), ())), preferred_element_type=F32
        )

    acc_ref[...] = jnp.zeros_like(acc_ref)
    select(0, sel_a)
    select(1, sel_b)
    hats(sel_a, basis_a)
    select(2, sel_a)

    @pl.loop(0, units // 2 - 1)
    def _(it):
        u = 2 * it + 1
        hats(sel_b, basis_b)
        sums(u - 1, basis_a)
        select(u + 2, sel_b)
        hats(sel_a, basis_a)
        sums(u, basis_b)
        select(u + 3, sel_a)

    hats(sel_b, basis_b)
    sums(units - 2, basis_a)
    sums(units - 1, basis_b)

    for j, o in enumerate((o0, o1, o2, o3)):
        s = lax.rem(z + j, RING) * RING + y
        total = None
        for t in range(RING):
            value = acc_ref[t, pl.ds(j * 128, 128), :]
            count = counts_ref[s, z * RING + t].astype(F32)
            term = count * jnp.exp(-GAMMA * value + pltpu.roll(value, 128 - DIM, 1))
            total = term if total is None else total + term
        o[...] = total.T[:HALF]


def partial_sums(where, counts, tables, queries):
    vm = pl.BlockSpec(memory_space=pltpu.VMEM)
    sm = pl.BlockSpec(memory_space=pltpu.SMEM)
    return pl.pallas_call(
        kernel,
        out_shape=[jax.ShapeDtypeStruct((HALF, 128), F32)] * RING,
        in_specs=[sm, sm] + [vm] * 6,
        out_specs=[vm] * RING,
        scratch_shapes=[
            pltpu.VMEM((512, HALF), BF),
            pltpu.VMEM((UNIT, 3, HALF, 256), BF),
            pltpu.VMEM((UNIT, 3, HALF, 256), BF),
            pltpu.VMEM((512, UNIT * 256), BF),
            pltpu.VMEM((512, UNIT * 256), BF),
            pltpu.VMEM((RING, 512, 128), F32),
        ],
        compiler_params=pltpu.CompilerParams(vmem_limit_bytes=40 << 20),
        name="euler_basis",
    )(where, counts, *tables, *queries)


def shift(dz):
    return [(z * RING + y, (z + dz) % RING * RING + y) for z in range(RING) for y in range(RING)]


def spread(current):
    nq = current.shape[1]
    own = jnp.concatenate([current.astype(BF), jnp.ones((1, nq), BF), jnp.zeros((HALF - DIM - 1, nq), BF)], axis=0)
    return [own] + [lax.ppermute(own, "shk", shift(-j)) for j in range(1, RING)]


def per_device(savings, wealth, surplus, point_dims, point_levels, point_index, live_count, trans_counts):
    blocks = pack(surplus[0], point_dims, point_levels, point_index, live_count)
    groups = [
        [(2 * x + c) * 16 + z * RING + y for x in range(RING) for y in range(RING)] for c in range(2) for z in range(RING)
    ]
    mine = lax.all_to_all(blocks, ("pts", "shk"), 0, 0, tiled=True, axis_index_groups=groups)
    current = savings[0]
    income = wealth[0]
    queries = spread(current)
    mine, *queries = lax.optimization_barrier((mine, *queries))
    tables = (mine, lax.ppermute(mine, "pts", [(i, i ^ 1) for i in range(8)]))
    shock = lax.axis_index("shk")
    where = jnp.stack([shock // RING, shock % RING]).astype(jnp.int32)
    rowsum = jnp.sum(lax.dynamic_index_in_dim(trans_counts, shock, 0, keepdims=False))
    for sweep in range(ITERS):
        if sweep:
            queries = spread(current)
        parts = partial_sums(where, trans_counts, tables, queries)
        got = [parts[0]] + [lax.ppermute(parts[j], "shk", shift(j)) for j in range(1, RING)]
        if sweep == ITERS - 1:
            return finish(rowsum[None], current, jnp.transpose(wealth, (1, 0, 2)), got)
        expect = ((got[0] + got[1]) + (got[2] + got[3]))[:DIM] / rowsum.astype(F32)
        consumption = (BETA * expect) ** (-1.0 / GAMMA)
        current = (1.0 - damping) * current + damping * jax.nn.sigmoid(income - consumption)


def solution(mesh):
    return jax.shard_map(
        per_device,
        mesh=mesh,
        in_specs=(
            P("shk", None, "pts"),
            P("shk", None, "pts"),
            P("shk", None, "pts"),
            P("shk", None, "pts"),
            P("shk", None, "pts"),
            P("shk", None, "pts"),
            P("shk", "pts"),
            P(),
        ),
        out_specs=(P("shk", None, "pts"), P("shk", None, "pts")),
        check_vma=False,
    )
```

time: 92.3 us -> 80.5 us (0.87)
  waiting for transfers between devices: 34.7 us -> 21.2 us
  starting transfers between devices: 24.3 us -> 28.8 us
  other arithmetic: 5.24 us -> 0.98 us
  Pallas kernels: 23.1 us -> 25.4 us
  local copies, waits for them, and re-layouts: 3.11 us -> 1.68 us
    all_to_all x1, waiting for transfers between devices: 18.7 us -> 8.19 us  [per_device(): lax.all_to_all(blocks, ('pts', 'shk'), 0, 0, tiled=True, axis_index_group...]
    ppermute x6, waiting for transfers between devices: 8.54 us -> 4.46 us  [per_device(): lax.ppermute(parts[j], 'shk', shift(j))]
    ppermute x6, starting transfers between devices: 7.96 us -> 10.8 us  [per_device(): lax.ppermute(parts[j], 'shk', shift(j))]
    pallas_call x0 -> x2, Pallas kernels: none -> 2.42 us  [the longest x1 1.31 us: finish(): pl.pallas_call(finish_kernel, out_shape=[flat, flat], in_specs=[sm, vm, v...]
    ppermute x6 -> x7, starting transfers between devices: 8.82 us -> 10.8 us  [the longest x6 10.8 us: spread(): return [own] + [lax.ppermute(own, 'shk', shift(-j)) for j in range(1, RING)]]
    broadcast_in_dim x2 -> x0, local copies, waits for them, and re-layouts: 1.58 us -> none  [the longest x1 1.57 us: per_device(): jnp.broadcast_to(block[None], (32,) + block.shape)]
    another operation x2 -> x0, other arithmetic: 1.49 us -> none
    convert_element_type x2 -> x1, other arithmetic: 1.38 us -> 0.05 us  [spread(): current.astype(BF)]
  transfers between devices with their start and end apart: 13 -> 14, of which waited for: 10 -> 11; matrix products, arithmetic and copies ran while one was open for 1% -> 1% of each run, Pallas kernels for 0% -> 0%
where the time goes in v3:
time: 80.5 us; the launch traced here: 80.1 us
  starting transfers between devices  28.8 us (36%)
  Pallas kernels  25.4 us (32%)
  waiting for transfers between devices  21.2 us (26%)
  between operations  2.03 us (3%)
  local copies, waits for them, and re-layouts  1.68 us (2%)
  other arithmetic  0.98 us (1%)
    pallas_call x2, Pallas kernels, partial_sums(): pl.pallas_call(kernel, out_shape=[jax.ShapeDtypeStruct((HALF, 128), F32)]...  22.9 us
    ppermute x6, starting transfers between devices, per_device(): lax.ppermute(parts[j], 'shk', shift(j))  10.8 us
    ppermute x6, starting transfers between devices, spread(): return [own] + [lax.ppermute(own, 'shk', shift(-j)) for j in range(1, RING)]  10.8 us
    all_to_all x1, waiting for transfers between devices, per_device(): lax.all_to_all(blocks, ('pts', 'shk'), 0, 0, tiled=True, axis_index_group...  8.19 us
    all_to_all x1, starting transfers between devices, per_device(): lax.all_to_all(blocks, ('pts', 'shk'), 0, 0, tiled=True, axis_index_group...  7.28 us
    ppermute x6, waiting for transfers between devices, spread(): return [own] + [lax.ppermute(own, 'shk', shift(-j)) for j in range(1, RING)]  6.01 us
    ppermute x6, waiting for transfers between devices, per_device(): lax.ppermute(parts[j], 'shk', shift(j))  4.46 us
    ppermute x1, waiting for transfers between devices, per_device(): tables = (mine, lax.ppermute(mine, 'pts', [(i, i ^ 1) for i in range(8)]))  2.58 us
  transfers between devices with their start and end apart: 14, of which 11 were waited for; matrix products, arithmetic and copies ran while one was open for 1% of the time, Pallas kernels for 0%

profile of v3, /device:TPU:0, one launch (start us, length us, event | category | flops | bytes accessed | tf_op | source)
XLA Modules:
  0.0 80.1 jit_solution(5082264886046222002)
XLA Ops:
  2.0 0.8 %copy-done.1 = bf16[1,118,256]{2,1,0:T(8,128)(2,1)S(1)} copy-done((bf16[1,118,256]{2,1,0:T(8,128)(2,1)S(1)}, bf16[1,118,256]{2,1,0:T(8,128)(2,1)}, u32[]{:S(2)}) %copy-start.1) | copy-done | bytes 60440
  2.8 1.1 %pack_tables.1 = bf16[16,128,256]{2,1,0:T(8,128)(2,1)} custom-call(s32[1,1]{1,0:T(1,128)S(6)} %copy.20.live_ref, bf16[118,256]{1,0:T(8,128)(2,1)S(1)} %bitcast.24, s32[3,1,256]{2,1,0:T(1,128)S(1)} %bitcast.25, s32[3,1,256]{2,1,0:T(1,128)S(1)} %bitcast.26, s32[3,1,256]{2,1,0:T(1,128)S(1)} %bitcast.27), custom_call_target="tpu_custom_call" | custom-call | tf_op jit(solution)/shard_map/pack_tables/pallas_call | solution.py:44
  3.9 7.3 %all-to-all-start = ((bf16[16,128,256]{2,1,0:T(8,128)(2,1)}), bf16[16,128,256]{2,1,0:T(8,128)(2,1)S(1)}, u32[]{:S(2)}, u32[]{:S(2)}) async-start(bf16[16,128,256]{2,1,0:T(8,128)(2,1)} %pack_tables.1), calls=%async_computation | async-start | bytes 2097152 | tf_op jit(solution)/shard_map/all_to_all | solution.py:183
  11.5 2.0 %collective-permute-start.2 = (bf16[64,128]{1,0:T(8,128)(2,1)S(1)}, bf16[64,128]{1,0:T(8,128)(2,1)S(1)}, u32[]{:S(2)}, u32[]{:S(2)}) collective-permute-start(bf16[64,128]{1,0:T(8,128)(2,1)S(1)} %maximum_maximum_fusion.q0), channel_id=1, source_target_pairs={{0,4},{1,5},{2,6},{3,7},{4,8},{5,9},{6,10},{7,11},{8,12},{9,13},{1... | collective-permute-start | bytes 49160 | tf_op jit(solution)/shard_map/ppermute | solution.py:175
  13.5 3.6 %collective-permute-start.1 = (bf16[64,128]{1,0:T(8,128)(2,1)S(1)}, bf16[64,128]{1,0:T(8,128)(2,1)S(1)}, u32[]{:S(2)}, u32[]{:S(2)}) collective-permute-start(bf16[64,128]{1,0:T(8,128)(2,1)S(1)} %maximum_maximum_fusion.q0), channel_id=1, source_target_pairs={{0,8},{1,9},{2,10},{3,11},{4,12},{5,13},{6,14},{7,15},{8,0},{9,1},... | collective-permute-start | bytes 49160 | tf_op jit(solution)/shard_map/ppermute | solution.py:175
  17.1 1.0 %collective-permute-start = (bf16[64,128]{1,0:T(8,128)(2,1)S(1)}, bf16[64,128]{1,0:T(8,128)(2,1)S(1)}, u32[]{:S(2)}, u32[]{:S(2)}) collective-permute-start(bf16[64,128]{1,0:T(8,128)(2,1)S(1)} %maximum_maximum_fusion.q0), channel_id=1, source_target_pairs={{0,12},{1,13},{2,14},{3,15},{4,0},{5,1},{6,2},{7,3},{8,4},{9,5},{1... | collective-permute-start | bytes 49160 | tf_op jit(solution)/shard_map/ppermute | solution.py:175
  18.1 0.9 %collective-permute-done.1.q2 = bf16[64,128]{1,0:T(8,128)(2,1)S(1)} collective-permute-done((bf16[64,128]{1,0:T(8,128)(2,1)S(1)}, bf16[64,128]{1,0:T(8,128)(2,1)S(1)}, u32[]{:S(2)}, u32[]{:S(2)}) %collective-permute-start.1) | collective-permute-done | bytes 16416 | tf_op jit(solution)/shard_map/ppermute | solution.py:175
  18.9 1.9 %collective-permute-done.q1 = bf16[64,128]{1,0:T(8,128)(2,1)S(1)} collective-permute-done((bf16[64,128]{1,0:T(8,128)(2,1)S(1)}, bf16[64,128]{1,0:T(8,128)(2,1)S(1)}, u32[]{:S(2)}, u32[]{:S(2)}) %collective-permute-start) | collective-permute-done | bytes 16416 | tf_op jit(solution)/shard_map/ppermute | solution.py:175
  20.8 8.2 %all-to-all-done.tab_a = bf16[16,128,256]{2,1,0:T(8,128)(2,1)S(1)} async-done(((bf16[16,128,256]{2,1,0:T(8,128)(2,1)}), bf16[16,128,256]{2,1,0:T(8,128)(2,1)S(1)}, u32[]{:S(2)}, u32[]{:S(2)}) %all-to-all-start) | async-done | bytes 1048608 | tf_op jit(solution)/shard_map/all_to_all | solution.py:183
  29.1 2.6 %collective-permute-done.3.tab_b = bf16[16,128,256]{2,1,0:T(8,128)(2,1)S(1)} collective-permute-done((bf16[16,128,256]{2,1,0:T(8,128)(2,1)S(1)}, bf16[16,128,256]{2,1,0:T(8,128)(2,1)S(1)}, u32[]{:S(2)}, u32[]{:S(2)}) %collective-permute-start.3) | collective-permute-done | bytes 1048608 | tf_op jit(solution)/shard_map/ppermute | solution.py:188
  31.6 11.5 %euler_basis.2 = (f32[64,128]{1,0:T(8,128)S(1)}, f32[64,128]{1,0:T(8,128)S(1)}, f32[64,128]{1,0:T(8,128)S(1)}, f32[64,128]{1,0:T(8,128)S(1)}) custom-call(s32[2]{0:T(128)S(1)} %pad_add_fusion.where_ref, s32[16,16]{1,0:T(8,128)S(1)} %copy-done.2, bf16[16,128,256]{2,1,0:T(8,128)(2,1)S(1)} %all-to-all-done.tab_a, ...), custom_call_target="tpu_custom_call" | custom-call | tf_op jit(solution)/shard_map/euler_basis/pallas_call | solution.py:150
  43.1 2.0 %collective-permute-start.4 = (f32[64,128]{1,0:T(8,128)S(1)}, f32[64,128]{1,0:T(8,128)S(1)}, u32[]{:S(2)}, u32[]{:S(2)}) collective-permute-start(f32[64,128]{1,0:T(8,128)S(1)} %get-tuple-element.23), channel_id=1, source_target_pairs={{0,4},{1,5},{2,6},{3,7},{4,8},{5,9},{6,10},{7,11},{8,12},{9,13},{1... | collective-permute-start | bytes 98312 | tf_op jit(solution)/shard_map/ppermute | solution.py:196
  45.1 3.6 %collective-permute-start.5 = (f32[64,128]{1,0:T(8,128)S(1)}, f32[64,128]{1,0:T(8,128)S(1)}, u32[]{:S(2)}, u32[]{:S(2)}) collective-permute-start(f32[64,128]{1,0:T(8,128)S(1)} %get-tuple-element.24), channel_id=1, source_target_pairs={{0,8},{1,9},{2,10},{3,11},{4,12},{5,13},{6,14},{7,15},{8,0},{9,1},... | collective-permute-start | bytes 98312 | tf_op jit(solution)/shard_map/ppermute | solution.py:196
  48.7 1.0 %collective-permute-start.6 = (f32[64,128]{1,0:T(8,128)S(1)}, f32[64,128]{1,0:T(8,128)S(1)}, u32[]{:S(2)}, u32[]{:S(2)}) collective-permute-start(f32[64,128]{1,0:T(8,128)S(1)} %get-tuple-element.25), channel_id=1, source_target_pairs={{0,12},{1,13},{2,14},{3,15},{4,0},{5,1},{6,2},{7,3},{8,4},{9,5},{1... | collective-permute-start | bytes 98312 | tf_op jit(solution)/shard_map/ppermute | solution.py:196
  51.0 1.6 %collective-permute-done.6 = f32[64,128]{1,0:T(8,128)S(1)} collective-permute-done((f32[64,128]{1,0:T(8,128)S(1)}, f32[64,128]{1,0:T(8,128)S(1)}, u32[]{:S(2)}, u32[]{:S(2)}) %collective-permute-start.6) | collective-permute-done | bytes 32800 | tf_op jit(solution)/shard_map/ppermute | solution.py:196
  52.8 3.7 %collective-permute-start.8 = (bf16[64,128]{1,0:T(8,128)(2,1)S(1)}, bf16[64,128]{1,0:T(8,128)(2,1)S(1)}, u32[]{:S(2)}, u32[]{:S(2)}) collective-permute-start(bf16[64,128]{1,0:T(8,128)(2,1)S(1)} %maximum_maximum_fusion.1.q0), channel_id=1, source_target_pairs={{0,8},{1,9},{2,10},{3,11},{4,12},{5,13},{6,14},{7,15},{8,0},{9,1},... | collective-permute-start | bytes 49160 | tf_op jit(solution)/shard_map/ppermute | solution.py:175
  56.9 0.8 %collective-permute-done.9.q3 = bf16[64,128]{1,0:T(8,128)(2,1)S(1)} collective-permute-done((bf16[64,128]{1,0:T(8,128)(2,1)S(1)}, bf16[64,128]{1,0:T(8,128)(2,1)S(1)}, u32[]{:S(2)}, u32[]{:S(2)}) %collective-permute-start.9) | collective-permute-done | bytes 16416 | tf_op jit(solution)/shard_map/ppermute | solution.py:175
  58.4 1.9 %collective-permute-done.7.q1 = bf16[64,128]{1,0:T(8,128)(2,1)S(1)} collective-permute-done((bf16[64,128]{1,0:T(8,128)(2,1)S(1)}, bf16[64,128]{1,0:T(8,128)(2,1)S(1)}, u32[]{:S(2)}, u32[]{:S(2)}) %collective-permute-start.7) | collective-permute-done | bytes 16416 | tf_op jit(solution)/shard_map/ppermute | solution.py:175
  60.2 11.5 %euler_basis.3 = (f32[64,128]{1,0:T(8,128)S(1)}, f32[64,128]{1,0:T(8,128)S(1)}, f32[64,128]{1,0:T(8,128)S(1)}, f32[64,128]{1,0:T(8,128)S(1)}) custom-call(s32[2]{0:T(128)S(1)} %pad_add_fusion.where_ref, s32[16,16]{1,0:T(8,128)S(1)} %copy-done.2, bf16[16,128,256]{2,1,0:T(8,128)(2,1)S(1)} %all-to-all-done.tab_a, ...), custom_call_target="tpu_custom_call" | custom-call | tf_op jit(solution)/shard_map/euler_basis/pallas_call | solution.py:150
  72.2 2.7 %collective-permute-start.11 = (f32[64,128]{1,0:T(8,128)S(1)}, f32[64,128]{1,0:T(8,128)S(1)}, u32[]{:S(2)}, u32[]{:S(2)}) collective-permute-start(f32[64,128]{1,0:T(8,128)S(1)} %get-tuple-element.28), channel_id=1, source_target_pairs={{0,8},{1,9},{2,10},{3,11},{4,12},{5,13},{6,14},{7,15},{8,0},{9,1},... | collective-permute-start | bytes 98312 | tf_op jit(solution)/shard_map/ppermute | solution.py:196
  74.9 1.0 %collective-permute-start.12 = (f32[64,128]{1,0:T(8,128)S(1)}, f32[64,128]{1,0:T(8,128)S(1)}, u32[]{:S(2)}, u32[]{:S(2)}) collective-permute-start(f32[64,128]{1,0:T(8,128)S(1)} %get-tuple-element.29), channel_id=1, source_target_pairs={{0,12},{1,13},{2,14},{3,15},{4,0},{5,1},{6,2},{7,3},{8,4},{9,5},{1... | collective-permute-start | bytes 98312 | tf_op jit(solution)/shard_map/ppermute | solution.py:196
  75.9 1.0 %collective-permute-done.10.g1 = f32[64,128]{1,0:T(8,128)S(1)} collective-permute-done((f32[64,128]{1,0:T(8,128)S(1)}, f32[64,128]{1,0:T(8,128)S(1)}, u32[]{:S(2)}, u32[]{:S(2)}) %collective-permute-start.10) | collective-permute-done | bytes 32800 | tf_op jit(solution)/shard_map/ppermute | solution.py:196
  77.6 1.2 %collective-permute-done.12.g3 = f32[64,128]{1,0:T(8,128)S(1)} collective-permute-done((f32[64,128]{1,0:T(8,128)S(1)}, f32[64,128]{1,0:T(8,128)S(1)}, u32[]{:S(2)}, u32[]{:S(2)}) %collective-permute-start.12) | collective-permute-done | bytes 32800 | tf_op jit(solution)/shard_map/ppermute | solution.py:196
  78.8 1.3 %finish.1 = (f32[59,1,128]{2,1,0:T(1,128)}, f32[59,1,128]{2,1,0:T(1,128)}) custom-call(s32[1]{0:T(128)} %bitcast.rowsum_ref, f32[59,128]{1,0:T(8,128)S(1)} %get-tuple-element.33.now_ref, f32[59,1,128]{2,1,0:T(1,128)S(1)} %bitcast.23, f32[64,128]{1,0:T(8,128)S(1)} %get-tuple-element.26.g0, f32[64,128]{1,0:T(8,128)S(1)} %collective-permute-done.10.g1, ...), custom_call_target="tpu_custom_call" | custom-call | tf_op jit(solution)/shard_map/finish/pallas_call | solution.py:68
  (31 shorter events, 4.2 us)
Async XLA Ops:
  0.6 0.7 copy-start.5
  1.3 0.7 copy-start.4
  1.3 0.7 copy-start.3
  2.0 0.8 %copy-start.1 = (bf16[1,118,256]{2,1,0:T(8,128)(2,1)S(1)}, bf16[1,118,256]{2,1,0:T(8,128)(2,1)}, u32[]{:S(2)}) copy-start(bf16[1,118,256]{2,1,0:T(8,128)(2,1)} %param.10) | copy-start | bytes 181252
  3.9 7.4 %copy-start.6 = (f32[1,59,128]{2,0,1:T(1,128)S(1)}, f32[1,59,128]{2,0,1:T(1,128)}, u32[]{:S(2)}) copy-start(f32[1,59,128]{2,0,1:T(1,128)} %param.8) | copy-start | bytes 90628
  3.9 25.0 %all-to-all-start = ((bf16[16,128,256]{2,1,0:T(8,128)(2,1)}), bf16[16,128,256]{2,1,0:T(8,128)(2,1)S(1)}, u32[]{:S(2)}, u32[]{:S(2)}) async-start(bf16[16,128,256]{2,1,0:T(8,128)(2,1)} %pack_tables.1), calls=%async_computation | async-start | bytes 2097152 | tf_op jit(solution)/shard_map/all_to_all | solution.py:183
  11.5 6.6 %collective-permute-start.2 = (bf16[64,128]{1,0:T(8,128)(2,1)S(1)}, bf16[64,128]{1,0:T(8,128)(2,1)S(1)}, u32[]{:S(2)}, u32[]{:S(2)}) collective-permute-start(bf16[64,128]{1,0:T(8,128)(2,1)S(1)} %maximum_maximum_fusion.q0), channel_id=1, source_target_pairs={{0,4},{1,5},{2,6},{3,7},{4,8},{5,9},{6,10},{7,11},{8,12},{9,13},{1... | collective-permute-start | bytes 49160 | tf_op jit(solution)/shard_map/ppermute | solution.py:175
  13.5 5.5 %collective-permute-start.1 = (bf16[64,128]{1,0:T(8,128)(2,1)S(1)}, bf16[64,128]{1,0:T(8,128)(2,1)S(1)}, u32[]{:S(2)}, u32[]{:S(2)}) collective-permute-start(bf16[64,128]{1,0:T(8,128)(2,1)S(1)} %maximum_maximum_fusion.q0), channel_id=1, source_target_pairs={{0,8},{1,9},{2,10},{3,11},{4,12},{5,13},{6,14},{7,15},{8,0},{9,1},... | collective-permute-start | bytes 49160 | tf_op jit(solution)/shard_map/ppermute | solution.py:175
  17.1 3.7 %collective-permute-start = (bf16[64,128]{1,0:T(8,128)(2,1)S(1)}, bf16[64,128]{1,0:T(8,128)(2,1)S(1)}, u32[]{:S(2)}, u32[]{:S(2)}) collective-permute-start(bf16[64,128]{1,0:T(8,128)(2,1)S(1)} %maximum_maximum_fusion.q0), channel_id=1, source_target_pairs={{0,12},{1,13},{2,14},{3,15},{4,0},{5,1},{6,2},{7,3},{8,4},{9,5},{1... | collective-permute-start | bytes 49160 | tf_op jit(solution)/shard_map/ppermute | solution.py:175
  29.0 2.7 %collective-permute-start.3 = (bf16[16,128,256]{2,1,0:T(8,128)(2,1)S(1)}, bf16[16,128,256]{2,1,0:T(8,128)(2,1)S(1)}, u32[]{:S(2)}, u32[]{:S(2)}) collective-permute-start(bf16[16,128,256]{2,1,0:T(8,128)(2,1)S(1)} %all-to-all-done.tab_a), channel_id=1, source_target_pairs={{0,16},{16,0},{32,48},{48,32},{64,80},{80,64},{96,112},{112,96},{1... | collective-permute-start | bytes 3145736 | tf_op jit(solution)/shard_map/ppermute | solution.py:188
  29.0 2.7 %copy-start.2 = (s32[16,16]{1,0:T(8,128)S(1)}, s32[16,16]{1,0:T(8,128)}, u32[]{:S(2)}) copy-start(s32[16,16]{1,0:T(8,128)} %counts_ref.3) | copy-start | bytes 3076
  31.6 21.0 %copy-start = (f32[1,59,128]{2,0,1:T(1,128)S(1)}, f32[1,59,128]{2,0,1:T(1,128)}, u32[]{:S(2)}) copy-start(f32[1,59,128]{2,0,1:T(1,128)} %param.9) | copy-start | bytes 90628
  43.1 7.9 %collective-permute-start.4 = (f32[64,128]{1,0:T(8,128)S(1)}, f32[64,128]{1,0:T(8,128)S(1)}, u32[]{:S(2)}, u32[]{:S(2)}) collective-permute-start(f32[64,128]{1,0:T(8,128)S(1)} %get-tuple-element.23), channel_id=1, source_target_pairs={{0,4},{1,5},{2,6},{3,7},{4,8},{5,9},{6,10},{7,11},{8,12},{9,13},{1... | collective-permute-start | bytes 98312 | tf_op jit(solution)/shard_map/ppermute | solution.py:196
  45.1 5.9 %collective-permute-start.5 = (f32[64,128]{1,0:T(8,128)S(1)}, f32[64,128]{1,0:T(8,128)S(1)}, u32[]{:S(2)}, u32[]{:S(2)}) collective-permute-start(f32[64,128]{1,0:T(8,128)S(1)} %get-tuple-element.24), channel_id=1, source_target_pairs={{0,8},{1,9},{2,10},{3,11},{4,12},{5,13},{6,14},{7,15},{8,0},{9,1},... | collective-permute-start | bytes 98312 | tf_op jit(solution)/shard_map/ppermute | solution.py:196
  48.7 3.9 %collective-permute-start.6 = (f32[64,128]{1,0:T(8,128)S(1)}, f32[64,128]{1,0:T(8,128)S(1)}, u32[]{:S(2)}, u32[]{:S(2)}) collective-permute-start(f32[64,128]{1,0:T(8,128)S(1)} %get-tuple-element.25), channel_id=1, source_target_pairs={{0,12},{1,13},{2,14},{3,15},{4,0},{5,1},{6,2},{7,3},{8,4},{9,5},{1... | collective-permute-start | bytes 98312 | tf_op jit(solution)/shard_map/ppermute | solution.py:196
  52.7 5.0 %collective-permute-start.9 = (bf16[64,128]{1,0:T(8,128)(2,1)S(1)}, bf16[64,128]{1,0:T(8,128)(2,1)S(1)}, u32[]{:S(2)}, u32[]{:S(2)}) collective-permute-start(bf16[64,128]{1,0:T(8,128)(2,1)S(1)} %maximum_maximum_fusion.1.q0), channel_id=1, source_target_pairs={{0,4},{1,5},{2,6},{3,7},{4,8},{5,9},{6,10},{7,11},{8,12},{9,13},{1... | collective-permute-start | bytes 49160 | tf_op jit(solution)/shard_map/ppermute | solution.py:175
  52.8 5.6 %collective-permute-start.8 = (bf16[64,128]{1,0:T(8,128)(2,1)S(1)}, bf16[64,128]{1,0:T(8,128)(2,1)S(1)}, u32[]{:S(2)}, u32[]{:S(2)}) collective-permute-start(bf16[64,128]{1,0:T(8,128)(2,1)S(1)} %maximum_maximum_fusion.1.q0), channel_id=1, source_target_pairs={{0,8},{1,9},{2,10},{3,11},{4,12},{5,13},{6,14},{7,15},{8,0},{9,1},... | collective-permute-start | bytes 49160 | tf_op jit(solution)/shard_map/ppermute | solution.py:175
  56.5 3.7 %collective-permute-start.7 = (bf16[64,128]{1,0:T(8,128)(2,1)S(1)}, bf16[64,128]{1,0:T(8,128)(2,1)S(1)}, u32[]{:S(2)}, u32[]{:S(2)}) collective-permute-start(bf16[64,128]{1,0:T(8,128)(2,1)S(1)} %maximum_maximum_fusion.1.q0), channel_id=1, source_target_pairs={{0,12},{1,13},{2,14},{3,15},{4,0},{5,1},{6,2},{7,3},{8,4},{9,5},{1... | collective-permute-start | bytes 49160 | tf_op jit(solution)/shard_map/ppermute | solution.py:175
  71.7 5.2 %collective-permute-start.10 = (f32[64,128]{1,0:T(8,128)S(1)}, f32[64,128]{1,0:T(8,128)S(1)}, u32[]{:S(2)}, u32[]{:S(2)}) collective-permute-start(f32[64,128]{1,0:T(8,128)S(1)} %get-tuple-element.27), channel_id=1, source_target_pairs={{0,4},{1,5},{2,6},{3,7},{4,8},{5,9},{6,10},{7,11},{8,12},{9,13},{1... | collective-permute-start | bytes 98312 | tf_op jit(solution)/shard_map/ppermute | solution.py:196
  72.2 5.4 %collective-permute-start.11 = (f32[64,128]{1,0:T(8,128)S(1)}, f32[64,128]{1,0:T(8,128)S(1)}, u32[]{:S(2)}, u32[]{:S(2)}) collective-permute-start(f32[64,128]{1,0:T(8,128)S(1)} %get-tuple-element.28), channel_id=1, source_target_pairs={{0,8},{1,9},{2,10},{3,11},{4,12},{5,13},{6,14},{7,15},{8,0},{9,1},... | collective-permute-start | bytes 98312 | tf_op jit(solution)/shard_map/ppermute | solution.py:196
  74.9 3.9 %collective-permute-start.12 = (f32[64,128]{1,0:T(8,128)S(1)}, f32[64,128]{1,0:T(8,128)S(1)}, u32[]{:S(2)}, u32[]{:S(2)}) collective-permute-start(f32[64,128]{1,0:T(8,128)S(1)} %get-tuple-element.29), channel_id=1, source_target_pairs={{0,12},{1,13},{2,14},{3,15},{4,0},{5,1},{6,2},{7,3},{8,4},{9,5},{1... | collective-permute-start | bytes 98312 | tf_op jit(solution)/shard_map/ppermute | solution.py:196

commit v4 on v3

--- a/solution.py
+++ b/solution.py
@@ -15,6 +15,8 @@
 UNIT = 2
 BF = jnp.bfloat16
 F32 = jnp.float32
+F8 = jnp.float8_e4m3fn
+SPLIT = 32.0
 
 
 def pack_kernel(live_ref, surplus_ref, dims_ref, levels_ref, index_ref, o_ref):
@@ -81,8 +83,12 @@
 ):
     z, y = where_ref[0], where_ref[1]
     for j, q in enumerate((q0, q1, q2, q3)):
-        qt_ref[pl.ds(j * 128, 128), :] = q[...].astype(F32).T.astype(BF)
-    row = lax.broadcasted_iota(jnp.int32, (HALF, 256), 0)
+        whole = q[...].astype(F32)
+        whole = jnp.where(lax.broadcasted_iota(jnp.int32, whole.shape, 0) < DIM, whole * SPLIT, whole)
+        high = whole.astype(F8).astype(F32)
+        qt_ref[pl.ds(j * 128, 128), :] = jnp.concatenate([high, whole - high], axis=0).T.astype(F8)
+    row = lax.broadcasted_iota(jnp.int32, (2 * HALF, 256), 0)
+    coord = row % HALF
     units = 8 * RING // UNIT
 
     def block(u, b):
@@ -93,19 +99,19 @@
             par = block(jnp.minimum(u, units - 1), b)[112:128].astype(F32)
             for k in range(3):
                 dim = par[6 + k : 7 + k].astype(jnp.int32)
-                scale = par[9 + k : 10 + k]
+                scale = par[9 + k : 10 + k] * (1.0 / SPLIT)
                 bias = par[12 + k : 13 + k]
-                table = jnp.where(row == dim, scale, jnp.where(row == DIM, bias, 0.0))
-                sel_ref[b, k] = table.astype(BF)
+                table = jnp.where(coord == dim, scale, jnp.where(row == DIM, bias, 0.0))
+                sel_ref[b, k] = table.astype(F8)
 
     def hats(sel_ref, basis_ref):
         for b in range(UNIT):
             basis = None
             for k in range(3):
-                left = jnp.dot(qt_ref[...], sel_ref[b, k], preferred_element_type=F32)
-                factor = jnp.maximum(jnp.minimum(left, 2.0 - left), 0.0)
+                left = jnp.dot(qt_ref[...], sel_ref[b, k], preferred_element_type=F32).astype(BF)
+                factor = jnp.maximum(jnp.minimum(left, BF(2.0) - left), BF(0.0))
                 basis = factor if basis is None else basis * factor
-            basis_ref[:, pl.ds(b * 256, 256)] = basis.astype(BF)
+            basis_ref[:, pl.ds(b * 256, 256)] = basis
 
     def sums(u, basis_ref):
         weights = jnp.concatenate([block(u, b) for b in range(UNIT)], axis=1)
@@ -153,9 +159,9 @@
         in_specs=[sm, sm] + [vm] * 6,
         out_specs=[vm] * RING,
         scratch_shapes=[
-            pltpu.VMEM((512, HALF), BF),
-            pltpu.VMEM((UNIT, 3, HALF, 256), BF),
-            pltpu.VMEM((UNIT, 3, HALF, 256), BF),
+            pltpu.VMEM((512, 2 * HALF), F8),
+            pltpu.VMEM((UNIT, 3, 2 * HALF, 256), F8),
+            pltpu.VMEM((UNIT, 3, 2 * HALF, 256), F8),
             pltpu.VMEM((512, UNIT * 256), BF),
             pltpu.VMEM((512, UNIT * 256), BF),
             pltpu.VMEM((RING, 512, 128), F32),

time: 80.5 us -> 74.7 us (0.928)
  Pallas kernels: 25.4 us -> 19.5 us
    pallas_call x2, Pallas kernels: 22.9 us -> 17.1 us  [partial_sums(): pl.pallas_call(kernel, out_shape=[jax.ShapeDtypeStruct((HALF, 128), F32)]...]
where the time goes in v4:
time: 74.7 us; the launch traced here: 74.3 us
  starting transfers between devices  28.8 us (39%)
  waiting for transfers between devices  21.2 us (28%)
  Pallas kernels  19.5 us (26%)
  between operations  2.03 us (3%)
  local copies, waits for them, and re-layouts  1.68 us (2%)
  other arithmetic  0.98 us (1%)
    pallas_call x2, Pallas kernels, partial_sums(): pl.pallas_call(kernel, out_shape=[jax.ShapeDtypeStruct((HALF, 128), F32)]...  17.1 us
    ppermute x6, starting transfers between devices, per_device(): lax.ppermute(parts[j], 'shk', shift(j))  10.8 us
    ppermute x6, starting transfers between devices, spread(): return [own] + [lax.ppermute(own, 'shk', shift(-j)) for j in range(1, RING)]  10.8 us
    all_to_all x1, waiting for transfers between devices, per_device(): lax.all_to_all(blocks, ('pts', 'shk'), 0, 0, tiled=True, axis_index_group...  8.19 us
    all_to_all x1, starting transfers between devices, per_device(): lax.all_to_all(blocks, ('pts', 'shk'), 0, 0, tiled=True, axis_index_group...  7.28 us
    ppermute x6, waiting for transfers between devices, spread(): return [own] + [lax.ppermute(own, 'shk', shift(-j)) for j in range(1, RING)]  6.01 us
    ppermute x6, waiting for transfers between devices, per_device(): lax.ppermute(parts[j], 'shk', shift(j))  4.47 us
    ppermute x1, waiting for transfers between devices, per_device(): tables = (mine, lax.ppermute(mine, 'pts', [(i, i ^ 1) for i in range(8)]))  2.58 us
  transfers between devices with their start and end apart: 14, of which 11 were waited for; matrix products, arithmetic and copies ran while one was open for 1% of the time, Pallas kernels for 0%

profile of v4, /device:TPU:0, one launch (start us, length us, event | category | flops | bytes accessed | tf_op | source)
XLA Modules:
  0.0 74.3 jit_solution(3657281505677416924)
XLA Ops:
  2.0 0.8 %copy-done.1 = bf16[1,118,256]{2,1,0:T(8,128)(2,1)S(1)} copy-done((bf16[1,118,256]{2,1,0:T(8,128)(2,1)S(1)}, bf16[1,118,256]{2,1,0:T(8,128)(2,1)}, u32[]{:S(2)}) %copy-start.1) | copy-done | bytes 60440
  2.8 1.1 %pack_tables.1 = bf16[16,128,256]{2,1,0:T(8,128)(2,1)} custom-call(s32[1,1]{1,0:T(1,128)S(6)} %copy.20.live_ref, bf16[118,256]{1,0:T(8,128)(2,1)S(1)} %bitcast.24, s32[3,1,256]{2,1,0:T(1,128)S(1)} %bitcast.25, s32[3,1,256]{2,1,0:T(1,128)S(1)} %bitcast.26, s32[3,1,256]{2,1,0:T(1,128)S(1)} %bitcast.27), custom_call_target="tpu_custom_call" | custom-call | tf_op jit(solution)/shard_map/pack_tables/pallas_call | solution.py:46
  3.9 7.3 %all-to-all-start = ((bf16[16,128,256]{2,1,0:T(8,128)(2,1)}), bf16[16,128,256]{2,1,0:T(8,128)(2,1)S(1)}, u32[]{:S(2)}, u32[]{:S(2)}) async-start(bf16[16,128,256]{2,1,0:T(8,128)(2,1)} %pack_tables.1), calls=%async_computation | async-start | bytes 2097152 | tf_op jit(solution)/shard_map/all_to_all | solution.py:189
  11.5 2.0 %collective-permute-start.2 = (bf16[64,128]{1,0:T(8,128)(2,1)S(1)}, bf16[64,128]{1,0:T(8,128)(2,1)S(1)}, u32[]{:S(2)}, u32[]{:S(2)}) collective-permute-start(bf16[64,128]{1,0:T(8,128)(2,1)S(1)} %maximum_maximum_fusion.q0), channel_id=1, source_target_pairs={{0,4},{1,5},{2,6},{3,7},{4,8},{5,9},{6,10},{7,11},{8,12},{9,13},{1... | collective-permute-start | bytes 49160 | tf_op jit(solution)/shard_map/ppermute | solution.py:181
  13.5 3.6 %collective-permute-start.1 = (bf16[64,128]{1,0:T(8,128)(2,1)S(1)}, bf16[64,128]{1,0:T(8,128)(2,1)S(1)}, u32[]{:S(2)}, u32[]{:S(2)}) collective-permute-start(bf16[64,128]{1,0:T(8,128)(2,1)S(1)} %maximum_maximum_fusion.q0), channel_id=1, source_target_pairs={{0,8},{1,9},{2,10},{3,11},{4,12},{5,13},{6,14},{7,15},{8,0},{9,1},... | collective-permute-start | bytes 49160 | tf_op jit(solution)/shard_map/ppermute | solution.py:181
  17.1 1.0 %collective-permute-start = (bf16[64,128]{1,0:T(8,128)(2,1)S(1)}, bf16[64,128]{1,0:T(8,128)(2,1)S(1)}, u32[]{:S(2)}, u32[]{:S(2)}) collective-permute-start(bf16[64,128]{1,0:T(8,128)(2,1)S(1)} %maximum_maximum_fusion.q0), channel_id=1, source_target_pairs={{0,12},{1,13},{2,14},{3,15},{4,0},{5,1},{6,2},{7,3},{8,4},{9,5},{1... | collective-permute-start | bytes 49160 | tf_op jit(solution)/shard_map/ppermute | solution.py:181
  18.1 0.9 %collective-permute-done.1.q2 = bf16[64,128]{1,0:T(8,128)(2,1)S(1)} collective-permute-done((bf16[64,128]{1,0:T(8,128)(2,1)S(1)}, bf16[64,128]{1,0:T(8,128)(2,1)S(1)}, u32[]{:S(2)}, u32[]{:S(2)}) %collective-permute-start.1) | collective-permute-done | bytes 16416 | tf_op jit(solution)/shard_map/ppermute | solution.py:181
  18.9 1.9 %collective-permute-done.q1 = bf16[64,128]{1,0:T(8,128)(2,1)S(1)} collective-permute-done((bf16[64,128]{1,0:T(8,128)(2,1)S(1)}, bf16[64,128]{1,0:T(8,128)(2,1)S(1)}, u32[]{:S(2)}, u32[]{:S(2)}) %collective-permute-start) | collective-permute-done | bytes 16416 | tf_op jit(solution)/shard_map/ppermute | solution.py:181
  20.8 8.2 %all-to-all-done.tab_a = bf16[16,128,256]{2,1,0:T(8,128)(2,1)S(1)} async-done(((bf16[16,128,256]{2,1,0:T(8,128)(2,1)}), bf16[16,128,256]{2,1,0:T(8,128)(2,1)S(1)}, u32[]{:S(2)}, u32[]{:S(2)}) %all-to-all-start) | async-done | bytes 1048608 | tf_op jit(solution)/shard_map/all_to_all | solution.py:189
  29.1 2.6 %collective-permute-done.3.tab_b = bf16[16,128,256]{2,1,0:T(8,128)(2,1)S(1)} collective-permute-done((bf16[16,128,256]{2,1,0:T(8,128)(2,1)S(1)}, bf16[16,128,256]{2,1,0:T(8,128)(2,1)S(1)}, u32[]{:S(2)}, u32[]{:S(2)}) %collective-permute-start.3) | collective-permute-done | bytes 1048608 | tf_op jit(solution)/shard_map/ppermute | solution.py:194
  31.6 8.6 %euler_basis.2 = (f32[64,128]{1,0:T(8,128)S(1)}, f32[64,128]{1,0:T(8,128)S(1)}, f32[64,128]{1,0:T(8,128)S(1)}, f32[64,128]{1,0:T(8,128)S(1)}) custom-call(s32[2]{0:T(128)S(1)} %pad_add_fusion.where_ref, s32[16,16]{1,0:T(8,128)S(1)} %copy-done.2, bf16[16,128,256]{2,1,0:T(8,128)(2,1)S(1)} %all-to-all-done.tab_a, ...), custom_call_target="tpu_custom_call" | custom-call | tf_op jit(solution)/shard_map/euler_basis/pallas_call | solution.py:156
  40.2 2.0 %collective-permute-start.4 = (f32[64,128]{1,0:T(8,128)S(1)}, f32[64,128]{1,0:T(8,128)S(1)}, u32[]{:S(2)}, u32[]{:S(2)}) collective-permute-start(f32[64,128]{1,0:T(8,128)S(1)} %get-tuple-element.23), channel_id=1, source_target_pairs={{0,4},{1,5},{2,6},{3,7},{4,8},{5,9},{6,10},{7,11},{8,12},{9,13},{1... | collective-permute-start | bytes 98312 | tf_op jit(solution)/shard_map/ppermute | solution.py:202
  42.2 3.6 %collective-permute-start.5 = (f32[64,128]{1,0:T(8,128)S(1)}, f32[64,128]{1,0:T(8,128)S(1)}, u32[]{:S(2)}, u32[]{:S(2)}) collective-permute-start(f32[64,128]{1,0:T(8,128)S(1)} %get-tuple-element.24), channel_id=1, source_target_pairs={{0,8},{1,9},{2,10},{3,11},{4,12},{5,13},{6,14},{7,15},{8,0},{9,1},... | collective-permute-start | bytes 98312 | tf_op jit(solution)/shard_map/ppermute | solution.py:202
  45.8 1.0 %collective-permute-start.6 = (f32[64,128]{1,0:T(8,128)S(1)}, f32[64,128]{1,0:T(8,128)S(1)}, u32[]{:S(2)}, u32[]{:S(2)}) collective-permute-start(f32[64,128]{1,0:T(8,128)S(1)} %get-tuple-element.25), channel_id=1, source_target_pairs={{0,12},{1,13},{2,14},{3,15},{4,0},{5,1},{6,2},{7,3},{8,4},{9,5},{1... | collective-permute-start | bytes 98312 | tf_op jit(solution)/shard_map/ppermute | solution.py:202
  48.1 1.6 %collective-permute-done.6 = f32[64,128]{1,0:T(8,128)S(1)} collective-permute-done((f32[64,128]{1,0:T(8,128)S(1)}, f32[64,128]{1,0:T(8,128)S(1)}, u32[]{:S(2)}, u32[]{:S(2)}) %collective-permute-start.6) | collective-permute-done | bytes 32800 | tf_op jit(solution)/shard_map/ppermute | solution.py:202
  49.9 3.7 %collective-permute-start.8 = (bf16[64,128]{1,0:T(8,128)(2,1)S(1)}, bf16[64,128]{1,0:T(8,128)(2,1)S(1)}, u32[]{:S(2)}, u32[]{:S(2)}) collective-permute-start(bf16[64,128]{1,0:T(8,128)(2,1)S(1)} %maximum_maximum_fusion.1.q0), channel_id=1, source_target_pairs={{0,8},{1,9},{2,10},{3,11},{4,12},{5,13},{6,14},{7,15},{8,0},{9,1},... | collective-permute-start | bytes 49160 | tf_op jit(solution)/shard_map/ppermute | solution.py:181
  54.0 0.8 %collective-permute-done.9.q3 = bf16[64,128]{1,0:T(8,128)(2,1)S(1)} collective-permute-done((bf16[64,128]{1,0:T(8,128)(2,1)S(1)}, bf16[64,128]{1,0:T(8,128)(2,1)S(1)}, u32[]{:S(2)}, u32[]{:S(2)}) %collective-permute-start.9) | collective-permute-done | bytes 16416 | tf_op jit(solution)/shard_map/ppermute | solution.py:181
  55.5 1.9 %collective-permute-done.7.q1 = bf16[64,128]{1,0:T(8,128)(2,1)S(1)} collective-permute-done((bf16[64,128]{1,0:T(8,128)(2,1)S(1)}, bf16[64,128]{1,0:T(8,128)(2,1)S(1)}, u32[]{:S(2)}, u32[]{:S(2)}) %collective-permute-start.7) | collective-permute-done | bytes 16416 | tf_op jit(solution)/shard_map/ppermute | solution.py:181
  57.3 8.5 %euler_basis.3 = (f32[64,128]{1,0:T(8,128)S(1)}, f32[64,128]{1,0:T(8,128)S(1)}, f32[64,128]{1,0:T(8,128)S(1)}, f32[64,128]{1,0:T(8,128)S(1)}) custom-call(s32[2]{0:T(128)S(1)} %pad_add_fusion.where_ref, s32[16,16]{1,0:T(8,128)S(1)} %copy-done.2, bf16[16,128,256]{2,1,0:T(8,128)(2,1)S(1)} %all-to-all-done.tab_a, ...), custom_call_target="tpu_custom_call" | custom-call | tf_op jit(solution)/shard_map/euler_basis/pallas_call | solution.py:156
  66.3 2.7 %collective-permute-start.11 = (f32[64,128]{1,0:T(8,128)S(1)}, f32[64,128]{1,0:T(8,128)S(1)}, u32[]{:S(2)}, u32[]{:S(2)}) collective-permute-start(f32[64,128]{1,0:T(8,128)S(1)} %get-tuple-element.28), channel_id=1, source_target_pairs={{0,8},{1,9},{2,10},{3,11},{4,12},{5,13},{6,14},{7,15},{8,0},{9,1},... | collective-permute-start | bytes 98312 | tf_op jit(solution)/shard_map/ppermute | solution.py:202
  69.1 1.0 %collective-permute-start.12 = (f32[64,128]{1,0:T(8,128)S(1)}, f32[64,128]{1,0:T(8,128)S(1)}, u32[]{:S(2)}, u32[]{:S(2)}) collective-permute-start(f32[64,128]{1,0:T(8,128)S(1)} %get-tuple-element.29), channel_id=1, source_target_pairs={{0,12},{1,13},{2,14},{3,15},{4,0},{5,1},{6,2},{7,3},{8,4},{9,5},{1... | collective-permute-start | bytes 98312 | tf_op jit(solution)/shard_map/ppermute | solution.py:202
  70.1 1.0 %collective-permute-done.10.g1 = f32[64,128]{1,0:T(8,128)S(1)} collective-permute-done((f32[64,128]{1,0:T(8,128)S(1)}, f32[64,128]{1,0:T(8,128)S(1)}, u32[]{:S(2)}, u32[]{:S(2)}) %collective-permute-start.10) | collective-permute-done | bytes 32800 | tf_op jit(solution)/shard_map/ppermute | solution.py:202
  71.8 1.2 %collective-permute-done.12.g3 = f32[64,128]{1,0:T(8,128)S(1)} collective-permute-done((f32[64,128]{1,0:T(8,128)S(1)}, f32[64,128]{1,0:T(8,128)S(1)}, u32[]{:S(2)}, u32[]{:S(2)}) %collective-permute-start.12) | collective-permute-done | bytes 32800 | tf_op jit(solution)/shard_map/ppermute | solution.py:202
  73.0 1.3 %finish.1 = (f32[59,1,128]{2,1,0:T(1,128)}, f32[59,1,128]{2,1,0:T(1,128)}) custom-call(s32[1]{0:T(128)} %bitcast.rowsum_ref, f32[59,128]{1,0:T(8,128)S(1)} %get-tuple-element.33.now_ref, f32[59,1,128]{2,1,0:T(1,128)S(1)} %bitcast.23, f32[64,128]{1,0:T(8,128)S(1)} %get-tuple-element.26.g0, f32[64,128]{1,0:T(8,128)S(1)} %collective-permute-done.10.g1, ...), custom_call_target="tpu_custom_call" | custom-call | tf_op jit(solution)/shard_map/finish/pallas_call | solution.py:70
  (31 shorter events, 4.2 us)
Async XLA Ops:
  0.6 0.7 copy-start.5
  1.3 0.7 copy-start.4
  1.3 0.7 copy-start.3
  2.0 0.8 %copy-start.1 = (bf16[1,118,256]{2,1,0:T(8,128)(2,1)S(1)}, bf16[1,118,256]{2,1,0:T(8,128)(2,1)}, u32[]{:S(2)}) copy-start(bf16[1,118,256]{2,1,0:T(8,128)(2,1)} %param.10) | copy-start | bytes 181252
  3.9 7.4 %copy-start.6 = (f32[1,59,128]{2,0,1:T(1,128)S(1)}, f32[1,59,128]{2,0,1:T(1,128)}, u32[]{:S(2)}) copy-start(f32[1,59,128]{2,0,1:T(1,128)} %param.8) | copy-start | bytes 90628
  3.9 25.0 %all-to-all-start = ((bf16[16,128,256]{2,1,0:T(8,128)(2,1)}), bf16[16,128,256]{2,1,0:T(8,128)(2,1)S(1)}, u32[]{:S(2)}, u32[]{:S(2)}) async-start(bf16[16,128,256]{2,1,0:T(8,128)(2,1)} %pack_tables.1), calls=%async_computation | async-start | bytes 2097152 | tf_op jit(solution)/shard_map/all_to_all | solution.py:189
  11.5 6.6 %collective-permute-start.2 = (bf16[64,128]{1,0:T(8,128)(2,1)S(1)}, bf16[64,128]{1,0:T(8,128)(2,1)S(1)}, u32[]{:S(2)}, u32[]{:S(2)}) collective-permute-start(bf16[64,128]{1,0:T(8,128)(2,1)S(1)} %maximum_maximum_fusion.q0), channel_id=1, source_target_pairs={{0,4},{1,5},{2,6},{3,7},{4,8},{5,9},{6,10},{7,11},{8,12},{9,13},{1... | collective-permute-start | bytes 49160 | tf_op jit(solution)/shard_map/ppermute | solution.py:181
  13.5 5.5 %collective-permute-start.1 = (bf16[64,128]{1,0:T(8,128)(2,1)S(1)}, bf16[64,128]{1,0:T(8,128)(2,1)S(1)}, u32[]{:S(2)}, u32[]{:S(2)}) collective-permute-start(bf16[64,128]{1,0:T(8,128)(2,1)S(1)} %maximum_maximum_fusion.q0), channel_id=1, source_target_pairs={{0,8},{1,9},{2,10},{3,11},{4,12},{5,13},{6,14},{7,15},{8,0},{9,1},... | collective-permute-start | bytes 49160 | tf_op jit(solution)/shard_map/ppermute | solution.py:181
  17.1 3.7 %collective-permute-start = (bf16[64,128]{1,0:T(8,128)(2,1)S(1)}, bf16[64,128]{1,0:T(8,128)(2,1)S(1)}, u32[]{:S(2)}, u32[]{:S(2)}) collective-permute-start(bf16[64,128]{1,0:T(8,128)(2,1)S(1)} %maximum_maximum_fusion.q0), channel_id=1, source_target_pairs={{0,12},{1,13},{2,14},{3,15},{4,0},{5,1},{6,2},{7,3},{8,4},{9,5},{1... | collective-permute-start | bytes 49160 | tf_op jit(solution)/shard_map/ppermute | solution.py:181
  29.0 2.7 %collective-permute-start.3 = (bf16[16,128,256]{2,1,0:T(8,128)(2,1)S(1)}, bf16[16,128,256]{2,1,0:T(8,128)(2,1)S(1)}, u32[]{:S(2)}, u32[]{:S(2)}) collective-permute-start(bf16[16,128,256]{2,1,0:T(8,128)(2,1)S(1)} %all-to-all-done.tab_a), channel_id=1, source_target_pairs={{0,16},{16,0},{32,48},{48,32},{64,80},{80,64},{96,112},{112,96},{1... | collective-permute-start | bytes 3145736 | tf_op jit(solution)/shard_map/ppermute | solution.py:194
  29.0 2.7 %copy-start.2 = (s32[16,16]{1,0:T(8,128)S(1)}, s32[16,16]{1,0:T(8,128)}, u32[]{:S(2)}) copy-start(s32[16,16]{1,0:T(8,128)} %counts_ref.3) | copy-start | bytes 3076
  31.6 18.0 %copy-start = (f32[1,59,128]{2,0,1:T(1,128)S(1)}, f32[1,59,128]{2,0,1:T(1,128)}, u32[]{:S(2)}) copy-start(f32[1,59,128]{2,0,1:T(1,128)} %param.9) | copy-start | bytes 90628
  40.2 7.9 %collective-permute-start.4 = (f32[64,128]{1,0:T(8,128)S(1)}, f32[64,128]{1,0:T(8,128)S(1)}, u32[]{:S(2)}, u32[]{:S(2)}) collective-permute-start(f32[64,128]{1,0:T(8,128)S(1)} %get-tuple-element.23), channel_id=1, source_target_pairs={{0,4},{1,5},{2,6},{3,7},{4,8},{5,9},{6,10},{7,11},{8,12},{9,13},{1... | collective-permute-start | bytes 98312 | tf_op jit(solution)/shard_map/ppermute | solution.py:202
  42.2 5.9 %collective-permute-start.5 = (f32[64,128]{1,0:T(8,128)S(1)}, f32[64,128]{1,0:T(8,128)S(1)}, u32[]{:S(2)}, u32[]{:S(2)}) collective-permute-start(f32[64,128]{1,0:T(8,128)S(1)} %get-tuple-element.24), channel_id=1, source_target_pairs={{0,8},{1,9},{2,10},{3,11},{4,12},{5,13},{6,14},{7,15},{8,0},{9,1},... | collective-permute-start | bytes 98312 | tf_op jit(solution)/shard_map/ppermute | solution.py:202
  45.8 3.9 %collective-permute-start.6 = (f32[64,128]{1,0:T(8,128)S(1)}, f32[64,128]{1,0:T(8,128)S(1)}, u32[]{:S(2)}, u32[]{:S(2)}) collective-permute-start(f32[64,128]{1,0:T(8,128)S(1)} %get-tuple-element.25), channel_id=1, source_target_pairs={{0,12},{1,13},{2,14},{3,15},{4,0},{5,1},{6,2},{7,3},{8,4},{9,5},{1... | collective-permute-start | bytes 98312 | tf_op jit(solution)/shard_map/ppermute | solution.py:202
  49.8 5.0 %collective-permute-start.9 = (bf16[64,128]{1,0:T(8,128)(2,1)S(1)}, bf16[64,128]{1,0:T(8,128)(2,1)S(1)}, u32[]{:S(2)}, u32[]{:S(2)}) collective-permute-start(bf16[64,128]{1,0:T(8,128)(2,1)S(1)} %maximum_maximum_fusion.1.q0), channel_id=1, source_target_pairs={{0,4},{1,5},{2,6},{3,7},{4,8},{5,9},{6,10},{7,11},{8,12},{9,13},{1... | collective-permute-start | bytes 49160 | tf_op jit(solution)/shard_map/ppermute | solution.py:181
  49.9 5.6 %collective-permute-start.8 = (bf16[64,128]{1,0:T(8,128)(2,1)S(1)}, bf16[64,128]{1,0:T(8,128)(2,1)S(1)}, u32[]{:S(2)}, u32[]{:S(2)}) collective-permute-start(bf16[64,128]{1,0:T(8,128)(2,1)S(1)} %maximum_maximum_fusion.1.q0), channel_id=1, source_target_pairs={{0,8},{1,9},{2,10},{3,11},{4,12},{5,13},{6,14},{7,15},{8,0},{9,1},... | collective-permute-start | bytes 49160 | tf_op jit(solution)/shard_map/ppermute | solution.py:181
  53.6 3.7 %collective-permute-start.7 = (bf16[64,128]{1,0:T(8,128)(2,1)S(1)}, bf16[64,128]{1,0:T(8,128)(2,1)S(1)}, u32[]{:S(2)}, u32[]{:S(2)}) collective-permute-start(bf16[64,128]{1,0:T(8,128)(2,1)S(1)} %maximum_maximum_fusion.1.q0), channel_id=1, source_target_pairs={{0,12},{1,13},{2,14},{3,15},{4,0},{5,1},{6,2},{7,3},{8,4},{9,5},{1... | collective-permute-start | bytes 49160 | tf_op jit(solution)/shard_map/ppermute | solution.py:181
  65.9 5.2 %collective-permute-start.10 = (f32[64,128]{1,0:T(8,128)S(1)}, f32[64,128]{1,0:T(8,128)S(1)}, u32[]{:S(2)}, u32[]{:S(2)}) collective-permute-start(f32[64,128]{1,0:T(8,128)S(1)} %get-tuple-element.27), channel_id=1, source_target_pairs={{0,4},{1,5},{2,6},{3,7},{4,8},{5,9},{6,10},{7,11},{8,12},{9,13},{1... | collective-permute-start | bytes 98312 | tf_op jit(solution)/shard_map/ppermute | solution.py:202
  66.3 5.4 %collective-permute-start.11 = (f32[64,128]{1,0:T(8,128)S(1)}, f32[64,128]{1,0:T(8,128)S(1)}, u32[]{:S(2)}, u32[]{:S(2)}) collective-permute-start(f32[64,128]{1,0:T(8,128)S(1)} %get-tuple-element.28), channel_id=1, source_target_pairs={{0,8},{1,9},{2,10},{3,11},{4,12},{5,13},{6,14},{7,15},{8,0},{9,1},... | collective-permute-start | bytes 98312 | tf_op jit(solution)/shard_map/ppermute | solution.py:202
  69.1 3.9 %collective-permute-start.12 = (f32[64,128]{1,0:T(8,128)S(1)}, f32[64,128]{1,0:T(8,128)S(1)}, u32[]{:S(2)}, u32[]{:S(2)}) collective-permute-start(f32[64,128]{1,0:T(8,128)S(1)} %get-tuple-element.29), channel_id=1, source_target_pairs={{0,12},{1,13},{2,14},{3,15},{4,0},{5,1},{6,2},{7,3},{8,4},{9,5},{1... | collective-permute-start | bytes 98312 | tf_op jit(solution)/shard_map/ppermute | solution.py:202

commit v5 on v4

--- a/solution.py
+++ b/solution.py
@@ -13,42 +13,43 @@
 HALF = 64
 RING = 4
 UNIT = 2
+ROWS = 72
 BF = jnp.bfloat16
 F32 = jnp.float32
 F8 = jnp.float8_e4m3fn
 SPLIT = 32.0
 
 
-def pack_kernel(live_ref, surplus_ref, dims_ref, levels_ref, index_ref, o_ref):
+def pack_kernel(live_ref, surplus_ref, dims_ref, levels_ref, index_ref, o_ref, wide_ref):
     npoints = surplus_ref.shape[1]
     position = lax.broadcasted_iota(jnp.int32, (1, npoints), 1)
-    kept = position < live_ref[0, 0]
-    body = jnp.where(kept, surplus_ref[0:112, :].astype(F32), 0.0).astype(BF)
-    row = lax.broadcasted_iota(jnp.int32, (16, npoints), 0)
-    tail = jnp.where(kept, surplus_ref[112:118, :].astype(F32), 0.0)
-    tail = jnp.concatenate([tail, jnp.zeros((10, npoints), F32)], axis=0)
+    kept = position < live_ref[...]
+    wide_ref[0 : 2 * DIM, :] = surplus_ref[...].astype(F32)
+    exponent = wide_ref[DIM : 2 * DIM, :] - GAMMA * wide_ref[0:DIM, :]
+    wide_ref[0:DIM, :] = jnp.where(kept, exponent, 0.0)
+    row = lax.broadcasted_iota(jnp.int32, (16, npoints), 0) + (ROWS - 16)
+    tail = jnp.where(row < DIM, wide_ref[ROWS - 16 : ROWS, :], 0.0)
     for k in range(3):
         level = levels_ref[k]
         refined = level > 0
         scale = jnp.where(refined, jnp.left_shift(jnp.ones_like(level), level), 0).astype(F32)
         bias = jnp.where(refined, 1 - index_ref[k], 1).astype(F32)
-        for place, value in ((6 + k, dims_ref[k].astype(F32)), (9 + k, scale), (12 + k, bias)):
+        for place, value in ((DIM + k, dims_ref[k].astype(F32)), (DIM + 3 + k, scale), (DIM + 6 + k, bias)):
             tail = jnp.where(row == place, value, tail)
-    tail = tail.astype(BF)
+    wide_ref[ROWS - 16 : ROWS, :] = tail
+    block = wide_ref[0:ROWS, :].astype(BF)
     for g in range(o_ref.shape[0]):
-        o_ref[g, 0:112, :] = body
-        o_ref[g, 112:128, :] = tail
+        o_ref[g] = block
 
 
 def pack(surplus, dims, levels, index, live):
     vm = pl.BlockSpec(memory_space=pltpu.VMEM)
-    sm = pl.BlockSpec(memory_space=pltpu.SMEM)
     return pl.pallas_call(
         pack_kernel,
-        out_shape=jax.ShapeDtypeStruct((16, 128, surplus.shape[1]), BF),
-        in_specs=[sm, vm, vm, vm, vm],
+        out_shape=jax.ShapeDtypeStruct((16, ROWS, surplus.shape[1]), BF),
+        in_specs=[vm] * 5,
         out_specs=vm,
-        compiler_params=pltpu.CompilerParams(vmem_limit_bytes=8 << 20),
+        scratch_shapes=[pltpu.VMEM((120, surplus.shape[1]), F32)],
         name="pack_tables",
     )(live, surplus, *(jnp.transpose(v, (1, 0, 2)) for v in (dims, levels, index)))
 
@@ -96,11 +97,11 @@
 
     def select(u, sel_ref):
         for b in range(UNIT):
-            par = block(jnp.minimum(u, units - 1), b)[112:128].astype(F32)
+            par = block(jnp.minimum(u, units - 1), b)[ROWS - 16 : ROWS].astype(F32)
             for k in range(3):
-                dim = par[6 + k : 7 + k].astype(jnp.int32)
-                scale = par[9 + k : 10 + k] * (1.0 / SPLIT)
-                bias = par[12 + k : 13 + k]
+                dim = par[3 + k : 4 + k].astype(jnp.int32)
+                scale = par[6 + k : 7 + k] * (1.0 / SPLIT)
+                bias = par[9 + k : 10 + k]
                 table = jnp.where(coord == dim, scale, jnp.where(row == DIM, bias, 0.0))
                 sel_ref[b, k] = table.astype(F8)
 
@@ -145,7 +146,7 @@
         for t in range(RING):
             value = acc_ref[t, pl.ds(j * 128, 128), :]
             count = counts_ref[s, z * RING + t].astype(F32)
-            term = count * jnp.exp(-GAMMA * value + pltpu.roll(value, 128 - DIM, 1))
+            term = count * jnp.exp(value)
             total = term if total is None else total + term
         o[...] = total.T[:HALF]
 
@@ -164,7 +165,7 @@
             pltpu.VMEM((UNIT, 3, 2 * HALF, 256), F8),
             pltpu.VMEM((512, UNIT * 256), BF),
             pltpu.VMEM((512, UNIT * 256), BF),
-            pltpu.VMEM((RING, 512, 128), F32),
+            pltpu.VMEM((RING, 512, ROWS), F32),
         ],
         compiler_params=pltpu.CompilerParams(vmem_limit_bytes=40 << 20),
         name="euler_basis",

time: 74.7 us -> 67.5 us (0.904)
  waiting for transfers between devices: 21.2 us -> 14.9 us
  local copies, waits for them, and re-layouts: 1.68 us -> 0.17 us
    all_to_all x1, waiting for transfers between devices: 8.19 us -> 2.63 us  [per_device(): lax.all_to_all(blocks, ('pts', 'shk'), 0, 0, tiled=True, axis_index_group...]
    unnamed x15 -> x7, local copies, waits for them, and re-layouts: 1.52 us -> 0.01 us
  transfers between devices with their start and end apart: 14 -> 14, of which waited for: 11 -> 11; matrix products, arithmetic and copies ran while one was open for 1% -> 2% of each run, Pallas kernels for 0% -> 0%
where the time goes in v5:
time: 67.5 us; the launch traced here: 67.2 us
  starting transfers between devices  28.8 us (43%)
  Pallas kernels  20.2 us (30%)
  waiting for transfers between devices  14.9 us (22%)
  between operations  2.04 us (3%)
  other arithmetic  0.99 us (1%)
    pallas_call x2, Pallas kernels, partial_sums(): pl.pallas_call(kernel, out_shape=[jax.ShapeDtypeStruct((HALF, 128), F32)]...  17.1 us
    ppermute x6, starting transfers between devices, per_device(): lax.ppermute(parts[j], 'shk', shift(j))  10.8 us
    ppermute x6, starting transfers between devices, spread(): return [own] + [lax.ppermute(own, 'shk', shift(-j)) for j in range(1, RING)]  10.8 us
    all_to_all x1, starting transfers between devices, per_device(): lax.all_to_all(blocks, ('pts', 'shk'), 0, 0, tiled=True, axis_index_group...  7.28 us
    ppermute x6, waiting for transfers between devices, spread(): return [own] + [lax.ppermute(own, 'shk', shift(-j)) for j in range(1, RING)]  6.01 us
    ppermute x6, waiting for transfers between devices, per_device(): lax.ppermute(parts[j], 'shk', shift(j))  4.38 us
    all_to_all x1, waiting for transfers between devices, per_device(): lax.all_to_all(blocks, ('pts', 'shk'), 0, 0, tiled=True, axis_index_group...  2.63 us
    ppermute x1, waiting for transfers between devices, per_device(): tables = (mine, lax.ppermute(mine, 'pts', [(i, i ^ 1) for i in range(8)]))  1.92 us
  transfers between devices with their start and end apart: 14, of which 11 were waited for; matrix products, arithmetic and copies ran while one was open for 2% of the time, Pallas kernels for 0%

profile of v5, /device:TPU:0, one launch (start us, length us, event | category | flops | bytes accessed | tf_op | source)
XLA Modules:
  0.0 67.2 jit_solution(11439810981033370925)
XLA Ops:
  1.3 1.8 %pack_tables.1 = bf16[16,72,256]{2,1,0:T(8,128)(2,1)} custom-call(s32[1,1]{1,0:T(1,128)S(6)} %copy.20.live_ref, bf16[118,256]{1,0:T(8,128)(2,1)} %bitcast.25, s32[3,1,256]{2,1,0:T(1,128)} %bitcast.26, s32[3,1,256]{2,1,0:T(1,128)} %bitcast.27, s32[3,1,256]{2,1,0:T(1,128)} %bitcast.28), custom_call_target="tpu_custom_call" | custom-call | tf_op jit(solution)/shard_map/pack_tables/pallas_call | solution.py:47
  3.1 7.3 %all-to-all-start = ((bf16[16,72,256]{2,1,0:T(8,128)(2,1)}), bf16[16,72,256]{2,1,0:T(8,128)(2,1)S(1)}, u32[]{:S(2)}, u32[]{:S(2)}) async-start(bf16[16,72,256]{2,1,0:T(8,128)(2,1)} %pack_tables.1), calls=%async_computation | async-start | bytes 1179648 | tf_op jit(solution)/shard_map/all_to_all | solution.py:190
  10.6 2.0 %collective-permute-start.2 = (bf16[64,128]{1,0:T(8,128)(2,1)S(1)}, bf16[64,128]{1,0:T(8,128)(2,1)S(1)}, u32[]{:S(2)}, u32[]{:S(2)}) collective-permute-start(bf16[64,128]{1,0:T(8,128)(2,1)S(1)} %maximum_maximum_fusion.q0), channel_id=1, source_target_pairs={{0,4},{1,5},{2,6},{3,7},{4,8},{5,9},{6,10},{7,11},{8,12},{9,13},{1... | collective-permute-start | bytes 49160 | tf_op jit(solution)/shard_map/ppermute | solution.py:182
  12.6 3.6 %collective-permute-start.1 = (bf16[64,128]{1,0:T(8,128)(2,1)S(1)}, bf16[64,128]{1,0:T(8,128)(2,1)S(1)}, u32[]{:S(2)}, u32[]{:S(2)}) collective-permute-start(bf16[64,128]{1,0:T(8,128)(2,1)S(1)} %maximum_maximum_fusion.q0), channel_id=1, source_target_pairs={{0,8},{1,9},{2,10},{3,11},{4,12},{5,13},{6,14},{7,15},{8,0},{9,1},... | collective-permute-start | bytes 49160 | tf_op jit(solution)/shard_map/ppermute | solution.py:182
  16.2 1.0 %collective-permute-start = (bf16[64,128]{1,0:T(8,128)(2,1)S(1)}, bf16[64,128]{1,0:T(8,128)(2,1)S(1)}, u32[]{:S(2)}, u32[]{:S(2)}) collective-permute-start(bf16[64,128]{1,0:T(8,128)(2,1)S(1)} %maximum_maximum_fusion.q0), channel_id=1, source_target_pairs={{0,12},{1,13},{2,14},{3,15},{4,0},{5,1},{6,2},{7,3},{8,4},{9,5},{1... | collective-permute-start | bytes 49160 | tf_op jit(solution)/shard_map/ppermute | solution.py:182
  17.2 0.9 %collective-permute-done.1.q2 = bf16[64,128]{1,0:T(8,128)(2,1)S(1)} collective-permute-done((bf16[64,128]{1,0:T(8,128)(2,1)S(1)}, bf16[64,128]{1,0:T(8,128)(2,1)S(1)}, u32[]{:S(2)}, u32[]{:S(2)}) %collective-permute-start.1) | collective-permute-done | bytes 16416 | tf_op jit(solution)/shard_map/ppermute | solution.py:182
  18.1 1.9 %collective-permute-done.q1 = bf16[64,128]{1,0:T(8,128)(2,1)S(1)} collective-permute-done((bf16[64,128]{1,0:T(8,128)(2,1)S(1)}, bf16[64,128]{1,0:T(8,128)(2,1)S(1)}, u32[]{:S(2)}, u32[]{:S(2)}) %collective-permute-start) | collective-permute-done | bytes 16416 | tf_op jit(solution)/shard_map/ppermute | solution.py:182
  19.9 2.6 %all-to-all-done.tab_a = bf16[16,72,256]{2,1,0:T(8,128)(2,1)S(1)} async-done(((bf16[16,72,256]{2,1,0:T(8,128)(2,1)}), bf16[16,72,256]{2,1,0:T(8,128)(2,1)S(1)}, u32[]{:S(2)}, u32[]{:S(2)}) %all-to-all-start) | async-done | bytes 589856 | tf_op jit(solution)/shard_map/all_to_all | solution.py:190
  22.6 1.9 %collective-permute-done.3.tab_b = bf16[16,72,256]{2,1,0:T(8,128)(2,1)S(1)} collective-permute-done((bf16[16,72,256]{2,1,0:T(8,128)(2,1)S(1)}, bf16[16,72,256]{2,1,0:T(8,128)(2,1)S(1)}, u32[]{:S(2)}, u32[]{:S(2)}) %collective-permute-start.3) | collective-permute-done | bytes 589856 | tf_op jit(solution)/shard_map/ppermute | solution.py:195
  24.6 8.5 %euler_basis.2 = (f32[64,128]{1,0:T(8,128)S(1)}, f32[64,128]{1,0:T(8,128)S(1)}, f32[64,128]{1,0:T(8,128)S(1)}, f32[64,128]{1,0:T(8,128)S(1)}) custom-call(s32[2]{0:T(128)S(1)} %pad_add_fusion.where_ref, s32[16,16]{1,0:T(8,128)S(1)} %copy-done.1, bf16[16,72,256]{2,1,0:T(8,128)(2,1)S(1)} %all-to-all-done.tab_a, ...), custom_call_target="tpu_custom_call" | custom-call | tf_op jit(solution)/shard_map/euler_basis/pallas_call | solution.py:157
  33.1 2.0 %collective-permute-start.4 = (f32[64,128]{1,0:T(8,128)S(1)}, f32[64,128]{1,0:T(8,128)S(1)}, u32[]{:S(2)}, u32[]{:S(2)}) collective-permute-start(f32[64,128]{1,0:T(8,128)S(1)} %get-tuple-element.23), channel_id=1, source_target_pairs={{0,4},{1,5},{2,6},{3,7},{4,8},{5,9},{6,10},{7,11},{8,12},{9,13},{1... | collective-permute-start | bytes 98312 | tf_op jit(solution)/shard_map/ppermute | solution.py:203
  35.1 3.6 %collective-permute-start.5 = (f32[64,128]{1,0:T(8,128)S(1)}, f32[64,128]{1,0:T(8,128)S(1)}, u32[]{:S(2)}, u32[]{:S(2)}) collective-permute-start(f32[64,128]{1,0:T(8,128)S(1)} %get-tuple-element.24), channel_id=1, source_target_pairs={{0,8},{1,9},{2,10},{3,11},{4,12},{5,13},{6,14},{7,15},{8,0},{9,1},... | collective-permute-start | bytes 98312 | tf_op jit(solution)/shard_map/ppermute | solution.py:203
  38.6 1.0 %collective-permute-start.6 = (f32[64,128]{1,0:T(8,128)S(1)}, f32[64,128]{1,0:T(8,128)S(1)}, u32[]{:S(2)}, u32[]{:S(2)}) collective-permute-start(f32[64,128]{1,0:T(8,128)S(1)} %get-tuple-element.25), channel_id=1, source_target_pairs={{0,12},{1,13},{2,14},{3,15},{4,0},{5,1},{6,2},{7,3},{8,4},{9,5},{1... | collective-permute-start | bytes 98312 | tf_op jit(solution)/shard_map/ppermute | solution.py:203
  39.7 0.7 %dynamic-slice_reduce_fusion = s32[]{:T(128)} fusion(s32[16,16]{1,0:T(8,128)S(1)} %copy-done.1, s32[]{:T(128)S(6)} %select_n.15), kind=kLoop, calls=%fused_computation.14 | loop fusion | flops 15 | bytes 72 | tf_op jit(solution)/shard_map/reduce_sum | solution.py:198
  41.1 1.5 %collective-permute-done.6 = f32[64,128]{1,0:T(8,128)S(1)} collective-permute-done((f32[64,128]{1,0:T(8,128)S(1)}, f32[64,128]{1,0:T(8,128)S(1)}, u32[]{:S(2)}, u32[]{:S(2)}) %collective-permute-start.6) | collective-permute-done | bytes 32800 | tf_op jit(solution)/shard_map/ppermute | solution.py:203
  42.8 3.7 %collective-permute-start.8 = (bf16[64,128]{1,0:T(8,128)(2,1)S(1)}, bf16[64,128]{1,0:T(8,128)(2,1)S(1)}, u32[]{:S(2)}, u32[]{:S(2)}) collective-permute-start(bf16[64,128]{1,0:T(8,128)(2,1)S(1)} %maximum_maximum_fusion.1.q0), channel_id=1, source_target_pairs={{0,8},{1,9},{2,10},{3,11},{4,12},{5,13},{6,14},{7,15},{8,0},{9,1},... | collective-permute-start | bytes 49160 | tf_op jit(solution)/shard_map/ppermute | solution.py:182
  46.9 0.8 %collective-permute-done.9.q3 = bf16[64,128]{1,0:T(8,128)(2,1)S(1)} collective-permute-done((bf16[64,128]{1,0:T(8,128)(2,1)S(1)}, bf16[64,128]{1,0:T(8,128)(2,1)S(1)}, u32[]{:S(2)}, u32[]{:S(2)}) %collective-permute-start.9) | collective-permute-done | bytes 16416 | tf_op jit(solution)/shard_map/ppermute | solution.py:182
  48.3 1.9 %collective-permute-done.7.q1 = bf16[64,128]{1,0:T(8,128)(2,1)S(1)} collective-permute-done((bf16[64,128]{1,0:T(8,128)(2,1)S(1)}, bf16[64,128]{1,0:T(8,128)(2,1)S(1)}, u32[]{:S(2)}, u32[]{:S(2)}) %collective-permute-start.7) | collective-permute-done | bytes 16416 | tf_op jit(solution)/shard_map/ppermute | solution.py:182
  50.2 8.5 %euler_basis.3 = (f32[64,128]{1,0:T(8,128)S(1)}, f32[64,128]{1,0:T(8,128)S(1)}, f32[64,128]{1,0:T(8,128)S(1)}, f32[64,128]{1,0:T(8,128)S(1)}) custom-call(s32[2]{0:T(128)S(1)} %pad_add_fusion.where_ref, s32[16,16]{1,0:T(8,128)S(1)} %copy-done.1, bf16[16,72,256]{2,1,0:T(8,128)(2,1)S(1)} %all-to-all-done.tab_a, ...), custom_call_target="tpu_custom_call" | custom-call | tf_op jit(solution)/shard_map/euler_basis/pallas_call | solution.py:157
  59.2 2.7 %collective-permute-start.11 = (f32[64,128]{1,0:T(8,128)S(1)}, f32[64,128]{1,0:T(8,128)S(1)}, u32[]{:S(2)}, u32[]{:S(2)}) collective-permute-start(f32[64,128]{1,0:T(8,128)S(1)} %get-tuple-element.28), channel_id=1, source_target_pairs={{0,8},{1,9},{2,10},{3,11},{4,12},{5,13},{6,14},{7,15},{8,0},{9,1},... | collective-permute-start | bytes 98312 | tf_op jit(solution)/shard_map/ppermute | solution.py:203
  61.9 1.0 %collective-permute-start.12 = (f32[64,128]{1,0:T(8,128)S(1)}, f32[64,128]{1,0:T(8,128)S(1)}, u32[]{:S(2)}, u32[]{:S(2)}) collective-permute-start(f32[64,128]{1,0:T(8,128)S(1)} %get-tuple-element.29), channel_id=1, source_target_pairs={{0,12},{1,13},{2,14},{3,15},{4,0},{5,1},{6,2},{7,3},{8,4},{9,5},{1... | collective-permute-start | bytes 98312 | tf_op jit(solution)/shard_map/ppermute | solution.py:203
  62.9 1.0 %collective-permute-done.10.g1 = f32[64,128]{1,0:T(8,128)S(1)} collective-permute-done((f32[64,128]{1,0:T(8,128)S(1)}, f32[64,128]{1,0:T(8,128)S(1)}, u32[]{:S(2)}, u32[]{:S(2)}) %collective-permute-start.10) | collective-permute-done | bytes 32800 | tf_op jit(solution)/shard_map/ppermute | solution.py:203
  64.6 1.2 %collective-permute-done.12.g3 = f32[64,128]{1,0:T(8,128)S(1)} collective-permute-done((f32[64,128]{1,0:T(8,128)S(1)}, f32[64,128]{1,0:T(8,128)S(1)}, u32[]{:S(2)}, u32[]{:S(2)}) %collective-permute-start.12) | collective-permute-done | bytes 32800 | tf_op jit(solution)/shard_map/ppermute | solution.py:203
  65.8 1.4 %finish.1 = (f32[59,1,128]{2,1,0:T(1,128)}, f32[59,1,128]{2,1,0:T(1,128)}) custom-call(s32[1]{0:T(128)} %bitcast.rowsum_ref, f32[59,128]{1,0:T(8,128)S(1)} %get-tuple-element.33.now_ref, f32[59,1,128]{2,1,0:T(1,128)S(1)} %bitcast.23, f32[64,128]{1,0:T(8,128)S(1)} %get-tuple-element.26.g0, f32[64,128]{1,0:T(8,128)S(1)} %collective-permute-done.10.g1, ...), custom_call_target="tpu_custom_call" | custom-call | tf_op jit(solution)/shard_map/finish/pallas_call | solution.py:71
  (23 shorter events, 2.8 us)
Async XLA Ops:
  3.1 7.4 %copy-start.2 = (f32[1,59,128]{2,0,1:T(1,128)S(1)}, f32[1,59,128]{2,0,1:T(1,128)}, u32[]{:S(2)}) copy-start(f32[1,59,128]{2,0,1:T(1,128)} %param.8) | copy-start | bytes 90628
  3.1 19.5 %all-to-all-start = ((bf16[16,72,256]{2,1,0:T(8,128)(2,1)}), bf16[16,72,256]{2,1,0:T(8,128)(2,1)S(1)}, u32[]{:S(2)}, u32[]{:S(2)}) async-start(bf16[16,72,256]{2,1,0:T(8,128)(2,1)} %pack_tables.1), calls=%async_computation | async-start | bytes 1179648 | tf_op jit(solution)/shard_map/all_to_all | solution.py:190
  10.6 6.6 %collective-permute-start.2 = (bf16[64,128]{1,0:T(8,128)(2,1)S(1)}, bf16[64,128]{1,0:T(8,128)(2,1)S(1)}, u32[]{:S(2)}, u32[]{:S(2)}) collective-permute-start(bf16[64,128]{1,0:T(8,128)(2,1)S(1)} %maximum_maximum_fusion.q0), channel_id=1, source_target_pairs={{0,4},{1,5},{2,6},{3,7},{4,8},{5,9},{6,10},{7,11},{8,12},{9,13},{1... | collective-permute-start | bytes 49160 | tf_op jit(solution)/shard_map/ppermute | solution.py:182
  12.6 5.5 %collective-permute-start.1 = (bf16[64,128]{1,0:T(8,128)(2,1)S(1)}, bf16[64,128]{1,0:T(8,128)(2,1)S(1)}, u32[]{:S(2)}, u32[]{:S(2)}) collective-permute-start(bf16[64,128]{1,0:T(8,128)(2,1)S(1)} %maximum_maximum_fusion.q0), channel_id=1, source_target_pairs={{0,8},{1,9},{2,10},{3,11},{4,12},{5,13},{6,14},{7,15},{8,0},{9,1},... | collective-permute-start | bytes 49160 | tf_op jit(solution)/shard_map/ppermute | solution.py:182
  16.2 3.7 %collective-permute-start = (bf16[64,128]{1,0:T(8,128)(2,1)S(1)}, bf16[64,128]{1,0:T(8,128)(2,1)S(1)}, u32[]{:S(2)}, u32[]{:S(2)}) collective-permute-start(bf16[64,128]{1,0:T(8,128)(2,1)S(1)} %maximum_maximum_fusion.q0), channel_id=1, source_target_pairs={{0,12},{1,13},{2,14},{3,15},{4,0},{5,1},{6,2},{7,3},{8,4},{9,5},{1... | collective-permute-start | bytes 49160 | tf_op jit(solution)/shard_map/ppermute | solution.py:182
  22.5 2.0 %collective-permute-start.3 = (bf16[16,72,256]{2,1,0:T(8,128)(2,1)S(1)}, bf16[16,72,256]{2,1,0:T(8,128)(2,1)S(1)}, u32[]{:S(2)}, u32[]{:S(2)}) collective-permute-start(bf16[16,72,256]{2,1,0:T(8,128)(2,1)S(1)} %all-to-all-done.tab_a), channel_id=1, source_target_pairs={{0,16},{16,0},{32,48},{48,32},{64,80},{80,64},{96,112},{112,96},{1... | collective-permute-start | bytes 1769480 | tf_op jit(solution)/shard_map/ppermute | solution.py:195
  22.5 2.0 %copy-start.1 = (s32[16,16]{1,0:T(8,128)S(1)}, s32[16,16]{1,0:T(8,128)}, u32[]{:S(2)}) copy-start(s32[16,16]{1,0:T(8,128)} %counts_ref.3) | copy-start | bytes 3076
  24.6 18.0 %copy-start = (f32[1,59,128]{2,0,1:T(1,128)S(1)}, f32[1,59,128]{2,0,1:T(1,128)}, u32[]{:S(2)}) copy-start(f32[1,59,128]{2,0,1:T(1,128)} %param.9) | copy-start | bytes 90628
  33.1 8.0 %collective-permute-start.4 = (f32[64,128]{1,0:T(8,128)S(1)}, f32[64,128]{1,0:T(8,128)S(1)}, u32[]{:S(2)}, u32[]{:S(2)}) collective-permute-start(f32[64,128]{1,0:T(8,128)S(1)} %get-tuple-element.23), channel_id=1, source_target_pairs={{0,4},{1,5},{2,6},{3,7},{4,8},{5,9},{6,10},{7,11},{8,12},{9,13},{1... | collective-permute-start | bytes 98312 | tf_op jit(solution)/shard_map/ppermute | solution.py:203
  35.1 6.0 %collective-permute-start.5 = (f32[64,128]{1,0:T(8,128)S(1)}, f32[64,128]{1,0:T(8,128)S(1)}, u32[]{:S(2)}, u32[]{:S(2)}) collective-permute-start(f32[64,128]{1,0:T(8,128)S(1)} %get-tuple-element.24), channel_id=1, source_target_pairs={{0,8},{1,9},{2,10},{3,11},{4,12},{5,13},{6,14},{7,15},{8,0},{9,1},... | collective-permute-start | bytes 98312 | tf_op jit(solution)/shard_map/ppermute | solution.py:203
  38.6 3.9 %collective-permute-start.6 = (f32[64,128]{1,0:T(8,128)S(1)}, f32[64,128]{1,0:T(8,128)S(1)}, u32[]{:S(2)}, u32[]{:S(2)}) collective-permute-start(f32[64,128]{1,0:T(8,128)S(1)} %get-tuple-element.25), channel_id=1, source_target_pairs={{0,12},{1,13},{2,14},{3,15},{4,0},{5,1},{6,2},{7,3},{8,4},{9,5},{1... | collective-permute-start | bytes 98312 | tf_op jit(solution)/shard_map/ppermute | solution.py:203
  42.7 5.0 %collective-permute-start.9 = (bf16[64,128]{1,0:T(8,128)(2,1)S(1)}, bf16[64,128]{1,0:T(8,128)(2,1)S(1)}, u32[]{:S(2)}, u32[]{:S(2)}) collective-permute-start(bf16[64,128]{1,0:T(8,128)(2,1)S(1)} %maximum_maximum_fusion.1.q0), channel_id=1, source_target_pairs={{0,4},{1,5},{2,6},{3,7},{4,8},{5,9},{6,10},{7,11},{8,12},{9,13},{1... | collective-permute-start | bytes 49160 | tf_op jit(solution)/shard_map/ppermute | solution.py:182
  42.8 5.6 %collective-permute-start.8 = (bf16[64,128]{1,0:T(8,128)(2,1)S(1)}, bf16[64,128]{1,0:T(8,128)(2,1)S(1)}, u32[]{:S(2)}, u32[]{:S(2)}) collective-permute-start(bf16[64,128]{1,0:T(8,128)(2,1)S(1)} %maximum_maximum_fusion.1.q0), channel_id=1, source_target_pairs={{0,8},{1,9},{2,10},{3,11},{4,12},{5,13},{6,14},{7,15},{8,0},{9,1},... | collective-permute-start | bytes 49160 | tf_op jit(solution)/shard_map/ppermute | solution.py:182
  46.4 3.7 %collective-permute-start.7 = (bf16[64,128]{1,0:T(8,128)(2,1)S(1)}, bf16[64,128]{1,0:T(8,128)(2,1)S(1)}, u32[]{:S(2)}, u32[]{:S(2)}) collective-permute-start(bf16[64,128]{1,0:T(8,128)(2,1)S(1)} %maximum_maximum_fusion.1.q0), channel_id=1, source_target_pairs={{0,12},{1,13},{2,14},{3,15},{4,0},{5,1},{6,2},{7,3},{8,4},{9,5},{1... | collective-permute-start | bytes 49160 | tf_op jit(solution)/shard_map/ppermute | solution.py:182
  58.7 5.2 %collective-permute-start.10 = (f32[64,128]{1,0:T(8,128)S(1)}, f32[64,128]{1,0:T(8,128)S(1)}, u32[]{:S(2)}, u32[]{:S(2)}) collective-permute-start(f32[64,128]{1,0:T(8,128)S(1)} %get-tuple-element.27), channel_id=1, source_target_pairs={{0,4},{1,5},{2,6},{3,7},{4,8},{5,9},{6,10},{7,11},{8,12},{9,13},{1... | collective-permute-start | bytes 98312 | tf_op jit(solution)/shard_map/ppermute | solution.py:203
  59.2 5.4 %collective-permute-start.11 = (f32[64,128]{1,0:T(8,128)S(1)}, f32[64,128]{1,0:T(8,128)S(1)}, u32[]{:S(2)}, u32[]{:S(2)}) collective-permute-start(f32[64,128]{1,0:T(8,128)S(1)} %get-tuple-element.28), channel_id=1, source_target_pairs={{0,8},{1,9},{2,10},{3,11},{4,12},{5,13},{6,14},{7,15},{8,0},{9,1},... | collective-permute-start | bytes 98312 | tf_op jit(solution)/shard_map/ppermute | solution.py:203
  61.9 3.9 %collective-permute-start.12 = (f32[64,128]{1,0:T(8,128)S(1)}, f32[64,128]{1,0:T(8,128)S(1)}, u32[]{:S(2)}, u32[]{:S(2)}) collective-permute-start(f32[64,128]{1,0:T(8,128)S(1)} %get-tuple-element.29), channel_id=1, source_target_pairs={{0,12},{1,13},{2,14},{3,15},{4,0},{5,1},{6,2},{7,3},{8,4},{9,5},{1... | collective-permute-start | bytes 98312 | tf_op jit(solution)/shard_map/ppermute | solution.py:203

commit v6 on v5

--- a/solution.py
+++ b/solution.py
@@ -14,6 +14,7 @@
 RING = 4
 UNIT = 2
 ROWS = 72
+STEP = 0.375 / 32768
 BF = jnp.bfloat16
 F32 = jnp.float32
 F8 = jnp.float8_e4m3fn
@@ -26,7 +27,8 @@
     kept = position < live_ref[...]
     wide_ref[0 : 2 * DIM, :] = surplus_ref[...].astype(F32)
     exponent = wide_ref[DIM : 2 * DIM, :] - GAMMA * wide_ref[0:DIM, :]
-    wide_ref[0:DIM, :] = jnp.where(kept, exponent, 0.0)
+    steps = jnp.clip(jnp.floor(exponent * (1.0 / STEP) + 0.5), -32767.0, 32767.0)
+    wide_ref[0:DIM, :] = jnp.where(kept, steps, 0.0)
     row = lax.broadcasted_iota(jnp.int32, (16, npoints), 0) + (ROWS - 16)
     tail = jnp.where(row < DIM, wide_ref[ROWS - 16 : ROWS, :], 0.0)
     for k in range(3):
@@ -37,7 +39,7 @@
         for place, value in ((DIM + k, dims_ref[k].astype(F32)), (DIM + 3 + k, scale), (DIM + 6 + k, bias)):
             tail = jnp.where(row == place, value, tail)
     wide_ref[ROWS - 16 : ROWS, :] = tail
-    block = wide_ref[0:ROWS, :].astype(BF)
+    block = wide_ref[0:ROWS, :].astype(jnp.int32).astype(jnp.int16)
     for g in range(o_ref.shape[0]):
         o_ref[g] = block
 
@@ -46,7 +48,7 @@
     vm = pl.BlockSpec(memory_space=pltpu.VMEM)
     return pl.pallas_call(
         pack_kernel,
-        out_shape=jax.ShapeDtypeStruct((16, ROWS, surplus.shape[1]), BF),
+        out_shape=jax.ShapeDtypeStruct((16, ROWS, surplus.shape[1]), jnp.int16),
         in_specs=[vm] * 5,
         out_specs=vm,
         scratch_shapes=[pltpu.VMEM((120, surplus.shape[1]), F32)],
@@ -88,8 +90,7 @@
         whole = jnp.where(lax.broadcasted_iota(jnp.int32, whole.shape, 0) < DIM, whole * SPLIT, whole)
         high = whole.astype(F8).astype(F32)
         qt_ref[pl.ds(j * 128, 128), :] = jnp.concatenate([high, whole - high], axis=0).T.astype(F8)
-    row = lax.broadcasted_iota(jnp.int32, (2 * HALF, 256), 0)
-    coord = row % HALF
+    row = lax.broadcasted_iota(jnp.int32, (HALF, 256), 0)
     units = 8 * RING // UNIT
 
     def block(u, b):
@@ -97,25 +98,32 @@
 
     def select(u, sel_ref):
         for b in range(UNIT):
-            par = block(jnp.minimum(u, units - 1), b)[ROWS - 16 : ROWS].astype(F32)
+            par = block(jnp.minimum(u, units - 1), b)[ROWS - 16 : ROWS].astype(jnp.int32)
             for k in range(3):
-                dim = par[3 + k : 4 + k].astype(jnp.int32)
-                scale = par[6 + k : 7 + k] * (1.0 / SPLIT)
-                bias = par[9 + k : 10 + k]
-                table = jnp.where(coord == dim, scale, jnp.where(row == DIM, bias, 0.0))
-                sel_ref[b, k] = table.astype(F8)
+                dim = par[3 + k : 4 + k]
+                scale = par[6 + k : 7 + k].astype(F32) * (1.0 / SPLIT)
+                bias = par[9 + k : 10 + k].astype(F32)
+                table = jnp.where(row == dim, scale, jnp.where(row == DIM, bias, 0.0)).astype(F8)
+                sel_ref[b, k, 0:HALF, :] = table
+                sel_ref[b, k, HALF : 2 * HALF, :] = table
 
     def hats(sel_ref, basis_ref):
         for b in range(UNIT):
             basis = None
             for k in range(3):
-                left = jnp.dot(qt_ref[...], sel_ref[b, k], preferred_element_type=F32).astype(BF)
-                factor = jnp.maximum(jnp.minimum(left, BF(2.0) - left), BF(0.0))
+                left = jnp.dot(qt_ref[...], sel_ref[b, k], preferred_element_type=F32)
+                factor = jnp.minimum(left, 2.0 - left)
+                factor = jnp.maximum(factor, 0.0) if k < 2 else factor
                 basis = factor if basis is None else basis * factor
-            basis_ref[:, pl.ds(b * 256, 256)] = basis
+            basis_ref[:, pl.ds(b * 256, 256)] = jnp.maximum(basis.astype(BF), BF(0.0))
+
+    def halves(blk):
+        steps = blk[0:HALF].astype(jnp.int32)
+        high = jnp.right_shift(steps, 8)
+        return jnp.concatenate([high.astype(F32), (steps - high * 256).astype(F32)], axis=0).astype(BF)
 
     def sums(u, basis_ref):
-        weights = jnp.concatenate([block(u, b) for b in range(UNIT)], axis=1)
+        weights = jnp.concatenate([halves(block(u, b)) for b in range(UNIT)], axis=1)
         acc_ref[u // RING] += lax.dot_general(
             basis_ref[...], weights, (((1,), (1,)), ((), ())), preferred_element_type=F32
         )
@@ -146,7 +154,7 @@
         for t in range(RING):
             value = acc_ref[t, pl.ds(j * 128, 128), :]
             count = counts_ref[s, z * RING + t].astype(F32)
-            term = count * jnp.exp(value)
+            term = count * jnp.exp((256.0 * STEP) * value + STEP * pltpu.roll(value, HALF, 1))
             total = term if total is None else total + term
         o[...] = total.T[:HALF]
 
@@ -165,7 +173,7 @@
             pltpu.VMEM((UNIT, 3, 2 * HALF, 256), F8),
             pltpu.VMEM((512, UNIT * 256), BF),
             pltpu.VMEM((512, UNIT * 256), BF),
-            pltpu.VMEM((RING, 512, ROWS), F32),
+            pltpu.VMEM((RING, 512, 128), F32),
         ],
         compiler_params=pltpu.CompilerParams(vmem_limit_bytes=40 << 20),
         name="euler_basis",

time: 67.5 us -> 72 us (1.067)
  Pallas kernels: 20.2 us -> 24.6 us
    pallas_call x2, Pallas kernels: 17.1 us -> 21.4 us  [partial_sums(): pl.pallas_call(kernel, out_shape=[jax.ShapeDtypeStruct((HALF, 128), F32)]...]
  transfers between devices with their start and end apart: 14 -> 14, of which waited for: 11 -> 11; matrix products, arithmetic and copies ran while one was open for 2% -> 1% of each run, Pallas kernels for 0% -> 0%
where the time goes in v6:
time: 72 us; the launch traced here: 71.6 us
  starting transfers between devices  28.9 us (40%)
  Pallas kernels  24.6 us (34%)
  waiting for transfers between devices  14.9 us (21%)
  between operations  2.05 us (3%)
  other arithmetic  0.99 us (1%)
    pallas_call x2, Pallas kernels, partial_sums(): pl.pallas_call(kernel, out_shape=[jax.ShapeDtypeStruct((HALF, 128), F32)]...  21.4 us
    ppermute x6, starting transfers between devices, per_device(): lax.ppermute(parts[j], 'shk', shift(j))  10.8 us
    ppermute x6, starting transfers between devices, spread(): return [own] + [lax.ppermute(own, 'shk', shift(-j)) for j in range(1, RING)]  10.8 us
    all_to_all x1, starting transfers between devices, per_device(): lax.all_to_all(blocks, ('pts', 'shk'), 0, 0, tiled=True, axis_index_group...  7.28 us
    ppermute x6, waiting for transfers between devices, spread(): return [own] + [lax.ppermute(own, 'shk', shift(-j)) for j in range(1, RING)]  6.02 us
    ppermute x6, waiting for transfers between devices, per_device(): lax.ppermute(parts[j], 'shk', shift(j))  4.36 us
    all_to_all x1, waiting for transfers between devices, per_device(): lax.all_to_all(blocks, ('pts', 'shk'), 0, 0, tiled=True, axis_index_group...  2.63 us
    ppermute x1, waiting for transfers between devices, per_device(): tables = (mine, lax.ppermute(mine, 'pts', [(i, i ^ 1) for i in range(8)]))  1.92 us
  transfers between devices with their start and end apart: 14, of which 11 were waited for; matrix products, arithmetic and copies ran while one was open for 1% of the time, Pallas kernels for 0%

profile of v6, /device:TPU:0, one launch (start us, length us, event | category | flops | bytes accessed | tf_op | source)
XLA Modules:
  0.0 71.6 jit_solution(6908130587713024544)
XLA Ops:
  1.3 1.8 %pack_tables.1 = s16[16,72,256]{2,1,0:T(8,128)(2,1)} custom-call(s32[1,1]{1,0:T(1,128)S(6)} %copy.20.live_ref, bf16[118,256]{1,0:T(8,128)(2,1)} %bitcast.25, s32[3,1,256]{2,1,0:T(1,128)} %bitcast.26, s32[3,1,256]{2,1,0:T(1,128)} %bitcast.27, s32[3,1,256]{2,1,0:T(1,128)} %bitcast.28), custom_call_target="tpu_custom_call" | custom-call | tf_op jit(solution)/shard_map/pack_tables/pallas_call | solution.py:49
  3.1 7.3 %all-to-all-start = ((s16[16,72,256]{2,1,0:T(8,128)(2,1)}), s16[16,72,256]{2,1,0:T(8,128)(2,1)S(1)}, u32[]{:S(2)}, u32[]{:S(2)}) async-start(s16[16,72,256]{2,1,0:T(8,128)(2,1)} %pack_tables.1), calls=%async_computation | async-start | bytes 1179648 | tf_op jit(solution)/shard_map/all_to_all | solution.py:198
  10.6 2.0 %collective-permute-start.2 = (bf16[64,128]{1,0:T(8,128)(2,1)S(1)}, bf16[64,128]{1,0:T(8,128)(2,1)S(1)}, u32[]{:S(2)}, u32[]{:S(2)}) collective-permute-start(bf16[64,128]{1,0:T(8,128)(2,1)S(1)} %maximum_maximum_fusion.q0), channel_id=1, source_target_pairs={{0,4},{1,5},{2,6},{3,7},{4,8},{5,9},{6,10},{7,11},{8,12},{9,13},{1... | collective-permute-start | bytes 49160 | tf_op jit(solution)/shard_map/ppermute | solution.py:190
  12.6 3.6 %collective-permute-start.1 = (bf16[64,128]{1,0:T(8,128)(2,1)S(1)}, bf16[64,128]{1,0:T(8,128)(2,1)S(1)}, u32[]{:S(2)}, u32[]{:S(2)}) collective-permute-start(bf16[64,128]{1,0:T(8,128)(2,1)S(1)} %maximum_maximum_fusion.q0), channel_id=1, source_target_pairs={{0,8},{1,9},{2,10},{3,11},{4,12},{5,13},{6,14},{7,15},{8,0},{9,1},... | collective-permute-start | bytes 49160 | tf_op jit(solution)/shard_map/ppermute | solution.py:190
  16.2 1.0 %collective-permute-start = (bf16[64,128]{1,0:T(8,128)(2,1)S(1)}, bf16[64,128]{1,0:T(8,128)(2,1)S(1)}, u32[]{:S(2)}, u32[]{:S(2)}) collective-permute-start(bf16[64,128]{1,0:T(8,128)(2,1)S(1)} %maximum_maximum_fusion.q0), channel_id=1, source_target_pairs={{0,12},{1,13},{2,14},{3,15},{4,0},{5,1},{6,2},{7,3},{8,4},{9,5},{1... | collective-permute-start | bytes 49160 | tf_op jit(solution)/shard_map/ppermute | solution.py:190
  17.2 0.9 %collective-permute-done.1.q2 = bf16[64,128]{1,0:T(8,128)(2,1)S(1)} collective-permute-done((bf16[64,128]{1,0:T(8,128)(2,1)S(1)}, bf16[64,128]{1,0:T(8,128)(2,1)S(1)}, u32[]{:S(2)}, u32[]{:S(2)}) %collective-permute-start.1) | collective-permute-done | bytes 16416 | tf_op jit(solution)/shard_map/ppermute | solution.py:190
  18.1 1.9 %collective-permute-done.q1 = bf16[64,128]{1,0:T(8,128)(2,1)S(1)} collective-permute-done((bf16[64,128]{1,0:T(8,128)(2,1)S(1)}, bf16[64,128]{1,0:T(8,128)(2,1)S(1)}, u32[]{:S(2)}, u32[]{:S(2)}) %collective-permute-start) | collective-permute-done | bytes 16416 | tf_op jit(solution)/shard_map/ppermute | solution.py:190
  19.9 2.6 %all-to-all-done.tab_a = s16[16,72,256]{2,1,0:T(8,128)(2,1)S(1)} async-done(((s16[16,72,256]{2,1,0:T(8,128)(2,1)}), s16[16,72,256]{2,1,0:T(8,128)(2,1)S(1)}, u32[]{:S(2)}, u32[]{:S(2)}) %all-to-all-start) | async-done | bytes 589856 | tf_op jit(solution)/shard_map/all_to_all | solution.py:198
  22.6 1.9 %collective-permute-done.3.tab_b = s16[16,72,256]{2,1,0:T(8,128)(2,1)S(1)} collective-permute-done((s16[16,72,256]{2,1,0:T(8,128)(2,1)S(1)}, s16[16,72,256]{2,1,0:T(8,128)(2,1)S(1)}, u32[]{:S(2)}, u32[]{:S(2)}) %collective-permute-start.3) | collective-permute-done | bytes 589856 | tf_op jit(solution)/shard_map/ppermute | solution.py:203
  24.6 10.7 %euler_basis.2 = (f32[64,128]{1,0:T(8,128)S(1)}, f32[64,128]{1,0:T(8,128)S(1)}, f32[64,128]{1,0:T(8,128)S(1)}, f32[64,128]{1,0:T(8,128)S(1)}) custom-call(s32[2]{0:T(128)S(1)} %pad_add_fusion.where_ref, s32[16,16]{1,0:T(8,128)S(1)} %copy-done.1, s16[16,72,256]{2,1,0:T(8,128)(2,1)S(1)} %all-to-all-done.tab_a, ...), custom_call_target="tpu_custom_call" | custom-call | tf_op jit(solution)/shard_map/euler_basis/pallas_call | solution.py:165
  35.3 2.0 %collective-permute-start.4 = (f32[64,128]{1,0:T(8,128)S(1)}, f32[64,128]{1,0:T(8,128)S(1)}, u32[]{:S(2)}, u32[]{:S(2)}) collective-permute-start(f32[64,128]{1,0:T(8,128)S(1)} %get-tuple-element.23), channel_id=1, source_target_pairs={{0,4},{1,5},{2,6},{3,7},{4,8},{5,9},{6,10},{7,11},{8,12},{9,13},{1... | collective-permute-start | bytes 98312 | tf_op jit(solution)/shard_map/ppermute | solution.py:211
  37.3 3.6 %collective-permute-start.5 = (f32[64,128]{1,0:T(8,128)S(1)}, f32[64,128]{1,0:T(8,128)S(1)}, u32[]{:S(2)}, u32[]{:S(2)}) collective-permute-start(f32[64,128]{1,0:T(8,128)S(1)} %get-tuple-element.24), channel_id=1, source_target_pairs={{0,8},{1,9},{2,10},{3,11},{4,12},{5,13},{6,14},{7,15},{8,0},{9,1},... | collective-permute-start | bytes 98312 | tf_op jit(solution)/shard_map/ppermute | solution.py:211
  40.8 1.0 %collective-permute-start.6 = (f32[64,128]{1,0:T(8,128)S(1)}, f32[64,128]{1,0:T(8,128)S(1)}, u32[]{:S(2)}, u32[]{:S(2)}) collective-permute-start(f32[64,128]{1,0:T(8,128)S(1)} %get-tuple-element.25), channel_id=1, source_target_pairs={{0,12},{1,13},{2,14},{3,15},{4,0},{5,1},{6,2},{7,3},{8,4},{9,5},{1... | collective-permute-start | bytes 98312 | tf_op jit(solution)/shard_map/ppermute | solution.py:211
  41.9 0.7 dynamic-slice_reduce_fusion
  43.3 1.5 %collective-permute-done.6 = f32[64,128]{1,0:T(8,128)S(1)} collective-permute-done((f32[64,128]{1,0:T(8,128)S(1)}, f32[64,128]{1,0:T(8,128)S(1)}, u32[]{:S(2)}, u32[]{:S(2)}) %collective-permute-start.6) | collective-permute-done | bytes 32800 | tf_op jit(solution)/shard_map/ppermute | solution.py:211
  45.0 3.7 %collective-permute-start.8 = (bf16[64,128]{1,0:T(8,128)(2,1)S(1)}, bf16[64,128]{1,0:T(8,128)(2,1)S(1)}, u32[]{:S(2)}, u32[]{:S(2)}) collective-permute-start(bf16[64,128]{1,0:T(8,128)(2,1)S(1)} %maximum_maximum_fusion.1.q0), channel_id=1, source_target_pairs={{0,8},{1,9},{2,10},{3,11},{4,12},{5,13},{6,14},{7,15},{8,0},{9,1},... | collective-permute-start | bytes 49160 | tf_op jit(solution)/shard_map/ppermute | solution.py:190
  49.1 0.8 %collective-permute-done.9.q3 = bf16[64,128]{1,0:T(8,128)(2,1)S(1)} collective-permute-done((bf16[64,128]{1,0:T(8,128)(2,1)S(1)}, bf16[64,128]{1,0:T(8,128)(2,1)S(1)}, u32[]{:S(2)}, u32[]{:S(2)}) %collective-permute-start.9) | collective-permute-done | bytes 16416 | tf_op jit(solution)/shard_map/ppermute | solution.py:190
  50.5 1.9 %collective-permute-done.7.q1 = bf16[64,128]{1,0:T(8,128)(2,1)S(1)} collective-permute-done((bf16[64,128]{1,0:T(8,128)(2,1)S(1)}, bf16[64,128]{1,0:T(8,128)(2,1)S(1)}, u32[]{:S(2)}, u32[]{:S(2)}) %collective-permute-start.7) | collective-permute-done | bytes 16416 | tf_op jit(solution)/shard_map/ppermute | solution.py:190
  52.4 10.7 %euler_basis.3 = (f32[64,128]{1,0:T(8,128)S(1)}, f32[64,128]{1,0:T(8,128)S(1)}, f32[64,128]{1,0:T(8,128)S(1)}, f32[64,128]{1,0:T(8,128)S(1)}) custom-call(s32[2]{0:T(128)S(1)} %pad_add_fusion.where_ref, s32[16,16]{1,0:T(8,128)S(1)} %copy-done.1, s16[16,72,256]{2,1,0:T(8,128)(2,1)S(1)} %all-to-all-done.tab_a, ...), custom_call_target="tpu_custom_call" | custom-call | tf_op jit(solution)/shard_map/euler_basis/pallas_call | solution.py:165
  63.6 2.7 %collective-permute-start.11 = (f32[64,128]{1,0:T(8,128)S(1)}, f32[64,128]{1,0:T(8,128)S(1)}, u32[]{:S(2)}, u32[]{:S(2)}) collective-permute-start(f32[64,128]{1,0:T(8,128)S(1)} %get-tuple-element.28), channel_id=1, source_target_pairs={{0,8},{1,9},{2,10},{3,11},{4,12},{5,13},{6,14},{7,15},{8,0},{9,1},... | collective-permute-start | bytes 98312 | tf_op jit(solution)/shard_map/ppermute | solution.py:211
  66.3 1.0 %collective-permute-start.12 = (f32[64,128]{1,0:T(8,128)S(1)}, f32[64,128]{1,0:T(8,128)S(1)}, u32[]{:S(2)}, u32[]{:S(2)}) collective-permute-start(f32[64,128]{1,0:T(8,128)S(1)} %get-tuple-element.29), channel_id=1, source_target_pairs={{0,12},{1,13},{2,14},{3,15},{4,0},{5,1},{6,2},{7,3},{8,4},{9,5},{1... | collective-permute-start | bytes 98312 | tf_op jit(solution)/shard_map/ppermute | solution.py:211
  67.3 1.0 %collective-permute-done.10.g1 = f32[64,128]{1,0:T(8,128)S(1)} collective-permute-done((f32[64,128]{1,0:T(8,128)S(1)}, f32[64,128]{1,0:T(8,128)S(1)}, u32[]{:S(2)}, u32[]{:S(2)}) %collective-permute-start.10) | collective-permute-done | bytes 32800 | tf_op jit(solution)/shard_map/ppermute | solution.py:211
  69.0 1.2 %collective-permute-done.12.g3 = f32[64,128]{1,0:T(8,128)S(1)} collective-permute-done((f32[64,128]{1,0:T(8,128)S(1)}, f32[64,128]{1,0:T(8,128)S(1)}, u32[]{:S(2)}, u32[]{:S(2)}) %collective-permute-start.12) | collective-permute-done | bytes 32800 | tf_op jit(solution)/shard_map/ppermute | solution.py:211
  70.2 1.4 %finish.1 = (f32[59,1,128]{2,1,0:T(1,128)}, f32[59,1,128]{2,1,0:T(1,128)}) custom-call(s32[1]{0:T(128)} %bitcast.rowsum_ref, f32[59,128]{1,0:T(8,128)S(1)} %get-tuple-element.33.now_ref, f32[59,1,128]{2,1,0:T(1,128)S(1)} %bitcast.23, f32[64,128]{1,0:T(8,128)S(1)} %get-tuple-element.26.g0, f32[64,128]{1,0:T(8,128)S(1)} %collective-permute-done.10.g1, ...), custom_call_target="tpu_custom_call" | custom-call | tf_op jit(solution)/shard_map/finish/pallas_call | solution.py:73
  (23 shorter events, 2.8 us)
Async XLA Ops:
  3.1 7.4 %copy-start.2 = (f32[1,59,128]{2,0,1:T(1,128)S(1)}, f32[1,59,128]{2,0,1:T(1,128)}, u32[]{:S(2)}) copy-start(f32[1,59,128]{2,0,1:T(1,128)} %param.8) | copy-start | bytes 90628
  3.1 19.5 %all-to-all-start = ((s16[16,72,256]{2,1,0:T(8,128)(2,1)}), s16[16,72,256]{2,1,0:T(8,128)(2,1)S(1)}, u32[]{:S(2)}, u32[]{:S(2)}) async-start(s16[16,72,256]{2,1,0:T(8,128)(2,1)} %pack_tables.1), calls=%async_computation | async-start | bytes 1179648 | tf_op jit(solution)/shard_map/all_to_all | solution.py:198
  10.6 6.6 %collective-permute-start.2 = (bf16[64,128]{1,0:T(8,128)(2,1)S(1)}, bf16[64,128]{1,0:T(8,128)(2,1)S(1)}, u32[]{:S(2)}, u32[]{:S(2)}) collective-permute-start(bf16[64,128]{1,0:T(8,128)(2,1)S(1)} %maximum_maximum_fusion.q0), channel_id=1, source_target_pairs={{0,4},{1,5},{2,6},{3,7},{4,8},{5,9},{6,10},{7,11},{8,12},{9,13},{1... | collective-permute-start | bytes 49160 | tf_op jit(solution)/shard_map/ppermute | solution.py:190
  12.6 5.5 %collective-permute-start.1 = (bf16[64,128]{1,0:T(8,128)(2,1)S(1)}, bf16[64,128]{1,0:T(8,128)(2,1)S(1)}, u32[]{:S(2)}, u32[]{:S(2)}) collective-permute-start(bf16[64,128]{1,0:T(8,128)(2,1)S(1)} %maximum_maximum_fusion.q0), channel_id=1, source_target_pairs={{0,8},{1,9},{2,10},{3,11},{4,12},{5,13},{6,14},{7,15},{8,0},{9,1},... | collective-permute-start | bytes 49160 | tf_op jit(solution)/shard_map/ppermute | solution.py:190
  16.2 3.7 %collective-permute-start = (bf16[64,128]{1,0:T(8,128)(2,1)S(1)}, bf16[64,128]{1,0:T(8,128)(2,1)S(1)}, u32[]{:S(2)}, u32[]{:S(2)}) collective-permute-start(bf16[64,128]{1,0:T(8,128)(2,1)S(1)} %maximum_maximum_fusion.q0), channel_id=1, source_target_pairs={{0,12},{1,13},{2,14},{3,15},{4,0},{5,1},{6,2},{7,3},{8,4},{9,5},{1... | collective-permute-start | bytes 49160 | tf_op jit(solution)/shard_map/ppermute | solution.py:190
  22.5 2.0 %collective-permute-start.3 = (s16[16,72,256]{2,1,0:T(8,128)(2,1)S(1)}, s16[16,72,256]{2,1,0:T(8,128)(2,1)S(1)}, u32[]{:S(2)}, u32[]{:S(2)}) collective-permute-start(s16[16,72,256]{2,1,0:T(8,128)(2,1)S(1)} %all-to-all-done.tab_a), channel_id=1, source_target_pairs={{0,16},{16,0},{32,48},{48,32},{64,80},{80,64},{96,112},{112,96},{1... | collective-permute-start | bytes 1769480 | tf_op jit(solution)/shard_map/ppermute | solution.py:203
  22.5 2.0 %copy-start.1 = (s32[16,16]{1,0:T(8,128)S(1)}, s32[16,16]{1,0:T(8,128)}, u32[]{:S(2)}) copy-start(s32[16,16]{1,0:T(8,128)} %counts_ref.3) | copy-start | bytes 3076
  24.6 20.2 %copy-start = (f32[1,59,128]{2,0,1:T(1,128)S(1)}, f32[1,59,128]{2,0,1:T(1,128)}, u32[]{:S(2)}) copy-start(f32[1,59,128]{2,0,1:T(1,128)} %param.9) | copy-start | bytes 90628
  35.3 8.0 %collective-permute-start.4 = (f32[64,128]{1,0:T(8,128)S(1)}, f32[64,128]{1,0:T(8,128)S(1)}, u32[]{:S(2)}, u32[]{:S(2)}) collective-permute-start(f32[64,128]{1,0:T(8,128)S(1)} %get-tuple-element.23), channel_id=1, source_target_pairs={{0,4},{1,5},{2,6},{3,7},{4,8},{5,9},{6,10},{7,11},{8,12},{9,13},{1... | collective-permute-start | bytes 98312 | tf_op jit(solution)/shard_map/ppermute | solution.py:211
  37.3 6.0 %collective-permute-start.5 = (f32[64,128]{1,0:T(8,128)S(1)}, f32[64,128]{1,0:T(8,128)S(1)}, u32[]{:S(2)}, u32[]{:S(2)}) collective-permute-start(f32[64,128]{1,0:T(8,128)S(1)} %get-tuple-element.24), channel_id=1, source_target_pairs={{0,8},{1,9},{2,10},{3,11},{4,12},{5,13},{6,14},{7,15},{8,0},{9,1},... | collective-permute-start | bytes 98312 | tf_op jit(solution)/shard_map/ppermute | solution.py:211
  40.8 3.9 %collective-permute-start.6 = (f32[64,128]{1,0:T(8,128)S(1)}, f32[64,128]{1,0:T(8,128)S(1)}, u32[]{:S(2)}, u32[]{:S(2)}) collective-permute-start(f32[64,128]{1,0:T(8,128)S(1)} %get-tuple-element.25), channel_id=1, source_target_pairs={{0,12},{1,13},{2,14},{3,15},{4,0},{5,1},{6,2},{7,3},{8,4},{9,5},{1... | collective-permute-start | bytes 98312 | tf_op jit(solution)/shard_map/ppermute | solution.py:211
  44.9 5.0 %collective-permute-start.9 = (bf16[64,128]{1,0:T(8,128)(2,1)S(1)}, bf16[64,128]{1,0:T(8,128)(2,1)S(1)}, u32[]{:S(2)}, u32[]{:S(2)}) collective-permute-start(bf16[64,128]{1,0:T(8,128)(2,1)S(1)} %maximum_maximum_fusion.1.q0), channel_id=1, source_target_pairs={{0,4},{1,5},{2,6},{3,7},{4,8},{5,9},{6,10},{7,11},{8,12},{9,13},{1... | collective-permute-start | bytes 49160 | tf_op jit(solution)/shard_map/ppermute | solution.py:190
  45.0 5.6 %collective-permute-start.8 = (bf16[64,128]{1,0:T(8,128)(2,1)S(1)}, bf16[64,128]{1,0:T(8,128)(2,1)S(1)}, u32[]{:S(2)}, u32[]{:S(2)}) collective-permute-start(bf16[64,128]{1,0:T(8,128)(2,1)S(1)} %maximum_maximum_fusion.1.q0), channel_id=1, source_target_pairs={{0,8},{1,9},{2,10},{3,11},{4,12},{5,13},{6,14},{7,15},{8,0},{9,1},... | collective-permute-start | bytes 49160 | tf_op jit(solution)/shard_map/ppermute | solution.py:190
  48.7 3.7 %collective-permute-start.7 = (bf16[64,128]{1,0:T(8,128)(2,1)S(1)}, bf16[64,128]{1,0:T(8,128)(2,1)S(1)}, u32[]{:S(2)}, u32[]{:S(2)}) collective-permute-start(bf16[64,128]{1,0:T(8,128)(2,1)S(1)} %maximum_maximum_fusion.1.q0), channel_id=1, source_target_pairs={{0,12},{1,13},{2,14},{3,15},{4,0},{5,1},{6,2},{7,3},{8,4},{9,5},{1... | collective-permute-start | bytes 49160 | tf_op jit(solution)/shard_map/ppermute | solution.py:190
  63.1 5.2 %collective-permute-start.10 = (f32[64,128]{1,0:T(8,128)S(1)}, f32[64,128]{1,0:T(8,128)S(1)}, u32[]{:S(2)}, u32[]{:S(2)}) collective-permute-start(f32[64,128]{1,0:T(8,128)S(1)} %get-tuple-element.27), channel_id=1, source_target_pairs={{0,4},{1,5},{2,6},{3,7},{4,8},{5,9},{6,10},{7,11},{8,12},{9,13},{1... | collective-permute-start | bytes 98312 | tf_op jit(solution)/shard_map/ppermute | solution.py:211
  63.6 5.4 %collective-permute-start.11 = (f32[64,128]{1,0:T(8,128)S(1)}, f32[64,128]{1,0:T(8,128)S(1)}, u32[]{:S(2)}, u32[]{:S(2)}) collective-permute-start(f32[64,128]{1,0:T(8,128)S(1)} %get-tuple-element.28), channel_id=1, source_target_pairs={{0,8},{1,9},{2,10},{3,11},{4,12},{5,13},{6,14},{7,15},{8,0},{9,1},... | collective-permute-start | bytes 98312 | tf_op jit(solution)/shard_map/ppermute | solution.py:211
  66.3 3.9 %collective-permute-start.12 = (f32[64,128]{1,0:T(8,128)S(1)}, f32[64,128]{1,0:T(8,128)S(1)}, u32[]{:S(2)}, u32[]{:S(2)}) collective-permute-start(f32[64,128]{1,0:T(8,128)S(1)} %get-tuple-element.29), channel_id=1, source_target_pairs={{0,12},{1,13},{2,14},{3,15},{4,0},{5,1},{6,2},{7,3},{8,4},{9,5},{1... | collective-permute-start | bytes 98312 | tf_op jit(solution)/shard_map/ppermute | solution.py:211

commit v7 on v6

--- a/solution.py
+++ b/solution.py
@@ -1,3 +1,5 @@
+import functools
+
 import jax
 import jax.numpy as jnp
 from jax import lax
@@ -5,7 +7,6 @@
 from jax.experimental.pallas import tpu as pltpu
 from jax.sharding import PartitionSpec as P
 
-ITERS = 2
 GAMMA = 2.0
 BETA = 0.96
 damping = 0.5
@@ -56,6 +57,38 @@
     )(live, surplus, *(jnp.transpose(v, (1, 0, 2)) for v in (dims, levels, index)))
 
 
+def advance_kernel(where_ref, counts_ref, p0, p1, p2, p3, s0, s1, s2, s3, q0, q1, q2, q3, cur_ref):
+    z, y = where_ref[0], where_ref[1]
+    row = lax.broadcasted_iota(jnp.int32, (HALF, 128), 0)
+    for j, (state, q) in enumerate(((s0, q0), (s1, q1), (s2, q2), (s3, q3))):
+        s = lax.rem(z + j, RING) * RING + y
+        rowsum = counts_ref[s, 0]
+        for t in range(1, RING * RING):
+            rowsum += counts_ref[s, t]
+        total = (p0[j] + p2[(j - 2) % RING]) + (p1[(j - 1) % RING] + p3[(j - 3) % RING])
+        consumption = (BETA * (total / rowsum.astype(F32))) ** (-1.0 / GAMMA)
+        share = 1.0 / (1.0 + jnp.exp(consumption - state[1]))
+        new = (1.0 - damping) * state[0] + damping * share
+        new = jnp.where(row < DIM, new, jnp.where(row == DIM, 1.0, 0.0))
+        q[...] = new.astype(BF)
+        if j == 0:
+            cur_ref[...] = new
+
+
+def advance(where, counts, parts, states):
+    vm = pl.BlockSpec(memory_space=pltpu.VMEM)
+    sm = pl.BlockSpec(memory_space=pltpu.SMEM)
+    *queries, current = pl.pallas_call(
+        advance_kernel,
+        out_shape=[jax.ShapeDtypeStruct((HALF, 128), BF)] * RING + [jax.ShapeDtypeStruct((HALF, 128), F32)],
+        in_specs=[sm, sm] + [vm] * (2 * RING),
+        out_specs=[vm] * (RING + 1),
+        compiler_params=pltpu.CompilerParams(vmem_limit_bytes=4 << 20),
+        name="advance",
+    )(where, counts, *parts, *states)
+    return queries, current
+
+
 def finish_kernel(rowsum_ref, now_ref, income_ref, g0, g1, g2, g3, cur_ref, con_ref):
     total = ((g0[...] + g1[...]) + (g2[...] + g3[...]))[:DIM]
     expect = total / rowsum_ref[0].astype(F32)
@@ -63,7 +96,7 @@
     value = income_ref[:, 0, :] - consumption
     share = 1.0 / (1.0 + jnp.exp(-value))
     con_ref[:, 0, :] = consumption
-    cur_ref[:, 0, :] = (1.0 - damping) * now_ref[...] + damping * share
+    cur_ref[:, 0, :] = (1.0 - damping) * now_ref[0:DIM, :] + damping * share
 
 
 def finish(rowsum, current, income, got):
@@ -82,11 +115,12 @@
 
 
 def kernel(
-    where_ref, counts_ref, tab_a, tab_b, q0, q1, q2, q3, o0, o1, o2, o3, qt_ref, sel_a, sel_b, basis_a, basis_b, acc_ref
+    first, where_ref, counts_ref, tab_a, tab_b, q0, q1, q2, q3, *refs
 ):
+    outs, (qt_ref, sel_a, sel_b, basis_a, basis_b, acc_ref) = refs[:-6], refs[-6:]
     z, y = where_ref[0], where_ref[1]
     for j, q in enumerate((q0, q1, q2, q3)):
-        whole = q[...].astype(F32)
+        whole = (q[0] if first else q[...]).astype(BF).astype(F32)
         whole = jnp.where(lax.broadcasted_iota(jnp.int32, whole.shape, 0) < DIM, whole * SPLIT, whole)
         high = whole.astype(F8).astype(F32)
         qt_ref[pl.ds(j * 128, 128), :] = jnp.concatenate([high, whole - high], axis=0).T.astype(F8)
@@ -118,9 +152,9 @@
             basis_ref[:, pl.ds(b * 256, 256)] = jnp.maximum(basis.astype(BF), BF(0.0))
 
     def halves(blk):
-        steps = blk[0:HALF].astype(jnp.int32)
-        high = jnp.right_shift(steps, 8)
-        return jnp.concatenate([high.astype(F32), (steps - high * 256).astype(F32)], axis=0).astype(BF)
+        steps = blk[0:HALF].astype(jnp.int32).astype(F32)
+        high = steps.astype(BF)
+        return jnp.concatenate([high, (steps - high.astype(F32)).astype(BF)], axis=0)
 
     def sums(u, basis_ref):
         weights = jnp.concatenate([halves(block(u, b)) for b in range(UNIT)], axis=1)
@@ -148,25 +182,32 @@
     sums(units - 2, basis_a)
     sums(units - 1, basis_b)
 
-    for j, o in enumerate((o0, o1, o2, o3)):
+    for j in range(RING):
         s = lax.rem(z + j, RING) * RING + y
         total = None
         for t in range(RING):
             value = acc_ref[t, pl.ds(j * 128, 128), :]
             count = counts_ref[s, z * RING + t].astype(F32)
-            term = count * jnp.exp((256.0 * STEP) * value + STEP * pltpu.roll(value, HALF, 1))
+            term = count * jnp.exp(STEP * (value + pltpu.roll(value, HALF, 1)))
             total = term if total is None else total + term
-        o[...] = total.T[:HALF]
-
-
-def partial_sums(where, counts, tables, queries):
+        if first:
+            outs[0][j] = total.T[:HALF]
+        else:
+            outs[j][...] = total.T[:HALF]
+
+
+def partial_sums(first, where, counts, tables, queries):
     vm = pl.BlockSpec(memory_space=pltpu.VMEM)
     sm = pl.BlockSpec(memory_space=pltpu.SMEM)
+    if first:
+        shapes = [jax.ShapeDtypeStruct((RING, HALF, 128), F32)]
+    else:
+        shapes = [jax.ShapeDtypeStruct((HALF, 128), F32)] * RING
     return pl.pallas_call(
-        kernel,
-        out_shape=[jax.ShapeDtypeStruct((HALF, 128), F32)] * RING,
+        functools.partial(kernel, first),
+        out_shape=shapes,
         in_specs=[sm, sm] + [vm] * 6,
-        out_specs=[vm] * RING,
+        out_specs=[vm] * len(shapes),
         scratch_shapes=[
             pltpu.VMEM((512, 2 * HALF), F8),
             pltpu.VMEM((UNIT, 3, 2 * HALF, 256), F8),
@@ -184,9 +225,11 @@
     return [(z * RING + y, (z + dz) % RING * RING + y) for z in range(RING) for y in range(RING)]
 
 
-def spread(current):
+def spread(current, income):
     nq = current.shape[1]
-    own = jnp.concatenate([current.astype(BF), jnp.ones((1, nq), BF), jnp.zeros((HALF - DIM - 1, nq), BF)], axis=0)
+    rest = jnp.zeros((HALF - DIM - 1, nq), F32)
+    one = jnp.ones((1, nq), F32)
+    own = jnp.stack([jnp.concatenate([v, one, rest], axis=0) for v in (current, income)])
     return [own] + [lax.ppermute(own, "shk", shift(-j)) for j in range(1, RING)]
 
 
@@ -196,24 +239,18 @@
         [(2 * x + c) * 16 + z * RING + y for x in range(RING) for y in range(RING)] for c in range(2) for z in range(RING)
     ]
     mine = lax.all_to_all(blocks, ("pts", "shk"), 0, 0, tiled=True, axis_index_groups=groups)
-    current = savings[0]
-    income = wealth[0]
-    queries = spread(current)
-    mine, *queries = lax.optimization_barrier((mine, *queries))
+    states = spread(savings[0], wealth[0])
+    mine, *states = lax.optimization_barrier((mine, *states))
     tables = (mine, lax.ppermute(mine, "pts", [(i, i ^ 1) for i in range(8)]))
     shock = lax.axis_index("shk")
     where = jnp.stack([shock // RING, shock % RING]).astype(jnp.int32)
     rowsum = jnp.sum(lax.dynamic_index_in_dim(trans_counts, shock, 0, keepdims=False))
-    for sweep in range(ITERS):
-        if sweep:
-            queries = spread(current)
-        parts = partial_sums(where, trans_counts, tables, queries)
-        got = [parts[0]] + [lax.ppermute(parts[j], "shk", shift(j)) for j in range(1, RING)]
-        if sweep == ITERS - 1:
-            return finish(rowsum[None], current, jnp.transpose(wealth, (1, 0, 2)), got)
-        expect = ((got[0] + got[1]) + (got[2] + got[3]))[:DIM] / rowsum.astype(F32)
-        consumption = (BETA * expect) ** (-1.0 / GAMMA)
-        current = (1.0 - damping) * current + damping * jax.nn.sigmoid(income - consumption)
+    (sums,) = partial_sums(True, where, trans_counts, tables, states)
+    parts = [sums] + [lax.ppermute(sums, "shk", shift(-k)) for k in range(1, RING)]
+    queries, current = advance(where, trans_counts, parts, states)
+    parts = partial_sums(False, where, trans_counts, tables, queries)
+    got = [parts[0]] + [lax.ppermute(parts[j], "shk", shift(j)) for j in range(1, RING)]
+    return finish(rowsum[None], current, jnp.transpose(wealth, (1, 0, 2)), got)
 
 
 def solution(mesh):

time: 72 us -> 67.5 us (0.938)
  starting transfers between devices: 28.9 us -> 25.4 us
    ppermute x0 -> x3, starting transfers between devices: none -> 6.58 us  [per_device(): lax.ppermute(sums, 'shk', shift(-k))]
    ppermute x6 -> x3, starting transfers between devices: 10.8 us -> 4.94 us  [per_device(): lax.ppermute(parts[j], 'shk', shift(j))]
    ppermute x0 -> x3, waiting for transfers between devices: none -> 5.31 us  [per_device(): lax.ppermute(sums, 'shk', shift(-k))]
    ppermute x6 -> x3, starting transfers between devices: 10.8 us -> 6.58 us  [spread(): return [own] + [lax.ppermute(own, 'shk', shift(-j)) for j in range(1, RING)]]
    ppermute x6 -> x3, waiting for transfers between devices: 6.02 us -> 3.26 us  [spread(): return [own] + [lax.ppermute(own, 'shk', shift(-j)) for j in range(1, RING)]]
    ppermute x6 -> x3, waiting for transfers between devices: 4.36 us -> 2.06 us  [per_device(): lax.ppermute(parts[j], 'shk', shift(j))]
    pallas_call x2 -> x3, Pallas kernels: 21.4 us -> 21.9 us  [the longest x2 21.1 us: partial_sums(): pl.pallas_call(functools.partial(kernel, first), out_shape=shapes, in_spe...]
  transfers between devices with their start and end apart: 14 -> 11, of which waited for: 11 -> 8; matrix products, arithmetic and copies ran while one was open for 1% -> 1% of each run, Pallas kernels for 0% -> 0%
where the time goes in v7:
time: 67.5 us; the launch traced here: 67.2 us
  starting transfers between devices  25.4 us (38%)
  Pallas kernels  24.9 us (37%)
  waiting for transfers between devices  14.6 us (22%)
  between operations  1.33 us (2%)
  other arithmetic  0.76 us (1%)
    pallas_call x2, Pallas kernels, partial_sums(): pl.pallas_call(functools.partial(kernel, first), out_shape=shapes, in_spe...  21.1 us
    all_to_all x1, starting transfers between devices, per_device(): lax.all_to_all(blocks, ('pts', 'shk'), 0, 0, tiled=True, axis_index_group...  7.28 us
    ppermute x3, starting transfers between devices, per_device(): lax.ppermute(sums, 'shk', shift(-k))  6.58 us
    ppermute x3, starting transfers between devices, spread(): return [own] + [lax.ppermute(own, 'shk', shift(-j)) for j in range(1, RING)]  6.58 us
    ppermute x3, waiting for transfers between devices, per_device(): lax.ppermute(sums, 'shk', shift(-k))  5.31 us
    ppermute x3, starting transfers between devices, per_device(): lax.ppermute(parts[j], 'shk', shift(j))  4.94 us
    ppermute x3, waiting for transfers between devices, spread(): return [own] + [lax.ppermute(own, 'shk', shift(-j)) for j in range(1, RING)]  3.26 us
    all_to_all x1, waiting for transfers between devices, per_device(): lax.all_to_all(blocks, ('pts', 'shk'), 0, 0, tiled=True, axis_index_group...  2.09 us
  transfers between devices with their start and end apart: 11, of which 8 were waited for; matrix products, arithmetic and copies ran while one was open for 1% of the time, Pallas kernels for 0%

profile of v7, /device:TPU:0, one launch (start us, length us, event | category | flops | bytes accessed | tf_op | source)
XLA Modules:
  0.0 67.2 jit_solution(12439625671621507192)
XLA Ops:
  1.3 1.8 %pack_tables.1 = s16[16,72,256]{2,1,0:T(8,128)(2,1)} custom-call(s32[1,1]{1,0:T(1,128)S(6)} %copy.14.live_ref, bf16[118,256]{1,0:T(8,128)(2,1)} %bitcast.20, s32[3,1,256]{2,1,0:T(1,128)} %bitcast.21, s32[3,1,256]{2,1,0:T(1,128)} %bitcast.22, s32[3,1,256]{2,1,0:T(1,128)} %bitcast.23), custom_call_target="tpu_custom_call" | custom-call | tf_op jit(solution)/shard_map/pack_tables/pallas_call | solution.py:50
  3.1 7.3 %all-to-all-start = ((s16[16,72,256]{2,1,0:T(8,128)(2,1)}), s16[16,72,256]{2,1,0:T(8,128)(2,1)S(1)}, u32[]{:S(2)}, u32[]{:S(2)}) async-start(s16[16,72,256]{2,1,0:T(8,128)(2,1)} %pack_tables.1), calls=%async_computation | async-start | bytes 1179648 | tf_op jit(solution)/shard_map/all_to_all | solution.py:241
  10.6 2.0 %collective-permute-start.2 = (f32[2,64,128]{2,1,0:T(8,128)S(1)}, f32[2,64,128]{2,1,0:T(8,128)S(1)}, u32[]{:S(2)}, u32[]{:S(2)}) collective-permute-start(f32[2,64,128]{2,1,0:T(8,128)S(1)} %pad_maximum_fusion.q0.s0), channel_id=1, source_target_pairs={{0,4},{1,5},{2,6},{3,7},{4,8},{5,9},{6,10},{7,11},{8,12},{9,13},{1... | collective-permute-start | bytes 196616 | tf_op jit(solution)/shard_map/ppermute | solution.py:233
  12.6 3.6 %collective-permute-start.1 = (f32[2,64,128]{2,1,0:T(8,128)S(1)}, f32[2,64,128]{2,1,0:T(8,128)S(1)}, u32[]{:S(2)}, u32[]{:S(2)}) collective-permute-start(f32[2,64,128]{2,1,0:T(8,128)S(1)} %pad_maximum_fusion.q0.s0), channel_id=1, source_target_pairs={{0,8},{1,9},{2,10},{3,11},{4,12},{5,13},{6,14},{7,15},{8,0},{9,1},... | collective-permute-start | bytes 196616 | tf_op jit(solution)/shard_map/ppermute | solution.py:233
  16.2 1.0 %collective-permute-start = (f32[2,64,128]{2,1,0:T(8,128)S(1)}, f32[2,64,128]{2,1,0:T(8,128)S(1)}, u32[]{:S(2)}, u32[]{:S(2)}) collective-permute-start(f32[2,64,128]{2,1,0:T(8,128)S(1)} %pad_maximum_fusion.q0.s0), channel_id=1, source_target_pairs={{0,12},{1,13},{2,14},{3,15},{4,0},{5,1},{6,2},{7,3},{8,4},{9,5},{1... | collective-permute-start | bytes 196616 | tf_op jit(solution)/shard_map/ppermute | solution.py:233
  17.2 1.9 %collective-permute-done.1.q2.s2 = f32[2,64,128]{2,1,0:T(8,128)S(1)} collective-permute-done((f32[2,64,128]{2,1,0:T(8,128)S(1)}, f32[2,64,128]{2,1,0:T(8,128)S(1)}, u32[]{:S(2)}, u32[]{:S(2)}) %collective-permute-start.1) | collective-permute-done | bytes 65568 | tf_op jit(solution)/shard_map/ppermute | solution.py:233
  19.1 1.3 %collective-permute-done.q1.s1 = f32[2,64,128]{2,1,0:T(8,128)S(1)} collective-permute-done((f32[2,64,128]{2,1,0:T(8,128)S(1)}, f32[2,64,128]{2,1,0:T(8,128)S(1)}, u32[]{:S(2)}, u32[]{:S(2)}) %collective-permute-start) | collective-permute-done | bytes 65568 | tf_op jit(solution)/shard_map/ppermute | solution.py:233
  20.5 2.1 %all-to-all-done.tab_a = s16[16,72,256]{2,1,0:T(8,128)(2,1)S(1)} async-done(((s16[16,72,256]{2,1,0:T(8,128)(2,1)}), s16[16,72,256]{2,1,0:T(8,128)(2,1)S(1)}, u32[]{:S(2)}, u32[]{:S(2)}) %all-to-all-start) | async-done | bytes 589856 | tf_op jit(solution)/shard_map/all_to_all | solution.py:241
  22.6 1.9 %collective-permute-done.3.tab_b = s16[16,72,256]{2,1,0:T(8,128)(2,1)S(1)} collective-permute-done((s16[16,72,256]{2,1,0:T(8,128)(2,1)S(1)}, s16[16,72,256]{2,1,0:T(8,128)(2,1)S(1)}, u32[]{:S(2)}, u32[]{:S(2)}) %collective-permute-start.3) | collective-permute-done | bytes 589856 | tf_op jit(solution)/shard_map/ppermute | solution.py:244
  24.6 10.6 %euler_basis.2.p0 = f32[4,64,128]{2,1,0:T(8,128)S(1)} custom-call(s32[2]{0:T(128)S(1)} %pad_add_fusion.where_ref, s32[16,16]{1,0:T(8,128)S(1)} %copy-done.1, s16[16,72,256]{2,1,0:T(8,128)(2,1)S(1)} %all-to-all-done.tab_a, s16[16,72,256]{2,1,0:T(8,128)(2,1)S(1)} %collective-permute-done.3.tab_b, f32[2,64,128]{2,1,0:T(8,128)S(1)} %pad_maximum_fusion.q0.s0, ...), custom_call_target="tpu_custom_call" | custom-call | tf_op jit(solution)/shard_map/euler_basis/pallas_call | solution.py:206
  35.1 2.0 %collective-permute-start.6 = (f32[4,64,128]{2,1,0:T(8,128)S(1)}, f32[4,64,128]{2,1,0:T(8,128)S(1)}, u32[]{:S(2)}, u32[]{:S(2)}) collective-permute-start(f32[4,64,128]{2,1,0:T(8,128)S(1)} %euler_basis.2.p0), channel_id=1, source_target_pairs={{0,4},{1,5},{2,6},{3,7},{4,8},{5,9},{6,10},{7,11},{8,12},{9,13},{1... | collective-permute-start | bytes 393224 | tf_op jit(solution)/shard_map/ppermute | solution.py:249
  37.1 3.6 %collective-permute-start.5 = (f32[4,64,128]{2,1,0:T(8,128)S(1)}, f32[4,64,128]{2,1,0:T(8,128)S(1)}, u32[]{:S(2)}, u32[]{:S(2)}) collective-permute-start(f32[4,64,128]{2,1,0:T(8,128)S(1)} %euler_basis.2.p0), channel_id=1, source_target_pairs={{0,8},{1,9},{2,10},{3,11},{4,12},{5,13},{6,14},{7,15},{8,0},{9,1},... | collective-permute-start | bytes 393224 | tf_op jit(solution)/shard_map/ppermute | solution.py:249
  40.7 1.0 %collective-permute-start.4 = (f32[4,64,128]{2,1,0:T(8,128)S(1)}, f32[4,64,128]{2,1,0:T(8,128)S(1)}, u32[]{:S(2)}, u32[]{:S(2)}) collective-permute-start(f32[4,64,128]{2,1,0:T(8,128)S(1)} %euler_basis.2.p0), channel_id=1, source_target_pairs={{0,12},{1,13},{2,14},{3,15},{4,0},{5,1},{6,2},{7,3},{8,4},{9,5},{1... | collective-permute-start | bytes 393224 | tf_op jit(solution)/shard_map/ppermute | solution.py:249
  41.7 1.3 %collective-permute-done.6.p3 = f32[4,64,128]{2,1,0:T(8,128)S(1)} collective-permute-done((f32[4,64,128]{2,1,0:T(8,128)S(1)}, f32[4,64,128]{2,1,0:T(8,128)S(1)}, u32[]{:S(2)}, u32[]{:S(2)}) %collective-permute-start.6) | collective-permute-done | bytes 131104 | tf_op jit(solution)/shard_map/ppermute | solution.py:249
  43.0 4.0 %collective-permute-done.5.p2 = f32[4,64,128]{2,1,0:T(8,128)S(1)} collective-permute-done((f32[4,64,128]{2,1,0:T(8,128)S(1)}, f32[4,64,128]{2,1,0:T(8,128)S(1)}, u32[]{:S(2)}, u32[]{:S(2)}) %collective-permute-start.5) | collective-permute-done | bytes 131104 | tf_op jit(solution)/shard_map/ppermute | solution.py:249
  47.0 0.8 %advance.1 = (bf16[64,128]{1,0:T(8,128)(2,1)S(1)}, bf16[64,128]{1,0:T(8,128)(2,1)S(1)}, bf16[64,128]{1,0:T(8,128)(2,1)S(1)}, bf16[64,128]{1,0:T(8,128)(2,1)S(1)}, f32[64,128]{1,0:T(8,128)S(1)}) custom-call(s32[2]{0:T(128)S(1)} %pad_add_fusion.where_ref, s32[16,16]{1,0:T(8,128)S(1)} %copy-done.1, f32[4,64,128]{2,1,0:T(8,128)S(1)} %euler_basis.2.p0, ...), custom_call_target="tpu_custom_call" | custom-call | tf_op jit(solution)/shard_map/advance/pallas_call | solution.py:81
  47.8 10.6 %euler_basis.3 = (f32[64,128]{1,0:T(8,128)S(1)}, f32[64,128]{1,0:T(8,128)S(1)}, f32[64,128]{1,0:T(8,128)S(1)}, f32[64,128]{1,0:T(8,128)S(1)}) custom-call(s32[2]{0:T(128)S(1)} %pad_add_fusion.where_ref, s32[16,16]{1,0:T(8,128)S(1)} %copy-done.1, s16[16,72,256]{2,1,0:T(8,128)(2,1)S(1)} %all-to-all-done.tab_a, ...), custom_call_target="tpu_custom_call" | custom-call | tf_op jit(solution)/shard_map/euler_basis/pallas_call | solution.py:206
  58.4 1.3 %collective-permute-start.7 = (f32[64,128]{1,0:T(8,128)S(1)}, f32[64,128]{1,0:T(8,128)S(1)}, u32[]{:S(2)}, u32[]{:S(2)}) collective-permute-start(f32[64,128]{1,0:T(8,128)S(1)} %get-tuple-element.29), channel_id=1, source_target_pairs={{0,4},{1,5},{2,6},{3,7},{4,8},{5,9},{6,10},{7,11},{8,12},{9,13},{1... | collective-permute-start | bytes 98312 | tf_op jit(solution)/shard_map/ppermute | solution.py:252
  59.7 2.4 %collective-permute-start.8 = (f32[64,128]{1,0:T(8,128)S(1)}, f32[64,128]{1,0:T(8,128)S(1)}, u32[]{:S(2)}, u32[]{:S(2)}) collective-permute-start(f32[64,128]{1,0:T(8,128)S(1)} %get-tuple-element.30), channel_id=1, source_target_pairs={{0,8},{1,9},{2,10},{3,11},{4,12},{5,13},{6,14},{7,15},{8,0},{9,1},... | collective-permute-start | bytes 98312 | tf_op jit(solution)/shard_map/ppermute | solution.py:252
  62.1 1.2 %collective-permute-start.9 = (f32[64,128]{1,0:T(8,128)S(1)}, f32[64,128]{1,0:T(8,128)S(1)}, u32[]{:S(2)}, u32[]{:S(2)}) collective-permute-start(f32[64,128]{1,0:T(8,128)S(1)} %get-tuple-element.31), channel_id=1, source_target_pairs={{0,12},{1,13},{2,14},{3,15},{4,0},{5,1},{6,2},{7,3},{8,4},{9,5},{1... | collective-permute-start | bytes 98312 | tf_op jit(solution)/shard_map/ppermute | solution.py:252
  63.3 0.6 dynamic-slice_reduce_fusion
  63.9 1.2 %collective-permute-done.8.g2 = f32[64,128]{1,0:T(8,128)S(1)} collective-permute-done((f32[64,128]{1,0:T(8,128)S(1)}, f32[64,128]{1,0:T(8,128)S(1)}, u32[]{:S(2)}, u32[]{:S(2)}) %collective-permute-start.8) | collective-permute-done | bytes 32800 | tf_op jit(solution)/shard_map/ppermute | solution.py:252
  65.1 0.9 %collective-permute-done.9.g3 = f32[64,128]{1,0:T(8,128)S(1)} collective-permute-done((f32[64,128]{1,0:T(8,128)S(1)}, f32[64,128]{1,0:T(8,128)S(1)}, u32[]{:S(2)}, u32[]{:S(2)}) %collective-permute-start.9) | collective-permute-done | bytes 32800 | tf_op jit(solution)/shard_map/ppermute | solution.py:252
  66.0 1.2 %finish.1 = (f32[59,1,128]{2,1,0:T(1,128)}, f32[59,1,128]{2,1,0:T(1,128)}) custom-call(s32[1]{0:T(128)} %bitcast.rowsum_ref, f32[64,128]{1,0:T(8,128)S(1)} %get-tuple-element.23.now_ref, f32[59,1,128]{2,1,0:T(1,128)S(1)} %bitcast.19, f32[64,128]{1,0:T(8,128)S(1)} %get-tuple-element.28.g0, f32[64,128]{1,0:T(8,128)S(1)} %collective-permute-done.7.g1, ...), custom_call_target="tpu_custom_call" | custom-call | tf_op jit(solution)/shard_map/finish/pallas_call | solution.py:106
  (17 shorter events, 0.3 us)
Async XLA Ops:
  3.1 7.4 %copy-start = (f32[1,59,128]{2,0,1:T(1,128)S(1)}, f32[1,59,128]{2,0,1:T(1,128)}, u32[]{:S(2)}) copy-start(f32[1,59,128]{2,0,1:T(1,128)} %param.9) | copy-start | bytes 90628
  3.1 7.4 %copy-start.2 = (f32[1,59,128]{2,0,1:T(1,128)S(1)}, f32[1,59,128]{2,0,1:T(1,128)}, u32[]{:S(2)}) copy-start(f32[1,59,128]{2,0,1:T(1,128)} %param.8) | copy-start | bytes 90628
  3.1 19.5 %all-to-all-start = ((s16[16,72,256]{2,1,0:T(8,128)(2,1)}), s16[16,72,256]{2,1,0:T(8,128)(2,1)S(1)}, u32[]{:S(2)}, u32[]{:S(2)}) async-start(s16[16,72,256]{2,1,0:T(8,128)(2,1)} %pack_tables.1), calls=%async_computation | async-start | bytes 1179648 | tf_op jit(solution)/shard_map/all_to_all | solution.py:241
  10.6 6.6 %collective-permute-start.2 = (f32[2,64,128]{2,1,0:T(8,128)S(1)}, f32[2,64,128]{2,1,0:T(8,128)S(1)}, u32[]{:S(2)}, u32[]{:S(2)}) collective-permute-start(f32[2,64,128]{2,1,0:T(8,128)S(1)} %pad_maximum_fusion.q0.s0), channel_id=1, source_target_pairs={{0,4},{1,5},{2,6},{3,7},{4,8},{5,9},{6,10},{7,11},{8,12},{9,13},{1... | collective-permute-start | bytes 196616 | tf_op jit(solution)/shard_map/ppermute | solution.py:233
  12.6 6.5 %collective-permute-start.1 = (f32[2,64,128]{2,1,0:T(8,128)S(1)}, f32[2,64,128]{2,1,0:T(8,128)S(1)}, u32[]{:S(2)}, u32[]{:S(2)}) collective-permute-start(f32[2,64,128]{2,1,0:T(8,128)S(1)} %pad_maximum_fusion.q0.s0), channel_id=1, source_target_pairs={{0,8},{1,9},{2,10},{3,11},{4,12},{5,13},{6,14},{7,15},{8,0},{9,1},... | collective-permute-start | bytes 196616 | tf_op jit(solution)/shard_map/ppermute | solution.py:233
  16.2 4.3 %collective-permute-start = (f32[2,64,128]{2,1,0:T(8,128)S(1)}, f32[2,64,128]{2,1,0:T(8,128)S(1)}, u32[]{:S(2)}, u32[]{:S(2)}) collective-permute-start(f32[2,64,128]{2,1,0:T(8,128)S(1)} %pad_maximum_fusion.q0.s0), channel_id=1, source_target_pairs={{0,12},{1,13},{2,14},{3,15},{4,0},{5,1},{6,2},{7,3},{8,4},{9,5},{1... | collective-permute-start | bytes 196616 | tf_op jit(solution)/shard_map/ppermute | solution.py:233
  22.6 2.0 %collective-permute-start.3 = (s16[16,72,256]{2,1,0:T(8,128)(2,1)S(1)}, s16[16,72,256]{2,1,0:T(8,128)(2,1)S(1)}, u32[]{:S(2)}, u32[]{:S(2)}) collective-permute-start(s16[16,72,256]{2,1,0:T(8,128)(2,1)S(1)} %all-to-all-done.tab_a), channel_id=1, source_target_pairs={{0,16},{16,0},{32,48},{48,32},{64,80},{80,64},{96,112},{112,96},{1... | collective-permute-start | bytes 1769480 | tf_op jit(solution)/shard_map/ppermute | solution.py:244
  22.6 2.0 %copy-start.1 = (s32[16,16]{1,0:T(8,128)S(1)}, s32[16,16]{1,0:T(8,128)}, u32[]{:S(2)}) copy-start(s32[16,16]{1,0:T(8,128)} %counts_ref.5) | copy-start | bytes 3076
  35.1 7.9 %collective-permute-start.6 = (f32[4,64,128]{2,1,0:T(8,128)S(1)}, f32[4,64,128]{2,1,0:T(8,128)S(1)}, u32[]{:S(2)}, u32[]{:S(2)}) collective-permute-start(f32[4,64,128]{2,1,0:T(8,128)S(1)} %euler_basis.2.p0), channel_id=1, source_target_pairs={{0,4},{1,5},{2,6},{3,7},{4,8},{5,9},{6,10},{7,11},{8,12},{9,13},{1... | collective-permute-start | bytes 393224 | tf_op jit(solution)/shard_map/ppermute | solution.py:249
  37.1 9.9 %collective-permute-start.5 = (f32[4,64,128]{2,1,0:T(8,128)S(1)}, f32[4,64,128]{2,1,0:T(8,128)S(1)}, u32[]{:S(2)}, u32[]{:S(2)}) collective-permute-start(f32[4,64,128]{2,1,0:T(8,128)S(1)} %euler_basis.2.p0), channel_id=1, source_target_pairs={{0,8},{1,9},{2,10},{3,11},{4,12},{5,13},{6,14},{7,15},{8,0},{9,1},... | collective-permute-start | bytes 393224 | tf_op jit(solution)/shard_map/ppermute | solution.py:249
  40.7 6.3 %collective-permute-start.4 = (f32[4,64,128]{2,1,0:T(8,128)S(1)}, f32[4,64,128]{2,1,0:T(8,128)S(1)}, u32[]{:S(2)}, u32[]{:S(2)}) collective-permute-start(f32[4,64,128]{2,1,0:T(8,128)S(1)} %euler_basis.2.p0), channel_id=1, source_target_pairs={{0,12},{1,13},{2,14},{3,15},{4,0},{5,1},{6,2},{7,3},{8,4},{9,5},{1... | collective-permute-start | bytes 393224 | tf_op jit(solution)/shard_map/ppermute | solution.py:249
  58.4 5.5 %collective-permute-start.7 = (f32[64,128]{1,0:T(8,128)S(1)}, f32[64,128]{1,0:T(8,128)S(1)}, u32[]{:S(2)}, u32[]{:S(2)}) collective-permute-start(f32[64,128]{1,0:T(8,128)S(1)} %get-tuple-element.29), channel_id=1, source_target_pairs={{0,4},{1,5},{2,6},{3,7},{4,8},{5,9},{6,10},{7,11},{8,12},{9,13},{1... | collective-permute-start | bytes 98312 | tf_op jit(solution)/shard_map/ppermute | solution.py:252
  59.7 5.4 %collective-permute-start.8 = (f32[64,128]{1,0:T(8,128)S(1)}, f32[64,128]{1,0:T(8,128)S(1)}, u32[]{:S(2)}, u32[]{:S(2)}) collective-permute-start(f32[64,128]{1,0:T(8,128)S(1)} %get-tuple-element.30), channel_id=1, source_target_pairs={{0,8},{1,9},{2,10},{3,11},{4,12},{5,13},{6,14},{7,15},{8,0},{9,1},... | collective-permute-start | bytes 98312 | tf_op jit(solution)/shard_map/ppermute | solution.py:252
  62.1 3.9 %collective-permute-start.9 = (f32[64,128]{1,0:T(8,128)S(1)}, f32[64,128]{1,0:T(8,128)S(1)}, u32[]{:S(2)}, u32[]{:S(2)}) collective-permute-start(f32[64,128]{1,0:T(8,128)S(1)} %get-tuple-element.31), channel_id=1, source_target_pairs={{0,12},{1,13},{2,14},{3,15},{4,0},{5,1},{6,2},{7,3},{8,4},{9,5},{1... | collective-permute-start | bytes 98312 | tf_op jit(solution)/shard_map/ppermute | solution.py:252

commit v8 on v7

--- a/solution.py
+++ b/solution.py
@@ -89,9 +89,13 @@
     return queries, current
 
 
-def finish_kernel(rowsum_ref, now_ref, income_ref, g0, g1, g2, g3, cur_ref, con_ref):
+def finish_kernel(where_ref, counts_ref, now_ref, income_ref, g0, g1, g2, g3, cur_ref, con_ref):
     total = ((g0[...] + g1[...]) + (g2[...] + g3[...]))[:DIM]
-    expect = total / rowsum_ref[0].astype(F32)
+    s = where_ref[0] * RING + where_ref[1]
+    rowsum = counts_ref[s, 0]
+    for t in range(1, RING * RING):
+        rowsum += counts_ref[s, t]
+    expect = total / rowsum.astype(F32)
     consumption = (BETA * expect) ** (-1.0 / GAMMA)
     value = income_ref[:, 0, :] - consumption
     share = 1.0 / (1.0 + jnp.exp(-value))
@@ -99,18 +103,18 @@
     cur_ref[:, 0, :] = (1.0 - damping) * now_ref[0:DIM, :] + damping * share
 
 
-def finish(rowsum, current, income, got):
+def finish(where, counts, current, income, got):
     vm = pl.BlockSpec(memory_space=pltpu.VMEM)
     sm = pl.BlockSpec(memory_space=pltpu.SMEM)
     flat = jax.ShapeDtypeStruct((DIM, 1, current.shape[1]), F32)
     new, consumption = pl.pallas_call(
         finish_kernel,
         out_shape=[flat, flat],
-        in_specs=[sm, vm, vm, vm, vm, vm, vm],
+        in_specs=[sm, sm] + [vm] * 6,
         out_specs=[vm, vm],
         compiler_params=pltpu.CompilerParams(vmem_limit_bytes=4 << 20),
         name="finish",
-    )(rowsum, current, income, *got)
+    )(where, counts, current, income, *got)
     return jnp.transpose(new, (1, 0, 2)), jnp.transpose(consumption, (1, 0, 2))
 
 
@@ -225,12 +229,19 @@
     return [(z * RING + y, (z + dz) % RING * RING + y) for z in range(RING) for y in range(RING)]
 
 
+def trade(sign, pick):
+    got = {}
+    for k in (2, 1, 3):
+        got[k] = lax.ppermute(pick(k), "shk", shift(sign * k))
+    return [got[k] for k in (1, 2, 3)]
+
+
 def spread(current, income):
     nq = current.shape[1]
     rest = jnp.zeros((HALF - DIM - 1, nq), F32)
     one = jnp.ones((1, nq), F32)
     own = jnp.stack([jnp.concatenate([v, one, rest], axis=0) for v in (current, income)])
-    return [own] + [lax.ppermute(own, "shk", shift(-j)) for j in range(1, RING)]
+    return [own] + trade(-1, lambda k: own)
 
 
 def per_device(savings, wealth, surplus, point_dims, point_levels, point_index, live_count, trans_counts):
@@ -244,13 +255,12 @@
     tables = (mine, lax.ppermute(mine, "pts", [(i, i ^ 1) for i in range(8)]))
     shock = lax.axis_index("shk")
     where = jnp.stack([shock // RING, shock % RING]).astype(jnp.int32)
-    rowsum = jnp.sum(lax.dynamic_index_in_dim(trans_counts, shock, 0, keepdims=False))
     (sums,) = partial_sums(True, where, trans_counts, tables, states)
-    parts = [sums] + [lax.ppermute(sums, "shk", shift(-k)) for k in range(1, RING)]
+    parts = [sums] + trade(-1, lambda k: sums)
     queries, current = advance(where, trans_counts, parts, states)
     parts = partial_sums(False, where, trans_counts, tables, queries)
-    got = [parts[0]] + [lax.ppermute(parts[j], "shk", shift(j)) for j in range(1, RING)]
-    return finish(rowsum[None], current, jnp.transpose(wealth, (1, 0, 2)), got)
+    got = [parts[0]] + trade(1, lambda k: parts[k])
+    return finish(where, trans_counts, current, jnp.transpose(wealth, (1, 0, 2)), got)
 
 
 def solution(mesh):

time: 67.5 us -> 67.7 us (level)
  transfers between devices with their start and end apart: 11 -> 11, of which waited for: 8 -> 9; matrix products, arithmetic and copies ran while one was open for 1% -> 0% of each run, Pallas kernels for 0% -> 0%
where the time goes in v8:
time: 67.7 us; the launch traced here: 67.3 us
  starting transfers between devices  25.4 us (38%)
  Pallas kernels  25.1 us (37%)
  waiting for transfers between devices  15.2 us (22%)
  between operations  1.33 us (2%)
    pallas_call x2, Pallas kernels, partial_sums(): pl.pallas_call(functools.partial(kernel, first), out_shape=shapes, in_spe...  21.1 us
    ppermute x9, starting transfers between devices, trade(): got[k] = lax.ppermute(pick(k), 'shk', shift(sign * k))  18.1 us
    ppermute x9, waiting for transfers between devices, trade(): got[k] = lax.ppermute(pick(k), 'shk', shift(sign * k))  11.2 us
    all_to_all x1, starting transfers between devices, per_device(): lax.all_to_all(blocks, ('pts', 'shk'), 0, 0, tiled=True, axis_index_group...  7.28 us
    all_to_all x1, waiting for transfers between devices, per_device(): lax.all_to_all(blocks, ('pts', 'shk'), 0, 0, tiled=True, axis_index_group...  2.09 us
    ppermute x1, waiting for transfers between devices, per_device(): tables = (mine, lax.ppermute(mine, 'pts', [(i, i ^ 1) for i in range(8)]))  1.92 us
    pallas_call x1, Pallas kernels, pack(): pl.pallas_call(pack_kernel, out_shape=jax.ShapeDtypeStruct((16, ROWS, sur...  1.79 us
    pallas_call x1, Pallas kernels, finish(): pl.pallas_call(finish_kernel, out_shape=[flat, flat], in_specs=[sm, sm] +...  1.36 us
  transfers between devices with their start and end apart: 11, of which 9 were waited for; matrix products, arithmetic and copies ran while one was open for 0% of the time, Pallas kernels for 0%

profile of v8, /device:TPU:0, one launch (start us, length us, event | category | flops | bytes accessed | tf_op | source)
XLA Modules:
  0.0 67.3 jit_solution(13025013809365087388)
XLA Ops:
  1.3 1.8 %pack_tables.1 = s16[16,72,256]{2,1,0:T(8,128)(2,1)} custom-call(s32[1,1]{1,0:T(1,128)S(6)} %copy.14.live_ref, bf16[118,256]{1,0:T(8,128)(2,1)} %bitcast.19, s32[3,1,256]{2,1,0:T(1,128)} %bitcast.20, s32[3,1,256]{2,1,0:T(1,128)} %bitcast.21, s32[3,1,256]{2,1,0:T(1,128)} %bitcast.22), custom_call_target="tpu_custom_call" | custom-call | tf_op jit(solution)/shard_map/pack_tables/pallas_call | solution.py:50
  3.1 7.3 %all-to-all-start = ((s16[16,72,256]{2,1,0:T(8,128)(2,1)}), s16[16,72,256]{2,1,0:T(8,128)(2,1)S(1)}, u32[]{:S(2)}, u32[]{:S(2)}) async-start(s16[16,72,256]{2,1,0:T(8,128)(2,1)} %pack_tables.1), calls=%async_computation | async-start | bytes 1179648 | tf_op jit(solution)/shard_map/all_to_all | solution.py:252
  10.6 2.0 %collective-permute-start.2 = (f32[2,64,128]{2,1,0:T(8,128)S(1)}, f32[2,64,128]{2,1,0:T(8,128)S(1)}, u32[]{:S(2)}, u32[]{:S(2)}) collective-permute-start(f32[2,64,128]{2,1,0:T(8,128)S(1)} %pad_maximum_fusion.q0.s0), channel_id=1, source_target_pairs={{0,4},{1,5},{2,6},{3,7},{4,8},{5,9},{6,10},{7,11},{8,12},{9,13},{1... | collective-permute-start | bytes 196616 | tf_op jit(solution)/shard_map/ppermute | solution.py:235
  12.6 3.6 %collective-permute-start.1 = (f32[2,64,128]{2,1,0:T(8,128)S(1)}, f32[2,64,128]{2,1,0:T(8,128)S(1)}, u32[]{:S(2)}, u32[]{:S(2)}) collective-permute-start(f32[2,64,128]{2,1,0:T(8,128)S(1)} %pad_maximum_fusion.q0.s0), channel_id=1, source_target_pairs={{0,8},{1,9},{2,10},{3,11},{4,12},{5,13},{6,14},{7,15},{8,0},{9,1},... | collective-permute-start | bytes 196616 | tf_op jit(solution)/shard_map/ppermute | solution.py:235
  16.2 1.0 %collective-permute-start = (f32[2,64,128]{2,1,0:T(8,128)S(1)}, f32[2,64,128]{2,1,0:T(8,128)S(1)}, u32[]{:S(2)}, u32[]{:S(2)}) collective-permute-start(f32[2,64,128]{2,1,0:T(8,128)S(1)} %pad_maximum_fusion.q0.s0), channel_id=1, source_target_pairs={{0,12},{1,13},{2,14},{3,15},{4,0},{5,1},{6,2},{7,3},{8,4},{9,5},{1... | collective-permute-start | bytes 196616 | tf_op jit(solution)/shard_map/ppermute | solution.py:235
  17.2 1.9 %collective-permute-done.1.q2.s2 = f32[2,64,128]{2,1,0:T(8,128)S(1)} collective-permute-done((f32[2,64,128]{2,1,0:T(8,128)S(1)}, f32[2,64,128]{2,1,0:T(8,128)S(1)}, u32[]{:S(2)}, u32[]{:S(2)}) %collective-permute-start.1) | collective-permute-done | bytes 65568 | tf_op jit(solution)/shard_map/ppermute | solution.py:235
  19.1 1.3 %collective-permute-done.q1.s1 = f32[2,64,128]{2,1,0:T(8,128)S(1)} collective-permute-done((f32[2,64,128]{2,1,0:T(8,128)S(1)}, f32[2,64,128]{2,1,0:T(8,128)S(1)}, u32[]{:S(2)}, u32[]{:S(2)}) %collective-permute-start) | collective-permute-done | bytes 65568 | tf_op jit(solution)/shard_map/ppermute | solution.py:235
  20.5 2.1 %all-to-all-done.tab_a = s16[16,72,256]{2,1,0:T(8,128)(2,1)S(1)} async-done(((s16[16,72,256]{2,1,0:T(8,128)(2,1)}), s16[16,72,256]{2,1,0:T(8,128)(2,1)S(1)}, u32[]{:S(2)}, u32[]{:S(2)}) %all-to-all-start) | async-done | bytes 589856 | tf_op jit(solution)/shard_map/all_to_all | solution.py:252
  22.6 1.9 %collective-permute-done.3.tab_b = s16[16,72,256]{2,1,0:T(8,128)(2,1)S(1)} collective-permute-done((s16[16,72,256]{2,1,0:T(8,128)(2,1)S(1)}, s16[16,72,256]{2,1,0:T(8,128)(2,1)S(1)}, u32[]{:S(2)}, u32[]{:S(2)}) %collective-permute-start.3) | collective-permute-done | bytes 589856 | tf_op jit(solution)/shard_map/ppermute | solution.py:255
  24.6 10.6 %euler_basis.2.p0 = f32[4,64,128]{2,1,0:T(8,128)S(1)} custom-call(s32[2]{0:T(128)S(1)} %pad_add_fusion.where_ref, s32[16,16]{1,0:T(8,128)S(1)} %copy-done, s16[16,72,256]{2,1,0:T(8,128)(2,1)S(1)} %all-to-all-done.tab_a, s16[16,72,256]{2,1,0:T(8,128)(2,1)S(1)} %collective-permute-done.3.tab_b, f32[2,64,128]{2,1,0:T(8,128)S(1)} %pad_maximum_fusion.q0.s0, ...), custom_call_target="tpu_custom_call" | custom-call | tf_op jit(solution)/shard_map/euler_basis/pallas_call | solution.py:210
  35.1 2.0 %collective-permute-start.6 = (f32[4,64,128]{2,1,0:T(8,128)S(1)}, f32[4,64,128]{2,1,0:T(8,128)S(1)}, u32[]{:S(2)}, u32[]{:S(2)}) collective-permute-start(f32[4,64,128]{2,1,0:T(8,128)S(1)} %euler_basis.2.p0), channel_id=1, source_target_pairs={{0,4},{1,5},{2,6},{3,7},{4,8},{5,9},{6,10},{7,11},{8,12},{9,13},{1... | collective-permute-start | bytes 393224 | tf_op jit(solution)/shard_map/ppermute | solution.py:235
  37.1 3.6 %collective-permute-start.5 = (f32[4,64,128]{2,1,0:T(8,128)S(1)}, f32[4,64,128]{2,1,0:T(8,128)S(1)}, u32[]{:S(2)}, u32[]{:S(2)}) collective-permute-start(f32[4,64,128]{2,1,0:T(8,128)S(1)} %euler_basis.2.p0), channel_id=1, source_target_pairs={{0,8},{1,9},{2,10},{3,11},{4,12},{5,13},{6,14},{7,15},{8,0},{9,1},... | collective-permute-start | bytes 393224 | tf_op jit(solution)/shard_map/ppermute | solution.py:235
  40.7 1.0 %collective-permute-start.4 = (f32[4,64,128]{2,1,0:T(8,128)S(1)}, f32[4,64,128]{2,1,0:T(8,128)S(1)}, u32[]{:S(2)}, u32[]{:S(2)}) collective-permute-start(f32[4,64,128]{2,1,0:T(8,128)S(1)} %euler_basis.2.p0), channel_id=1, source_target_pairs={{0,12},{1,13},{2,14},{3,15},{4,0},{5,1},{6,2},{7,3},{8,4},{9,5},{1... | collective-permute-start | bytes 393224 | tf_op jit(solution)/shard_map/ppermute | solution.py:235
  41.7 1.3 %collective-permute-done.6.p3 = f32[4,64,128]{2,1,0:T(8,128)S(1)} collective-permute-done((f32[4,64,128]{2,1,0:T(8,128)S(1)}, f32[4,64,128]{2,1,0:T(8,128)S(1)}, u32[]{:S(2)}, u32[]{:S(2)}) %collective-permute-start.6) | collective-permute-done | bytes 131104 | tf_op jit(solution)/shard_map/ppermute | solution.py:235
  43.0 4.0 %collective-permute-done.5.p2 = f32[4,64,128]{2,1,0:T(8,128)S(1)} collective-permute-done((f32[4,64,128]{2,1,0:T(8,128)S(1)}, f32[4,64,128]{2,1,0:T(8,128)S(1)}, u32[]{:S(2)}, u32[]{:S(2)}) %collective-permute-start.5) | collective-permute-done | bytes 131104 | tf_op jit(solution)/shard_map/ppermute | solution.py:235
  47.0 0.8 %advance.1 = (bf16[64,128]{1,0:T(8,128)(2,1)S(1)}, bf16[64,128]{1,0:T(8,128)(2,1)S(1)}, bf16[64,128]{1,0:T(8,128)(2,1)S(1)}, bf16[64,128]{1,0:T(8,128)(2,1)S(1)}, f32[64,128]{1,0:T(8,128)S(1)}) custom-call(s32[2]{0:T(128)S(1)} %pad_add_fusion.where_ref, s32[16,16]{1,0:T(8,128)S(1)} %copy-done, f32[4,64,128]{2,1,0:T(8,128)S(1)} %euler_basis.2.p0, ...), custom_call_target="tpu_custom_call" | custom-call | tf_op jit(solution)/shard_map/advance/pallas_call | solution.py:81
  47.8 10.6 %euler_basis.3 = (f32[64,128]{1,0:T(8,128)S(1)}, f32[64,128]{1,0:T(8,128)S(1)}, f32[64,128]{1,0:T(8,128)S(1)}, f32[64,128]{1,0:T(8,128)S(1)}) custom-call(s32[2]{0:T(128)S(1)} %pad_add_fusion.where_ref, s32[16,16]{1,0:T(8,128)S(1)} %copy-done, s16[16,72,256]{2,1,0:T(8,128)(2,1)S(1)} %all-to-all-done.tab_a, ...), custom_call_target="tpu_custom_call" | custom-call | tf_op jit(solution)/shard_map/euler_basis/pallas_call | solution.py:210
  58.4 1.3 %collective-permute-start.7 = (f32[64,128]{1,0:T(8,128)S(1)}, f32[64,128]{1,0:T(8,128)S(1)}, u32[]{:S(2)}, u32[]{:S(2)}) collective-permute-start(f32[64,128]{1,0:T(8,128)S(1)} %get-tuple-element.29), channel_id=1, source_target_pairs={{0,4},{1,5},{2,6},{3,7},{4,8},{5,9},{6,10},{7,11},{8,12},{9,13},{1... | collective-permute-start | bytes 98312 | tf_op jit(solution)/shard_map/ppermute | solution.py:235
  59.7 2.4 %collective-permute-start.8 = (f32[64,128]{1,0:T(8,128)S(1)}, f32[64,128]{1,0:T(8,128)S(1)}, u32[]{:S(2)}, u32[]{:S(2)}) collective-permute-start(f32[64,128]{1,0:T(8,128)S(1)} %get-tuple-element.30), channel_id=1, source_target_pairs={{0,8},{1,9},{2,10},{3,11},{4,12},{5,13},{6,14},{7,15},{8,0},{9,1},... | collective-permute-start | bytes 98312 | tf_op jit(solution)/shard_map/ppermute | solution.py:235
  62.1 1.2 %collective-permute-start.9 = (f32[64,128]{1,0:T(8,128)S(1)}, f32[64,128]{1,0:T(8,128)S(1)}, u32[]{:S(2)}, u32[]{:S(2)}) collective-permute-start(f32[64,128]{1,0:T(8,128)S(1)} %get-tuple-element.31), channel_id=1, source_target_pairs={{0,12},{1,13},{2,14},{3,15},{4,0},{5,1},{6,2},{7,3},{8,4},{9,5},{1... | collective-permute-start | bytes 98312 | tf_op jit(solution)/shard_map/ppermute | solution.py:235
  63.3 0.6 collective-permute-done.7.g1
  63.9 1.2 %collective-permute-done.8.g2 = f32[64,128]{1,0:T(8,128)S(1)} collective-permute-done((f32[64,128]{1,0:T(8,128)S(1)}, f32[64,128]{1,0:T(8,128)S(1)}, u32[]{:S(2)}, u32[]{:S(2)}) %collective-permute-start.8) | collective-permute-done | bytes 32800 | tf_op jit(solution)/shard_map/ppermute | solution.py:235
  65.1 0.9 %collective-permute-done.9.g3 = f32[64,128]{1,0:T(8,128)S(1)} collective-permute-done((f32[64,128]{1,0:T(8,128)S(1)}, f32[64,128]{1,0:T(8,128)S(1)}, u32[]{:S(2)}, u32[]{:S(2)}) %collective-permute-start.9) | collective-permute-done | bytes 32800 | tf_op jit(solution)/shard_map/ppermute | solution.py:235
  66.0 1.4 %finish.1 = (f32[59,1,128]{2,1,0:T(1,128)}, f32[59,1,128]{2,1,0:T(1,128)}) custom-call(s32[2]{0:T(128)S(1)} %pad_add_fusion.where_ref, s32[16,16]{1,0:T(8,128)S(1)} %copy-done, f32[64,128]{1,0:T(8,128)S(1)} %get-tuple-element.23.now_ref, f32[59,1,128]{2,1,0:T(1,128)S(1)} %bitcast.18, f32[64,128]{1,0:T(8,128)S(1)} %get-tuple-element.28.g0, ...), custom_call_target="tpu_custom_call" | custom-call | tf_op jit(solution)/shard_map/finish/pallas_call | solution.py:110
  (16 shorter events, 0.3 us)
Async XLA Ops:
  3.1 7.4 %copy-start.1 = (f32[1,59,128]{2,0,1:T(1,128)S(1)}, f32[1,59,128]{2,0,1:T(1,128)}, u32[]{:S(2)}) copy-start(f32[1,59,128]{2,0,1:T(1,128)} %param.9) | copy-start | bytes 90628
  3.1 7.4 %copy-start.2 = (f32[1,59,128]{2,0,1:T(1,128)S(1)}, f32[1,59,128]{2,0,1:T(1,128)}, u32[]{:S(2)}) copy-start(f32[1,59,128]{2,0,1:T(1,128)} %param.8) | copy-start | bytes 90628
  3.1 19.5 %all-to-all-start = ((s16[16,72,256]{2,1,0:T(8,128)(2,1)}), s16[16,72,256]{2,1,0:T(8,128)(2,1)S(1)}, u32[]{:S(2)}, u32[]{:S(2)}) async-start(s16[16,72,256]{2,1,0:T(8,128)(2,1)} %pack_tables.1), calls=%async_computation | async-start | bytes 1179648 | tf_op jit(solution)/shard_map/all_to_all | solution.py:252
  10.6 6.6 %collective-permute-start.2 = (f32[2,64,128]{2,1,0:T(8,128)S(1)}, f32[2,64,128]{2,1,0:T(8,128)S(1)}, u32[]{:S(2)}, u32[]{:S(2)}) collective-permute-start(f32[2,64,128]{2,1,0:T(8,128)S(1)} %pad_maximum_fusion.q0.s0), channel_id=1, source_target_pairs={{0,4},{1,5},{2,6},{3,7},{4,8},{5,9},{6,10},{7,11},{8,12},{9,13},{1... | collective-permute-start | bytes 196616 | tf_op jit(solution)/shard_map/ppermute | solution.py:235
  12.6 6.5 %collective-permute-start.1 = (f32[2,64,128]{2,1,0:T(8,128)S(1)}, f32[2,64,128]{2,1,0:T(8,128)S(1)}, u32[]{:S(2)}, u32[]{:S(2)}) collective-permute-start(f32[2,64,128]{2,1,0:T(8,128)S(1)} %pad_maximum_fusion.q0.s0), channel_id=1, source_target_pairs={{0,8},{1,9},{2,10},{3,11},{4,12},{5,13},{6,14},{7,15},{8,0},{9,1},... | collective-permute-start | bytes 196616 | tf_op jit(solution)/shard_map/ppermute | solution.py:235
  16.2 4.3 %collective-permute-start = (f32[2,64,128]{2,1,0:T(8,128)S(1)}, f32[2,64,128]{2,1,0:T(8,128)S(1)}, u32[]{:S(2)}, u32[]{:S(2)}) collective-permute-start(f32[2,64,128]{2,1,0:T(8,128)S(1)} %pad_maximum_fusion.q0.s0), channel_id=1, source_target_pairs={{0,12},{1,13},{2,14},{3,15},{4,0},{5,1},{6,2},{7,3},{8,4},{9,5},{1... | collective-permute-start | bytes 196616 | tf_op jit(solution)/shard_map/ppermute | solution.py:235
  22.5 2.0 %collective-permute-start.3 = (s16[16,72,256]{2,1,0:T(8,128)(2,1)S(1)}, s16[16,72,256]{2,1,0:T(8,128)(2,1)S(1)}, u32[]{:S(2)}, u32[]{:S(2)}) collective-permute-start(s16[16,72,256]{2,1,0:T(8,128)(2,1)S(1)} %all-to-all-done.tab_a), channel_id=1, source_target_pairs={{0,16},{16,0},{32,48},{48,32},{64,80},{80,64},{96,112},{112,96},{1... | collective-permute-start | bytes 1769480 | tf_op jit(solution)/shard_map/ppermute | solution.py:255
  22.6 2.0 %copy-start = (s32[16,16]{1,0:T(8,128)S(1)}, s32[16,16]{1,0:T(8,128)}, u32[]{:S(2)}) copy-start(s32[16,16]{1,0:T(8,128)} %counts_ref.7) | copy-start | bytes 3076
  35.1 7.9 %collective-permute-start.6 = (f32[4,64,128]{2,1,0:T(8,128)S(1)}, f32[4,64,128]{2,1,0:T(8,128)S(1)}, u32[]{:S(2)}, u32[]{:S(2)}) collective-permute-start(f32[4,64,128]{2,1,0:T(8,128)S(1)} %euler_basis.2.p0), channel_id=1, source_target_pairs={{0,4},{1,5},{2,6},{3,7},{4,8},{5,9},{6,10},{7,11},{8,12},{9,13},{1... | collective-permute-start | bytes 393224 | tf_op jit(solution)/shard_map/ppermute | solution.py:235
  37.1 9.9 %collective-permute-start.5 = (f32[4,64,128]{2,1,0:T(8,128)S(1)}, f32[4,64,128]{2,1,0:T(8,128)S(1)}, u32[]{:S(2)}, u32[]{:S(2)}) collective-permute-start(f32[4,64,128]{2,1,0:T(8,128)S(1)} %euler_basis.2.p0), channel_id=1, source_target_pairs={{0,8},{1,9},{2,10},{3,11},{4,12},{5,13},{6,14},{7,15},{8,0},{9,1},... | collective-permute-start | bytes 393224 | tf_op jit(solution)/shard_map/ppermute | solution.py:235
  40.7 6.3 %collective-permute-start.4 = (f32[4,64,128]{2,1,0:T(8,128)S(1)}, f32[4,64,128]{2,1,0:T(8,128)S(1)}, u32[]{:S(2)}, u32[]{:S(2)}) collective-permute-start(f32[4,64,128]{2,1,0:T(8,128)S(1)} %euler_basis.2.p0), channel_id=1, source_target_pairs={{0,12},{1,13},{2,14},{3,15},{4,0},{5,1},{6,2},{7,3},{8,4},{9,5},{1... | collective-permute-start | bytes 393224 | tf_op jit(solution)/shard_map/ppermute | solution.py:235
  58.4 5.5 %collective-permute-start.7 = (f32[64,128]{1,0:T(8,128)S(1)}, f32[64,128]{1,0:T(8,128)S(1)}, u32[]{:S(2)}, u32[]{:S(2)}) collective-permute-start(f32[64,128]{1,0:T(8,128)S(1)} %get-tuple-element.29), channel_id=1, source_target_pairs={{0,4},{1,5},{2,6},{3,7},{4,8},{5,9},{6,10},{7,11},{8,12},{9,13},{1... | collective-permute-start | bytes 98312 | tf_op jit(solution)/shard_map/ppermute | solution.py:235
  59.7 5.4 %collective-permute-start.8 = (f32[64,128]{1,0:T(8,128)S(1)}, f32[64,128]{1,0:T(8,128)S(1)}, u32[]{:S(2)}, u32[]{:S(2)}) collective-permute-start(f32[64,128]{1,0:T(8,128)S(1)} %get-tuple-element.30), channel_id=1, source_target_pairs={{0,8},{1,9},{2,10},{3,11},{4,12},{5,13},{6,14},{7,15},{8,0},{9,1},... | collective-permute-start | bytes 98312 | tf_op jit(solution)/shard_map/ppermute | solution.py:235
  62.1 3.9 %collective-permute-start.9 = (f32[64,128]{1,0:T(8,128)S(1)}, f32[64,128]{1,0:T(8,128)S(1)}, u32[]{:S(2)}, u32[]{:S(2)}) collective-permute-start(f32[64,128]{1,0:T(8,128)S(1)} %get-tuple-element.31), channel_id=1, source_target_pairs={{0,12},{1,13},{2,14},{3,15},{4,0},{5,1},{6,2},{7,3},{8,4},{9,5},{1... | collective-permute-start | bytes 98312 | tf_op jit(solution)/shard_map/ppermute | solution.py:235

commit v9 on v8

--- a/solution.py
+++ b/solution.py
@@ -15,6 +15,7 @@
 RING = 4
 UNIT = 2
 ROWS = 72
+WIDTH = 2560
 STEP = 0.375 / 32768
 BF = jnp.bfloat16
 F32 = jnp.float32
@@ -29,7 +30,7 @@
     wide_ref[0 : 2 * DIM, :] = surplus_ref[...].astype(F32)
     exponent = wide_ref[DIM : 2 * DIM, :] - GAMMA * wide_ref[0:DIM, :]
     steps = jnp.clip(jnp.floor(exponent * (1.0 / STEP) + 0.5), -32767.0, 32767.0)
-    wide_ref[0:DIM, :] = jnp.where(kept, steps, 0.0)
+    wide_ref[0:DIM, :] = steps
     row = lax.broadcasted_iota(jnp.int32, (16, npoints), 0) + (ROWS - 16)
     tail = jnp.where(row < DIM, wide_ref[ROWS - 16 : ROWS, :], 0.0)
     for k in range(3):
@@ -39,8 +40,8 @@
         bias = jnp.where(refined, 1 - index_ref[k], 1).astype(F32)
         for place, value in ((DIM + k, dims_ref[k].astype(F32)), (DIM + 3 + k, scale), (DIM + 6 + k, bias)):
             tail = jnp.where(row == place, value, tail)
-    wide_ref[ROWS - 16 : ROWS, :] = tail
-    block = wide_ref[0:ROWS, :].astype(jnp.int32).astype(jnp.int16)
+    wide_ref[ROWS - 16 : ROWS, :] = jnp.where(row == DIM + 9, live_ref[...].astype(F32), tail)
+    block = jnp.where(kept, wide_ref[0:ROWS, :], 0.0).astype(jnp.int32).astype(jnp.int16)
     for g in range(o_ref.shape[0]):
         o_ref[g] = block
 
@@ -118,10 +119,38 @@
     return jnp.transpose(new, (1, 0, 2)), jnp.transpose(consumption, (1, 0, 2))
 
 
+def compact(tab_a, tab_b, unit_ref, o_ref):
+    o_ref[...] = jnp.zeros_like(o_ref)
+    blocks = [[(tab_ref, x * RING + t) for x in range(RING) for tab_ref in (tab_a, tab_b)] for t in range(RING)]
+    lives = [
+        [jnp.max(ref[i, ROWS - 8 : ROWS, 0:128].astype(jnp.int32).astype(F32)[DIM + 17 - ROWS]) for ref, i in row]
+        for row in blocks
+    ]
+    offsets = [jnp.int32(0)] * RING
+    for n in range(2 * RING):
+        for t in range(RING):
+            ref, i = blocks[t][n]
+            block = ref[i].astype(jnp.int32).astype(F32)
+            wide = jnp.concatenate([block, jnp.zeros((ROWS, 128), F32)], axis=1)
+            lanes = pl.ds(pl.multiple_of(offsets[t] // 128 * 128, 128), 384)
+            o_ref[t, :, lanes] += pltpu.roll(wide, offsets[t] % 128, 1)
+            offsets[t] = offsets[t] + lives[t][n].astype(jnp.int32)
+    count = jnp.int32(0)
+    for t in range(RING):
+        for part in range(RING):
+            unit_ref[2 * (count + part)] = jnp.int32(t)
+            unit_ref[2 * (count + part) + 1] = jnp.int32(512 * part)
+        count = count + (offsets[t] + 511) // 512
+    unit_ref[2 * count] = jnp.int32(0)
+    unit_ref[2 * count + 1] = jnp.int32(2048)
+    return count + count % 2
+
+
 def kernel(
     first, where_ref, counts_ref, tab_a, tab_b, q0, q1, q2, q3, *refs
 ):
-    outs, (qt_ref, sel_a, sel_b, basis_a, basis_b, acc_ref) = refs[:-6], refs[-6:]
+    outs, (qt_ref, sel_a, sel_b, basis_a, basis_b, acc_ref, unit_ref, tab_ref) = refs[:-8], refs[-8:]
+    units = compact(tab_a, tab_b, unit_ref, tab_ref)
     z, y = where_ref[0], where_ref[1]
     for j, q in enumerate((q0, q1, q2, q3)):
         whole = (q[0] if first else q[...]).astype(BF).astype(F32)
@@ -129,18 +158,18 @@
         high = whole.astype(F8).astype(F32)
         qt_ref[pl.ds(j * 128, 128), :] = jnp.concatenate([high, whole - high], axis=0).T.astype(F8)
     row = lax.broadcasted_iota(jnp.int32, (HALF, 256), 0)
-    units = 8 * RING // UNIT
-
-    def block(u, b):
-        return (tab_a, tab_b)[b][(u % RING) * RING + u // RING]
+
+    def block(u, b, rows):
+        lanes = pl.ds(pl.multiple_of(unit_ref[2 * u + 1] + b * 256, 128), 256)
+        return tab_ref[unit_ref[2 * u], rows, lanes]
 
     def select(u, sel_ref):
         for b in range(UNIT):
-            par = block(jnp.minimum(u, units - 1), b)[ROWS - 16 : ROWS].astype(jnp.int32)
+            par = block(jnp.minimum(u, units - 1), b, slice(ROWS - 16, ROWS))
             for k in range(3):
-                dim = par[3 + k : 4 + k]
-                scale = par[6 + k : 7 + k].astype(F32) * (1.0 / SPLIT)
-                bias = par[9 + k : 10 + k].astype(F32)
+                dim = par[3 + k : 4 + k].astype(jnp.int32)
+                scale = par[6 + k : 7 + k] * (1.0 / SPLIT)
+                bias = par[9 + k : 10 + k]
                 table = jnp.where(row == dim, scale, jnp.where(row == DIM, bias, 0.0)).astype(F8)
                 sel_ref[b, k, 0:HALF, :] = table
                 sel_ref[b, k, HALF : 2 * HALF, :] = table
@@ -155,14 +184,13 @@
                 basis = factor if basis is None else basis * factor
             basis_ref[:, pl.ds(b * 256, 256)] = jnp.maximum(basis.astype(BF), BF(0.0))
 
-    def halves(blk):
-        steps = blk[0:HALF].astype(jnp.int32).astype(F32)
+    def halves(steps):
         high = steps.astype(BF)
         return jnp.concatenate([high, (steps - high.astype(F32)).astype(BF)], axis=0)
 
     def sums(u, basis_ref):
-        weights = jnp.concatenate([halves(block(u, b)) for b in range(UNIT)], axis=1)
-        acc_ref[u // RING] += lax.dot_general(
+        weights = jnp.concatenate([halves(block(u, b, slice(0, HALF))) for b in range(UNIT)], axis=1)
+        acc_ref[unit_ref[2 * u]] += lax.dot_general(
             basis_ref[...], weights, (((1,), (1,)), ((), ())), preferred_element_type=F32
         )
 
@@ -219,6 +247,8 @@
             pltpu.VMEM((512, UNIT * 256), BF),
             pltpu.VMEM((512, UNIT * 256), BF),
             pltpu.VMEM((RING, 512, 128), F32),
+            pltpu.SMEM((40,), jnp.int32),
+            pltpu.VMEM((RING, ROWS, WIDTH), F32),
         ],
         compiler_params=pltpu.CompilerParams(vmem_limit_bytes=40 << 20),
         name="euler_basis",

time: 67.7 us -> 65.4 us (0.966)
  Pallas kernels: 25.1 us -> 22.8 us
    pallas_call x2, Pallas kernels: 21.1 us -> 18.8 us  [partial_sums(): pl.pallas_call(functools.partial(kernel, first), out_shape=shapes, in_spe...]
where the time goes in v9:
time: 65.4 us; the launch traced here: 65.1 us
  starting transfers between devices  25.4 us (39%)
  Pallas kernels  22.8 us (35%)
  waiting for transfers between devices  15.2 us (23%)
  between operations  1.32 us (2%)
    pallas_call x2, Pallas kernels, partial_sums(): pl.pallas_call(functools.partial(kernel, first), out_shape=shapes, in_spe...  18.8 us
    ppermute x9, starting transfers between devices, trade(): got[k] = lax.ppermute(pick(k), 'shk', shift(sign * k))  18.1 us
    ppermute x9, waiting for transfers between devices, trade(): got[k] = lax.ppermute(pick(k), 'shk', shift(sign * k))  11.2 us
    all_to_all x1, starting transfers between devices, per_device(): lax.all_to_all(blocks, ('pts', 'shk'), 0, 0, tiled=True, axis_index_group...  7.28 us
    all_to_all x1, waiting for transfers between devices, per_device(): lax.all_to_all(blocks, ('pts', 'shk'), 0, 0, tiled=True, axis_index_group...  2.09 us
    ppermute x1, waiting for transfers between devices, per_device(): tables = (mine, lax.ppermute(mine, 'pts', [(i, i ^ 1) for i in range(8)]))  1.92 us
    pallas_call x1, Pallas kernels, pack(): pl.pallas_call(pack_kernel, out_shape=jax.ShapeDtypeStruct((16, ROWS, sur...  1.79 us
    pallas_call x1, Pallas kernels, finish(): pl.pallas_call(finish_kernel, out_shape=[flat, flat], in_specs=[sm, sm] +...  1.36 us
  transfers between devices with their start and end apart: 11, of which 9 were waited for; matrix products, arithmetic and copies ran while one was open for 0% of the time, Pallas kernels for 0%

profile of v9, /device:TPU:0, one launch (start us, length us, event | category | flops | bytes accessed | tf_op | source)
XLA Modules:
  0.0 65.1 jit_solution(3364720202012429516)
XLA Ops:
  1.3 1.8 %pack_tables.1 = s16[16,72,256]{2,1,0:T(8,128)(2,1)} custom-call(s32[1,1]{1,0:T(1,128)S(6)} %copy.14.live_ref, bf16[118,256]{1,0:T(8,128)(2,1)} %bitcast.19, s32[3,1,256]{2,1,0:T(1,128)} %bitcast.20, s32[3,1,256]{2,1,0:T(1,128)} %bitcast.21, s32[3,1,256]{2,1,0:T(1,128)} %bitcast.22), custom_call_target="tpu_custom_call" | custom-call | tf_op jit(solution)/shard_map/pack_tables/pallas_call | solution.py:51
  3.1 7.3 %all-to-all-start = ((s16[16,72,256]{2,1,0:T(8,128)(2,1)}), s16[16,72,256]{2,1,0:T(8,128)(2,1)S(1)}, u32[]{:S(2)}, u32[]{:S(2)}) async-start(s16[16,72,256]{2,1,0:T(8,128)(2,1)} %pack_tables.1), calls=%async_computation | async-start | bytes 1179648 | tf_op jit(solution)/shard_map/all_to_all | solution.py:282
  10.6 2.0 %collective-permute-start.2 = (f32[2,64,128]{2,1,0:T(8,128)S(1)}, f32[2,64,128]{2,1,0:T(8,128)S(1)}, u32[]{:S(2)}, u32[]{:S(2)}) collective-permute-start(f32[2,64,128]{2,1,0:T(8,128)S(1)} %pad_maximum_fusion.q0.s0), channel_id=1, source_target_pairs={{0,4},{1,5},{2,6},{3,7},{4,8},{5,9},{6,10},{7,11},{8,12},{9,13},{1... | collective-permute-start | bytes 196616 | tf_op jit(solution)/shard_map/ppermute | solution.py:265
  12.6 3.6 %collective-permute-start.1 = (f32[2,64,128]{2,1,0:T(8,128)S(1)}, f32[2,64,128]{2,1,0:T(8,128)S(1)}, u32[]{:S(2)}, u32[]{:S(2)}) collective-permute-start(f32[2,64,128]{2,1,0:T(8,128)S(1)} %pad_maximum_fusion.q0.s0), channel_id=1, source_target_pairs={{0,8},{1,9},{2,10},{3,11},{4,12},{5,13},{6,14},{7,15},{8,0},{9,1},... | collective-permute-start | bytes 196616 | tf_op jit(solution)/shard_map/ppermute | solution.py:265
  16.2 1.0 %collective-permute-start = (f32[2,64,128]{2,1,0:T(8,128)S(1)}, f32[2,64,128]{2,1,0:T(8,128)S(1)}, u32[]{:S(2)}, u32[]{:S(2)}) collective-permute-start(f32[2,64,128]{2,1,0:T(8,128)S(1)} %pad_maximum_fusion.q0.s0), channel_id=1, source_target_pairs={{0,12},{1,13},{2,14},{3,15},{4,0},{5,1},{6,2},{7,3},{8,4},{9,5},{1... | collective-permute-start | bytes 196616 | tf_op jit(solution)/shard_map/ppermute | solution.py:265
  17.2 1.9 %collective-permute-done.1.q2.s2 = f32[2,64,128]{2,1,0:T(8,128)S(1)} collective-permute-done((f32[2,64,128]{2,1,0:T(8,128)S(1)}, f32[2,64,128]{2,1,0:T(8,128)S(1)}, u32[]{:S(2)}, u32[]{:S(2)}) %collective-permute-start.1) | collective-permute-done | bytes 65568 | tf_op jit(solution)/shard_map/ppermute | solution.py:265
  19.1 1.3 %collective-permute-done.q1.s1 = f32[2,64,128]{2,1,0:T(8,128)S(1)} collective-permute-done((f32[2,64,128]{2,1,0:T(8,128)S(1)}, f32[2,64,128]{2,1,0:T(8,128)S(1)}, u32[]{:S(2)}, u32[]{:S(2)}) %collective-permute-start) | collective-permute-done | bytes 65568 | tf_op jit(solution)/shard_map/ppermute | solution.py:265
  20.5 2.1 %all-to-all-done.tab_a = s16[16,72,256]{2,1,0:T(8,128)(2,1)S(1)} async-done(((s16[16,72,256]{2,1,0:T(8,128)(2,1)}), s16[16,72,256]{2,1,0:T(8,128)(2,1)S(1)}, u32[]{:S(2)}, u32[]{:S(2)}) %all-to-all-start) | async-done | bytes 589856 | tf_op jit(solution)/shard_map/all_to_all | solution.py:282
  22.6 1.9 %collective-permute-done.3.tab_b = s16[16,72,256]{2,1,0:T(8,128)(2,1)S(1)} collective-permute-done((s16[16,72,256]{2,1,0:T(8,128)(2,1)S(1)}, s16[16,72,256]{2,1,0:T(8,128)(2,1)S(1)}, u32[]{:S(2)}, u32[]{:S(2)}) %collective-permute-start.3) | collective-permute-done | bytes 589856 | tf_op jit(solution)/shard_map/ppermute | solution.py:285
  24.6 9.4 %euler_basis.2.p0 = f32[4,64,128]{2,1,0:T(8,128)S(1)} custom-call(s32[2]{0:T(128)S(1)} %pad_add_fusion.where_ref, s32[16,16]{1,0:T(8,128)S(1)} %copy-done, s16[16,72,256]{2,1,0:T(8,128)(2,1)S(1)} %all-to-all-done.tab_a, s16[16,72,256]{2,1,0:T(8,128)(2,1)S(1)} %collective-permute-done.3.tab_b, f32[2,64,128]{2,1,0:T(8,128)S(1)} %pad_maximum_fusion.q0.s0, ...), custom_call_target="tpu_custom_call" | custom-call | tf_op jit(solution)/shard_map/euler_basis/pallas_call | solution.py:238
  34.0 0.8 %collective-permute-start.6 = (f32[4,64,128]{2,1,0:T(8,128)S(1)}, f32[4,64,128]{2,1,0:T(8,128)S(1)}, u32[]{:S(2)}, u32[]{:S(2)}) collective-permute-start(f32[4,64,128]{2,1,0:T(8,128)S(1)} %euler_basis.2.p0), channel_id=1, source_target_pairs={{0,4},{1,5},{2,6},{3,7},{4,8},{5,9},{6,10},{7,11},{8,12},{9,13},{1... | collective-permute-start | bytes 393224 | tf_op jit(solution)/shard_map/ppermute | solution.py:265
  34.8 4.7 %collective-permute-start.5 = (f32[4,64,128]{2,1,0:T(8,128)S(1)}, f32[4,64,128]{2,1,0:T(8,128)S(1)}, u32[]{:S(2)}, u32[]{:S(2)}) collective-permute-start(f32[4,64,128]{2,1,0:T(8,128)S(1)} %euler_basis.2.p0), channel_id=1, source_target_pairs={{0,8},{1,9},{2,10},{3,11},{4,12},{5,13},{6,14},{7,15},{8,0},{9,1},... | collective-permute-start | bytes 393224 | tf_op jit(solution)/shard_map/ppermute | solution.py:265
  39.5 1.0 %collective-permute-start.4 = (f32[4,64,128]{2,1,0:T(8,128)S(1)}, f32[4,64,128]{2,1,0:T(8,128)S(1)}, u32[]{:S(2)}, u32[]{:S(2)}) collective-permute-start(f32[4,64,128]{2,1,0:T(8,128)S(1)} %euler_basis.2.p0), channel_id=1, source_target_pairs={{0,12},{1,13},{2,14},{3,15},{4,0},{5,1},{6,2},{7,3},{8,4},{9,5},{1... | collective-permute-start | bytes 393224 | tf_op jit(solution)/shard_map/ppermute | solution.py:265
  40.5 1.3 %collective-permute-done.6.p3 = f32[4,64,128]{2,1,0:T(8,128)S(1)} collective-permute-done((f32[4,64,128]{2,1,0:T(8,128)S(1)}, f32[4,64,128]{2,1,0:T(8,128)S(1)}, u32[]{:S(2)}, u32[]{:S(2)}) %collective-permute-start.6) | collective-permute-done | bytes 131104 | tf_op jit(solution)/shard_map/ppermute | solution.py:265
  41.9 4.0 %collective-permute-done.5.p2 = f32[4,64,128]{2,1,0:T(8,128)S(1)} collective-permute-done((f32[4,64,128]{2,1,0:T(8,128)S(1)}, f32[4,64,128]{2,1,0:T(8,128)S(1)}, u32[]{:S(2)}, u32[]{:S(2)}) %collective-permute-start.5) | collective-permute-done | bytes 131104 | tf_op jit(solution)/shard_map/ppermute | solution.py:265
  45.9 0.8 %advance.1 = (bf16[64,128]{1,0:T(8,128)(2,1)S(1)}, bf16[64,128]{1,0:T(8,128)(2,1)S(1)}, bf16[64,128]{1,0:T(8,128)(2,1)S(1)}, bf16[64,128]{1,0:T(8,128)(2,1)S(1)}, f32[64,128]{1,0:T(8,128)S(1)}) custom-call(s32[2]{0:T(128)S(1)} %pad_add_fusion.where_ref, s32[16,16]{1,0:T(8,128)S(1)} %copy-done, f32[4,64,128]{2,1,0:T(8,128)S(1)} %euler_basis.2.p0, ...), custom_call_target="tpu_custom_call" | custom-call | tf_op jit(solution)/shard_map/advance/pallas_call | solution.py:82
  46.7 9.4 %euler_basis.3 = (f32[64,128]{1,0:T(8,128)S(1)}, f32[64,128]{1,0:T(8,128)S(1)}, f32[64,128]{1,0:T(8,128)S(1)}, f32[64,128]{1,0:T(8,128)S(1)}) custom-call(s32[2]{0:T(128)S(1)} %pad_add_fusion.where_ref, s32[16,16]{1,0:T(8,128)S(1)} %copy-done, s16[16,72,256]{2,1,0:T(8,128)(2,1)S(1)} %all-to-all-done.tab_a, ...), custom_call_target="tpu_custom_call" | custom-call | tf_op jit(solution)/shard_map/euler_basis/pallas_call | solution.py:238
  56.1 0.2 collective-permute-start.7
  56.2 3.5 %collective-permute-start.8 = (f32[64,128]{1,0:T(8,128)S(1)}, f32[64,128]{1,0:T(8,128)S(1)}, u32[]{:S(2)}, u32[]{:S(2)}) collective-permute-start(f32[64,128]{1,0:T(8,128)S(1)} %get-tuple-element.30), channel_id=1, source_target_pairs={{0,8},{1,9},{2,10},{3,11},{4,12},{5,13},{6,14},{7,15},{8,0},{9,1},... | collective-permute-start | bytes 98312 | tf_op jit(solution)/shard_map/ppermute | solution.py:265
  59.8 1.2 %collective-permute-start.9 = (f32[64,128]{1,0:T(8,128)S(1)}, f32[64,128]{1,0:T(8,128)S(1)}, u32[]{:S(2)}, u32[]{:S(2)}) collective-permute-start(f32[64,128]{1,0:T(8,128)S(1)} %get-tuple-element.31), channel_id=1, source_target_pairs={{0,12},{1,13},{2,14},{3,15},{4,0},{5,1},{6,2},{7,3},{8,4},{9,5},{1... | collective-permute-start | bytes 98312 | tf_op jit(solution)/shard_map/ppermute | solution.py:265
  61.0 0.3 collective-permute-done.7.g1
  61.3 0.7 %collective-permute-done.8.g2 = f32[64,128]{1,0:T(8,128)S(1)} collective-permute-done((f32[64,128]{1,0:T(8,128)S(1)}, f32[64,128]{1,0:T(8,128)S(1)}, u32[]{:S(2)}, u32[]{:S(2)}) %collective-permute-start.8) | collective-permute-done | bytes 32800 | tf_op jit(solution)/shard_map/ppermute | solution.py:265
  62.0 1.7 %collective-permute-done.9.g3 = f32[64,128]{1,0:T(8,128)S(1)} collective-permute-done((f32[64,128]{1,0:T(8,128)S(1)}, f32[64,128]{1,0:T(8,128)S(1)}, u32[]{:S(2)}, u32[]{:S(2)}) %collective-permute-start.9) | collective-permute-done | bytes 32800 | tf_op jit(solution)/shard_map/ppermute | solution.py:265
  63.7 1.4 %finish.1 = (f32[59,1,128]{2,1,0:T(1,128)}, f32[59,1,128]{2,1,0:T(1,128)}) custom-call(s32[2]{0:T(128)S(1)} %pad_add_fusion.where_ref, s32[16,16]{1,0:T(8,128)S(1)} %copy-done, f32[64,128]{1,0:T(8,128)S(1)} %get-tuple-element.23.now_ref, f32[59,1,128]{2,1,0:T(1,128)S(1)} %bitcast.18, f32[64,128]{1,0:T(8,128)S(1)} %get-tuple-element.28.g0, ...), custom_call_target="tpu_custom_call" | custom-call | tf_op jit(solution)/shard_map/finish/pallas_call | solution.py:111
  (16 shorter events, 0.3 us)
Async XLA Ops:
  3.1 7.4 %copy-start.1 = (f32[1,59,128]{2,0,1:T(1,128)S(1)}, f32[1,59,128]{2,0,1:T(1,128)}, u32[]{:S(2)}) copy-start(f32[1,59,128]{2,0,1:T(1,128)} %param.9) | copy-start | bytes 90628
  3.1 7.4 %copy-start.2 = (f32[1,59,128]{2,0,1:T(1,128)S(1)}, f32[1,59,128]{2,0,1:T(1,128)}, u32[]{:S(2)}) copy-start(f32[1,59,128]{2,0,1:T(1,128)} %param.8) | copy-start | bytes 90628
  3.1 19.5 %all-to-all-start = ((s16[16,72,256]{2,1,0:T(8,128)(2,1)}), s16[16,72,256]{2,1,0:T(8,128)(2,1)S(1)}, u32[]{:S(2)}, u32[]{:S(2)}) async-start(s16[16,72,256]{2,1,0:T(8,128)(2,1)} %pack_tables.1), calls=%async_computation | async-start | bytes 1179648 | tf_op jit(solution)/shard_map/all_to_all | solution.py:282
  10.6 6.6 %collective-permute-start.2 = (f32[2,64,128]{2,1,0:T(8,128)S(1)}, f32[2,64,128]{2,1,0:T(8,128)S(1)}, u32[]{:S(2)}, u32[]{:S(2)}) collective-permute-start(f32[2,64,128]{2,1,0:T(8,128)S(1)} %pad_maximum_fusion.q0.s0), channel_id=1, source_target_pairs={{0,4},{1,5},{2,6},{3,7},{4,8},{5,9},{6,10},{7,11},{8,12},{9,13},{1... | collective-permute-start | bytes 196616 | tf_op jit(solution)/shard_map/ppermute | solution.py:265
  12.6 6.5 %collective-permute-start.1 = (f32[2,64,128]{2,1,0:T(8,128)S(1)}, f32[2,64,128]{2,1,0:T(8,128)S(1)}, u32[]{:S(2)}, u32[]{:S(2)}) collective-permute-start(f32[2,64,128]{2,1,0:T(8,128)S(1)} %pad_maximum_fusion.q0.s0), channel_id=1, source_target_pairs={{0,8},{1,9},{2,10},{3,11},{4,12},{5,13},{6,14},{7,15},{8,0},{9,1},... | collective-permute-start | bytes 196616 | tf_op jit(solution)/shard_map/ppermute | solution.py:265
  16.2 4.3 %collective-permute-start = (f32[2,64,128]{2,1,0:T(8,128)S(1)}, f32[2,64,128]{2,1,0:T(8,128)S(1)}, u32[]{:S(2)}, u32[]{:S(2)}) collective-permute-start(f32[2,64,128]{2,1,0:T(8,128)S(1)} %pad_maximum_fusion.q0.s0), channel_id=1, source_target_pairs={{0,12},{1,13},{2,14},{3,15},{4,0},{5,1},{6,2},{7,3},{8,4},{9,5},{1... | collective-permute-start | bytes 196616 | tf_op jit(solution)/shard_map/ppermute | solution.py:265
  22.6 2.0 %collective-permute-start.3 = (s16[16,72,256]{2,1,0:T(8,128)(2,1)S(1)}, s16[16,72,256]{2,1,0:T(8,128)(2,1)S(1)}, u32[]{:S(2)}, u32[]{:S(2)}) collective-permute-start(s16[16,72,256]{2,1,0:T(8,128)(2,1)S(1)} %all-to-all-done.tab_a), channel_id=1, source_target_pairs={{0,16},{16,0},{32,48},{48,32},{64,80},{80,64},{96,112},{112,96},{1... | collective-permute-start | bytes 1769480 | tf_op jit(solution)/shard_map/ppermute | solution.py:285
  22.6 2.0 %copy-start = (s32[16,16]{1,0:T(8,128)S(1)}, s32[16,16]{1,0:T(8,128)}, u32[]{:S(2)}) copy-start(s32[16,16]{1,0:T(8,128)} %counts_ref.7) | copy-start | bytes 3076
  34.0 7.9 %collective-permute-start.6 = (f32[4,64,128]{2,1,0:T(8,128)S(1)}, f32[4,64,128]{2,1,0:T(8,128)S(1)}, u32[]{:S(2)}, u32[]{:S(2)}) collective-permute-start(f32[4,64,128]{2,1,0:T(8,128)S(1)} %euler_basis.2.p0), channel_id=1, source_target_pairs={{0,4},{1,5},{2,6},{3,7},{4,8},{5,9},{6,10},{7,11},{8,12},{9,13},{1... | collective-permute-start | bytes 393224 | tf_op jit(solution)/shard_map/ppermute | solution.py:265
  34.8 11.0 %collective-permute-start.5 = (f32[4,64,128]{2,1,0:T(8,128)S(1)}, f32[4,64,128]{2,1,0:T(8,128)S(1)}, u32[]{:S(2)}, u32[]{:S(2)}) collective-permute-start(f32[4,64,128]{2,1,0:T(8,128)S(1)} %euler_basis.2.p0), channel_id=1, source_target_pairs={{0,8},{1,9},{2,10},{3,11},{4,12},{5,13},{6,14},{7,15},{8,0},{9,1},... | collective-permute-start | bytes 393224 | tf_op jit(solution)/shard_map/ppermute | solution.py:265
  39.5 6.3 %collective-permute-start.4 = (f32[4,64,128]{2,1,0:T(8,128)S(1)}, f32[4,64,128]{2,1,0:T(8,128)S(1)}, u32[]{:S(2)}, u32[]{:S(2)}) collective-permute-start(f32[4,64,128]{2,1,0:T(8,128)S(1)} %euler_basis.2.p0), channel_id=1, source_target_pairs={{0,12},{1,13},{2,14},{3,15},{4,0},{5,1},{6,2},{7,3},{8,4},{9,5},{1... | collective-permute-start | bytes 393224 | tf_op jit(solution)/shard_map/ppermute | solution.py:265
  56.1 5.2 %collective-permute-start.7 = (f32[64,128]{1,0:T(8,128)S(1)}, f32[64,128]{1,0:T(8,128)S(1)}, u32[]{:S(2)}, u32[]{:S(2)}) collective-permute-start(f32[64,128]{1,0:T(8,128)S(1)} %get-tuple-element.29), channel_id=1, source_target_pairs={{0,4},{1,5},{2,6},{3,7},{4,8},{5,9},{6,10},{7,11},{8,12},{9,13},{1... | collective-permute-start | bytes 98312 | tf_op jit(solution)/shard_map/ppermute | solution.py:265
  56.2 5.8 %collective-permute-start.8 = (f32[64,128]{1,0:T(8,128)S(1)}, f32[64,128]{1,0:T(8,128)S(1)}, u32[]{:S(2)}, u32[]{:S(2)}) collective-permute-start(f32[64,128]{1,0:T(8,128)S(1)} %get-tuple-element.30), channel_id=1, source_target_pairs={{0,8},{1,9},{2,10},{3,11},{4,12},{5,13},{6,14},{7,15},{8,0},{9,1},... | collective-permute-start | bytes 98312 | tf_op jit(solution)/shard_map/ppermute | solution.py:265
  59.8 3.9 %collective-permute-start.9 = (f32[64,128]{1,0:T(8,128)S(1)}, f32[64,128]{1,0:T(8,128)S(1)}, u32[]{:S(2)}, u32[]{:S(2)}) collective-permute-start(f32[64,128]{1,0:T(8,128)S(1)} %get-tuple-element.31), channel_id=1, source_target_pairs={{0,12},{1,13},{2,14},{3,15},{4,0},{5,1},{6,2},{7,3},{8,4},{9,5},{1... | collective-permute-start | bytes 98312 | tf_op jit(solution)/shard_map/ppermute | solution.py:265

commit v10 on v9

--- a/solution.py
+++ b/solution.py
@@ -143,14 +143,19 @@
         count = count + (offsets[t] + 511) // 512
     unit_ref[2 * count] = jnp.int32(0)
     unit_ref[2 * count + 1] = jnp.int32(2048)
-    return count + count % 2
+    unit_ref[39] = count + count % 2
 
 
 def kernel(
-    first, where_ref, counts_ref, tab_a, tab_b, q0, q1, q2, q3, *refs
+    first, where_ref, counts_ref, one, two, q0, q1, q2, q3, *refs
 ):
-    outs, (qt_ref, sel_a, sel_b, basis_a, basis_b, acc_ref, unit_ref, tab_ref) = refs[:-8], refs[-8:]
-    units = compact(tab_a, tab_b, unit_ref, tab_ref)
+    if first:
+        outs, unit_ref, tab_ref = refs[:1], refs[1], refs[2]
+        compact(one, two, unit_ref, tab_ref)
+    else:
+        outs, unit_ref, tab_ref = refs[:4], one, two
+    qt_ref, sel_a, sel_b, basis_a, basis_b, acc_ref = refs[-6:]
+    units = unit_ref[39]
     z, y = where_ref[0], where_ref[1]
     for j, q in enumerate((q0, q1, q2, q3)):
         whole = (q[0] if first else q[...]).astype(BF).astype(F32)
@@ -232,14 +237,20 @@
     vm = pl.BlockSpec(memory_space=pltpu.VMEM)
     sm = pl.BlockSpec(memory_space=pltpu.SMEM)
     if first:
-        shapes = [jax.ShapeDtypeStruct((RING, HALF, 128), F32)]
+        shapes = [
+            jax.ShapeDtypeStruct((RING, HALF, 128), F32),
+            jax.ShapeDtypeStruct((40,), jnp.int32),
+            jax.ShapeDtypeStruct((RING, ROWS, WIDTH), F32),
+        ]
+        places = [vm, sm, vm]
     else:
         shapes = [jax.ShapeDtypeStruct((HALF, 128), F32)] * RING
+        places = [vm] * RING
     return pl.pallas_call(
         functools.partial(kernel, first),
         out_shape=shapes,
-        in_specs=[sm, sm] + [vm] * 6,
-        out_specs=[vm] * len(shapes),
+        in_specs=[sm, sm, vm if first else sm] + [vm] * 5,
+        out_specs=places,
         scratch_shapes=[
             pltpu.VMEM((512, 2 * HALF), F8),
             pltpu.VMEM((UNIT, 3, 2 * HALF, 256), F8),
@@ -247,8 +258,6 @@
             pltpu.VMEM((512, UNIT * 256), BF),
             pltpu.VMEM((512, UNIT * 256), BF),
             pltpu.VMEM((RING, 512, 128), F32),
-            pltpu.SMEM((40,), jnp.int32),
-            pltpu.VMEM((RING, ROWS, WIDTH), F32),
         ],
         compiler_params=pltpu.CompilerParams(vmem_limit_bytes=40 << 20),
         name="euler_basis",
@@ -285,7 +294,7 @@
     tables = (mine, lax.ppermute(mine, "pts", [(i, i ^ 1) for i in range(8)]))
     shock = lax.axis_index("shk")
     where = jnp.stack([shock // RING, shock % RING]).astype(jnp.int32)
-    (sums,) = partial_sums(True, where, trans_counts, tables, states)
+    sums, *tables = partial_sums(True, where, trans_counts, tables, states)
     parts = [sums] + trade(-1, lambda k: sums)
     queries, current = advance(where, trans_counts, parts, states)
     parts = partial_sums(False, where, trans_counts, tables, queries)

time: 65.4 us -> 65.6 us (level)
  local copies, waits for them, and re-layouts: 0.17 us -> 1.63 us
  waiting for transfers between devices: 15.2 us -> 14.5 us
    unnamed x7 -> x5, local copies, waits for them, and re-layouts: 0.02 us -> 1.48 us
    all_to_all x1, waiting for transfers between devices: 2.09 us -> 1.32 us  [per_device(): lax.all_to_all(blocks, ('pts', 'shk'), 0, 0, tiled=True, axis_index_group...]
  transfers between devices with their start and end apart: 11 -> 11, of which waited for: 9 -> 9; matrix products, arithmetic and copies ran while one was open for 0% -> 2% of each run, Pallas kernels for 0% -> 0%
where the time goes in v10:
time: 65.6 us; the launch traced here: 65.2 us
  starting transfers between devices  25.2 us (38%)
  Pallas kernels  22.4 us (34%)
  waiting for transfers between devices  14.5 us (22%)
  local copies, waits for them, and re-layouts  1.63 us (2%)
  between operations  1.34 us (2%)
    pallas_call x2, Pallas kernels, partial_sums(): pl.pallas_call(functools.partial(kernel, first), out_shape=shapes, in_spe...  18.4 us
    ppermute x9, starting transfers between devices, trade(): got[k] = lax.ppermute(pick(k), 'shk', shift(sign * k))  18.1 us
    ppermute x9, waiting for transfers between devices, trade(): got[k] = lax.ppermute(pick(k), 'shk', shift(sign * k))  11.2 us
    all_to_all x1, starting transfers between devices, per_device(): lax.all_to_all(blocks, ('pts', 'shk'), 0, 0, tiled=True, axis_index_group...  7.15 us
    ppermute x1, waiting for transfers between devices, per_device(): tables = (mine, lax.ppermute(mine, 'pts', [(i, i ^ 1) for i in range(8)]))  1.93 us
    pallas_call x1, Pallas kernels, pack(): pl.pallas_call(pack_kernel, out_shape=jax.ShapeDtypeStruct((16, ROWS, sur...  1.79 us
    unnamed x5, local copies, waits for them, and re-layouts  1.48 us
    pallas_call x1, Pallas kernels, finish(): pl.pallas_call(finish_kernel, out_shape=[flat, flat], in_specs=[sm, sm] +...  1.37 us
  transfers between devices with their start and end apart: 11, of which 9 were waited for; matrix products, arithmetic and copies ran while one was open for 2% of the time, Pallas kernels for 0%

profile of v10, /device:TPU:0, one launch (start us, length us, event | category | flops | bytes accessed | tf_op | source)
XLA Modules:
  0.0 65.2 jit_solution(1330604049706175017)
XLA Ops:
  1.3 1.8 %pack_tables.1 = s16[16,72,256]{2,1,0:T(8,128)(2,1)} custom-call(s32[1,1]{1,0:T(1,128)S(6)} %copy.14.live_ref, bf16[118,256]{1,0:T(8,128)(2,1)} %bitcast.19, s32[3,1,256]{2,1,0:T(1,128)} %bitcast.20, s32[3,1,256]{2,1,0:T(1,128)} %bitcast.21, s32[3,1,256]{2,1,0:T(1,128)} %bitcast.22), custom_call_target="tpu_custom_call" | custom-call | tf_op jit(solution)/shard_map/pack_tables/pallas_call | solution.py:51
  3.1 7.1 %all-to-all-start = ((s16[16,72,256]{2,1,0:T(8,128)(2,1)}), s16[16,72,256]{2,1,0:T(8,128)(2,1)S(1)}, u32[]{:S(2)}, u32[]{:S(2)}) async-start(s16[16,72,256]{2,1,0:T(8,128)(2,1)} %pack_tables.1), calls=%async_computation | async-start | bytes 1179648 | tf_op jit(solution)/shard_map/all_to_all | solution.py:291
  10.4 0.8 %copy_bitcast_fusion = (f32[59,128]{1,0:T(8,128)S(1)}, f32[59,128]{1,0:T(8,128)S(1)}) fusion(f32[1,59,128]{2,0,1:T(1,128)} %param.9, f32[1,59,128]{2,0,1:T(1,128)} %param.8), kind=kLoop, calls=%fused_computation.3 | loop fusion | bytes 120832
  11.3 2.0 %collective-permute-start.2 = (f32[2,64,128]{2,1,0:T(8,128)S(1)}, f32[2,64,128]{2,1,0:T(8,128)S(1)}, u32[]{:S(2)}, u32[]{:S(2)}) collective-permute-start(f32[2,64,128]{2,1,0:T(8,128)S(1)} %pad_maximum_fusion.q0.s0), channel_id=1, source_target_pairs={{0,4},{1,5},{2,6},{3,7},{4,8},{5,9},{6,10},{7,11},{8,12},{9,13},{1... | collective-permute-start | bytes 196616 | tf_op jit(solution)/shard_map/ppermute | solution.py:274
  13.3 3.6 %collective-permute-start.1 = (f32[2,64,128]{2,1,0:T(8,128)S(1)}, f32[2,64,128]{2,1,0:T(8,128)S(1)}, u32[]{:S(2)}, u32[]{:S(2)}) collective-permute-start(f32[2,64,128]{2,1,0:T(8,128)S(1)} %pad_maximum_fusion.q0.s0), channel_id=1, source_target_pairs={{0,8},{1,9},{2,10},{3,11},{4,12},{5,13},{6,14},{7,15},{8,0},{9,1},... | collective-permute-start | bytes 196616 | tf_op jit(solution)/shard_map/ppermute | solution.py:274
  16.8 1.0 %collective-permute-start = (f32[2,64,128]{2,1,0:T(8,128)S(1)}, f32[2,64,128]{2,1,0:T(8,128)S(1)}, u32[]{:S(2)}, u32[]{:S(2)}) collective-permute-start(f32[2,64,128]{2,1,0:T(8,128)S(1)} %pad_maximum_fusion.q0.s0), channel_id=1, source_target_pairs={{0,12},{1,13},{2,14},{3,15},{4,0},{5,1},{6,2},{7,3},{8,4},{9,5},{1... | collective-permute-start | bytes 196616 | tf_op jit(solution)/shard_map/ppermute | solution.py:274
  17.8 1.9 %collective-permute-done.1.q2.s2 = f32[2,64,128]{2,1,0:T(8,128)S(1)} collective-permute-done((f32[2,64,128]{2,1,0:T(8,128)S(1)}, f32[2,64,128]{2,1,0:T(8,128)S(1)}, u32[]{:S(2)}, u32[]{:S(2)}) %collective-permute-start.1) | collective-permute-done | bytes 65568 | tf_op jit(solution)/shard_map/ppermute | solution.py:274
  19.8 1.3 %collective-permute-done.q1.s1 = f32[2,64,128]{2,1,0:T(8,128)S(1)} collective-permute-done((f32[2,64,128]{2,1,0:T(8,128)S(1)}, f32[2,64,128]{2,1,0:T(8,128)S(1)}, u32[]{:S(2)}, u32[]{:S(2)}) %collective-permute-start) | collective-permute-done | bytes 65568 | tf_op jit(solution)/shard_map/ppermute | solution.py:274
  21.1 1.3 %all-to-all-done.one = s16[16,72,256]{2,1,0:T(8,128)(2,1)S(1)} async-done(((s16[16,72,256]{2,1,0:T(8,128)(2,1)}), s16[16,72,256]{2,1,0:T(8,128)(2,1)S(1)}, u32[]{:S(2)}, u32[]{:S(2)}) %all-to-all-start) | async-done | bytes 589856 | tf_op jit(solution)/shard_map/all_to_all | solution.py:291
  22.5 1.9 %collective-permute-done.3.two = s16[16,72,256]{2,1,0:T(8,128)(2,1)S(1)} collective-permute-done((s16[16,72,256]{2,1,0:T(8,128)(2,1)S(1)}, s16[16,72,256]{2,1,0:T(8,128)(2,1)S(1)}, u32[]{:S(2)}, u32[]{:S(2)}) %collective-permute-start.3) | collective-permute-done | bytes 589856 | tf_op jit(solution)/shard_map/ppermute | solution.py:294
  24.4 0.7 %copy-done = s32[16,16]{1,0:T(8,128)S(1)} copy-done((s32[16,16]{1,0:T(8,128)S(1)}, s32[16,16]{1,0:T(8,128)}, u32[]{:S(2)}) %copy-start) | copy-done | bytes 1048
  25.1 9.9 %euler_basis.2 = (f32[4,64,128]{2,1,0:T(8,128)S(1)}, s32[40]{0:T(128)S(1)}, f32[4,72,2560]{2,1,0:T(8,128)S(1)}) custom-call(s32[2]{0:T(128)S(1)} %pad_add_fusion.where_ref, s32[16,16]{1,0:T(8,128)S(1)} %copy-done, s16[16,72,256]{2,1,0:T(8,128)(2,1)S(1)} %all-to-all-done.one, s16[16,72,256]{2,1,0:T(8,128)(2,1)S(1)} %collective-permute-done.3.two, ...), custom_call_target="tpu_custom_call" | custom-call | tf_op jit(solution)/shard_map/euler_basis/pallas_call | solution.py:249
  35.0 0.8 %collective-permute-start.6 = (f32[4,64,128]{2,1,0:T(8,128)S(1)}, f32[4,64,128]{2,1,0:T(8,128)S(1)}, u32[]{:S(2)}, u32[]{:S(2)}) collective-permute-start(f32[4,64,128]{2,1,0:T(8,128)S(1)} %get-tuple-element.26.p0), channel_id=1, source_target_pairs={{0,4},{1,5},{2,6},{3,7},{4,8},{5,9},{6,10},{7,11},{8,12},{9,13},{1... | collective-permute-start | bytes 393224 | tf_op jit(solution)/shard_map/ppermute | solution.py:274
  35.8 4.7 %collective-permute-start.5 = (f32[4,64,128]{2,1,0:T(8,128)S(1)}, f32[4,64,128]{2,1,0:T(8,128)S(1)}, u32[]{:S(2)}, u32[]{:S(2)}) collective-permute-start(f32[4,64,128]{2,1,0:T(8,128)S(1)} %get-tuple-element.26.p0), channel_id=1, source_target_pairs={{0,8},{1,9},{2,10},{3,11},{4,12},{5,13},{6,14},{7,15},{8,0},{9,1},... | collective-permute-start | bytes 393224 | tf_op jit(solution)/shard_map/ppermute | solution.py:274
  40.5 1.0 %collective-permute-start.4 = (f32[4,64,128]{2,1,0:T(8,128)S(1)}, f32[4,64,128]{2,1,0:T(8,128)S(1)}, u32[]{:S(2)}, u32[]{:S(2)}) collective-permute-start(f32[4,64,128]{2,1,0:T(8,128)S(1)} %get-tuple-element.26.p0), channel_id=1, source_target_pairs={{0,12},{1,13},{2,14},{3,15},{4,0},{5,1},{6,2},{7,3},{8,4},{9,5},{1... | collective-permute-start | bytes 393224 | tf_op jit(solution)/shard_map/ppermute | solution.py:274
  41.6 1.3 %collective-permute-done.6.p3 = f32[4,64,128]{2,1,0:T(8,128)S(1)} collective-permute-done((f32[4,64,128]{2,1,0:T(8,128)S(1)}, f32[4,64,128]{2,1,0:T(8,128)S(1)}, u32[]{:S(2)}, u32[]{:S(2)}) %collective-permute-start.6) | collective-permute-done | bytes 131104 | tf_op jit(solution)/shard_map/ppermute | solution.py:274
  42.9 4.0 %collective-permute-done.5.p2 = f32[4,64,128]{2,1,0:T(8,128)S(1)} collective-permute-done((f32[4,64,128]{2,1,0:T(8,128)S(1)}, f32[4,64,128]{2,1,0:T(8,128)S(1)}, u32[]{:S(2)}, u32[]{:S(2)}) %collective-permute-start.5) | collective-permute-done | bytes 131104 | tf_op jit(solution)/shard_map/ppermute | solution.py:274
  46.9 0.8 %advance.1 = (bf16[64,128]{1,0:T(8,128)(2,1)S(1)}, bf16[64,128]{1,0:T(8,128)(2,1)S(1)}, bf16[64,128]{1,0:T(8,128)(2,1)S(1)}, bf16[64,128]{1,0:T(8,128)(2,1)S(1)}, f32[64,128]{1,0:T(8,128)S(1)}) custom-call(s32[2]{0:T(128)S(1)} %pad_add_fusion.where_ref, s32[16,16]{1,0:T(8,128)S(1)} %copy-done, f32[4,64,128]{2,1,0:T(8,128)S(1)} %get-tuple-element.26.p0, ...), custom_call_target="tpu_custom_call" | custom-call | tf_op jit(solution)/shard_map/advance/pallas_call | solution.py:82
  47.7 8.6 %euler_basis.3 = (f32[64,128]{1,0:T(8,128)S(1)}, f32[64,128]{1,0:T(8,128)S(1)}, f32[64,128]{1,0:T(8,128)S(1)}, f32[64,128]{1,0:T(8,128)S(1)}) custom-call(s32[2]{0:T(128)S(1)} %pad_add_fusion.where_ref, s32[16,16]{1,0:T(8,128)S(1)} %copy-done, s32[40]{0:T(128)S(1)} %get-tuple-element.28.one, f32[4,72,2560]{2,1,0:T(8,128)S(1)} %get-tuple-element.29.two, ...), custom_call_target="tpu_custom_call" | custom-call | tf_op jit(solution)/shard_map/euler_basis/pallas_call | solution.py:249
  56.4 3.6 %collective-permute-start.8 = (f32[64,128]{1,0:T(8,128)S(1)}, f32[64,128]{1,0:T(8,128)S(1)}, u32[]{:S(2)}, u32[]{:S(2)}) collective-permute-start(f32[64,128]{1,0:T(8,128)S(1)} %get-tuple-element.36), channel_id=1, source_target_pairs={{0,8},{1,9},{2,10},{3,11},{4,12},{5,13},{6,14},{7,15},{8,0},{9,1},... | collective-permute-start | bytes 98312 | tf_op jit(solution)/shard_map/ppermute | solution.py:274
  59.9 1.3 %collective-permute-start.9 = (f32[64,128]{1,0:T(8,128)S(1)}, f32[64,128]{1,0:T(8,128)S(1)}, u32[]{:S(2)}, u32[]{:S(2)}) collective-permute-start(f32[64,128]{1,0:T(8,128)S(1)} %get-tuple-element.37), channel_id=1, source_target_pairs={{0,12},{1,13},{2,14},{3,15},{4,0},{5,1},{6,2},{7,3},{8,4},{9,5},{1... | collective-permute-start | bytes 98312 | tf_op jit(solution)/shard_map/ppermute | solution.py:274
  61.4 0.7 %collective-permute-done.8.g2 = f32[64,128]{1,0:T(8,128)S(1)} collective-permute-done((f32[64,128]{1,0:T(8,128)S(1)}, f32[64,128]{1,0:T(8,128)S(1)}, u32[]{:S(2)}, u32[]{:S(2)}) %collective-permute-start.8) | collective-permute-done | bytes 32800 | tf_op jit(solution)/shard_map/ppermute | solution.py:274
  62.2 1.7 %collective-permute-done.9.g3 = f32[64,128]{1,0:T(8,128)S(1)} collective-permute-done((f32[64,128]{1,0:T(8,128)S(1)}, f32[64,128]{1,0:T(8,128)S(1)}, u32[]{:S(2)}, u32[]{:S(2)}) %collective-permute-start.9) | collective-permute-done | bytes 32800 | tf_op jit(solution)/shard_map/ppermute | solution.py:274
  63.8 1.4 %finish.1 = (f32[59,1,128]{2,1,0:T(1,128)}, f32[59,1,128]{2,1,0:T(1,128)}) custom-call(s32[2]{0:T(128)S(1)} %pad_add_fusion.where_ref, s32[16,16]{1,0:T(8,128)S(1)} %copy-done, f32[64,128]{1,0:T(8,128)S(1)} %get-tuple-element.27.now_ref, f32[59,1,128]{2,1,0:T(1,128)S(1)} %bitcast.18, f32[64,128]{1,0:T(8,128)S(1)} %get-tuple-element.34.g0, ...), custom_call_target="tpu_custom_call" | custom-call | tf_op jit(solution)/shard_map/finish/pallas_call | solution.py:111
  (14 shorter events, 0.7 us)
Async XLA Ops:
  3.1 19.3 %all-to-all-start = ((s16[16,72,256]{2,1,0:T(8,128)(2,1)}), s16[16,72,256]{2,1,0:T(8,128)(2,1)S(1)}, u32[]{:S(2)}, u32[]{:S(2)}) async-start(s16[16,72,256]{2,1,0:T(8,128)(2,1)} %pack_tables.1), calls=%async_computation | async-start | bytes 1179648 | tf_op jit(solution)/shard_map/all_to_all | solution.py:291
  10.2 53.6 %copy-start.1 = (f32[1,59,128]{2,0,1:T(1,128)S(1)}, f32[1,59,128]{2,0,1:T(1,128)}, u32[]{:S(2)}) copy-start(f32[1,59,128]{2,0,1:T(1,128)} %param.9) | copy-start | bytes 90628
  11.3 6.6 %collective-permute-start.2 = (f32[2,64,128]{2,1,0:T(8,128)S(1)}, f32[2,64,128]{2,1,0:T(8,128)S(1)}, u32[]{:S(2)}, u32[]{:S(2)}) collective-permute-start(f32[2,64,128]{2,1,0:T(8,128)S(1)} %pad_maximum_fusion.q0.s0), channel_id=1, source_target_pairs={{0,4},{1,5},{2,6},{3,7},{4,8},{5,9},{6,10},{7,11},{8,12},{9,13},{1... | collective-permute-start | bytes 196616 | tf_op jit(solution)/shard_map/ppermute | solution.py:274
  13.3 6.5 %collective-permute-start.1 = (f32[2,64,128]{2,1,0:T(8,128)S(1)}, f32[2,64,128]{2,1,0:T(8,128)S(1)}, u32[]{:S(2)}, u32[]{:S(2)}) collective-permute-start(f32[2,64,128]{2,1,0:T(8,128)S(1)} %pad_maximum_fusion.q0.s0), channel_id=1, source_target_pairs={{0,8},{1,9},{2,10},{3,11},{4,12},{5,13},{6,14},{7,15},{8,0},{9,1},... | collective-permute-start | bytes 196616 | tf_op jit(solution)/shard_map/ppermute | solution.py:274
  16.8 4.3 %collective-permute-start = (f32[2,64,128]{2,1,0:T(8,128)S(1)}, f32[2,64,128]{2,1,0:T(8,128)S(1)}, u32[]{:S(2)}, u32[]{:S(2)}) collective-permute-start(f32[2,64,128]{2,1,0:T(8,128)S(1)} %pad_maximum_fusion.q0.s0), channel_id=1, source_target_pairs={{0,12},{1,13},{2,14},{3,15},{4,0},{5,1},{6,2},{7,3},{8,4},{9,5},{1... | collective-permute-start | bytes 196616 | tf_op jit(solution)/shard_map/ppermute | solution.py:274
  22.4 2.0 %collective-permute-start.3 = (s16[16,72,256]{2,1,0:T(8,128)(2,1)S(1)}, s16[16,72,256]{2,1,0:T(8,128)(2,1)S(1)}, u32[]{:S(2)}, u32[]{:S(2)}) collective-permute-start(s16[16,72,256]{2,1,0:T(8,128)(2,1)S(1)} %all-to-all-done.one), channel_id=1, source_target_pairs={{0,16},{16,0},{32,48},{48,32},{64,80},{80,64},{96,112},{112,96},{1... | collective-permute-start | bytes 1769480 | tf_op jit(solution)/shard_map/ppermute | solution.py:294
  24.4 0.7 %copy-start = (s32[16,16]{1,0:T(8,128)S(1)}, s32[16,16]{1,0:T(8,128)}, u32[]{:S(2)}) copy-start(s32[16,16]{1,0:T(8,128)} %counts_ref.7) | copy-start | bytes 3076
  35.0 7.9 %collective-permute-start.6 = (f32[4,64,128]{2,1,0:T(8,128)S(1)}, f32[4,64,128]{2,1,0:T(8,128)S(1)}, u32[]{:S(2)}, u32[]{:S(2)}) collective-permute-start(f32[4,64,128]{2,1,0:T(8,128)S(1)} %get-tuple-element.26.p0), channel_id=1, source_target_pairs={{0,4},{1,5},{2,6},{3,7},{4,8},{5,9},{6,10},{7,11},{8,12},{9,13},{1... | collective-permute-start | bytes 393224 | tf_op jit(solution)/shard_map/ppermute | solution.py:274
  35.8 11.0 %collective-permute-start.5 = (f32[4,64,128]{2,1,0:T(8,128)S(1)}, f32[4,64,128]{2,1,0:T(8,128)S(1)}, u32[]{:S(2)}, u32[]{:S(2)}) collective-permute-start(f32[4,64,128]{2,1,0:T(8,128)S(1)} %get-tuple-element.26.p0), channel_id=1, source_target_pairs={{0,8},{1,9},{2,10},{3,11},{4,12},{5,13},{6,14},{7,15},{8,0},{9,1},... | collective-permute-start | bytes 393224 | tf_op jit(solution)/shard_map/ppermute | solution.py:274
  40.5 6.3 %collective-permute-start.4 = (f32[4,64,128]{2,1,0:T(8,128)S(1)}, f32[4,64,128]{2,1,0:T(8,128)S(1)}, u32[]{:S(2)}, u32[]{:S(2)}) collective-permute-start(f32[4,64,128]{2,1,0:T(8,128)S(1)} %get-tuple-element.26.p0), channel_id=1, source_target_pairs={{0,12},{1,13},{2,14},{3,15},{4,0},{5,1},{6,2},{7,3},{8,4},{9,5},{1... | collective-permute-start | bytes 393224 | tf_op jit(solution)/shard_map/ppermute | solution.py:274
  56.2 5.2 %collective-permute-start.7 = (f32[64,128]{1,0:T(8,128)S(1)}, f32[64,128]{1,0:T(8,128)S(1)}, u32[]{:S(2)}, u32[]{:S(2)}) collective-permute-start(f32[64,128]{1,0:T(8,128)S(1)} %get-tuple-element.35), channel_id=1, source_target_pairs={{0,4},{1,5},{2,6},{3,7},{4,8},{5,9},{6,10},{7,11},{8,12},{9,13},{1... | collective-permute-start | bytes 98312 | tf_op jit(solution)/shard_map/ppermute | solution.py:274
  56.4 5.8 %collective-permute-start.8 = (f32[64,128]{1,0:T(8,128)S(1)}, f32[64,128]{1,0:T(8,128)S(1)}, u32[]{:S(2)}, u32[]{:S(2)}) collective-permute-start(f32[64,128]{1,0:T(8,128)S(1)} %get-tuple-element.36), channel_id=1, source_target_pairs={{0,8},{1,9},{2,10},{3,11},{4,12},{5,13},{6,14},{7,15},{8,0},{9,1},... | collective-permute-start | bytes 98312 | tf_op jit(solution)/shard_map/ppermute | solution.py:274
  59.9 3.9 %collective-permute-start.9 = (f32[64,128]{1,0:T(8,128)S(1)}, f32[64,128]{1,0:T(8,128)S(1)}, u32[]{:S(2)}, u32[]{:S(2)}) collective-permute-start(f32[64,128]{1,0:T(8,128)S(1)} %get-tuple-element.37), channel_id=1, source_target_pairs={{0,12},{1,13},{2,14},{3,15},{4,0},{5,1},{6,2},{7,3},{8,4},{9,5},{1... | collective-permute-start | bytes 98312 | tf_op jit(solution)/shard_map/ppermute | solution.py:274

commit v11 on v10

--- a/solution.py
+++ b/solution.py
@@ -58,8 +58,8 @@
     )(live, surplus, *(jnp.transpose(v, (1, 0, 2)) for v in (dims, levels, index)))
 
 
-def advance_kernel(where_ref, counts_ref, p0, p1, p2, p3, s0, s1, s2, s3, q0, q1, q2, q3, cur_ref):
-    z, y = where_ref[0], where_ref[1]
+def advance_kernel(counts_ref, p0, p1, p2, p3, s0, s1, s2, s3, q0, q1, q2, q3, cur_ref):
+    z, y = counts_ref[16, 0], counts_ref[16, 1]
     row = lax.broadcasted_iota(jnp.int32, (HALF, 128), 0)
     for j, (state, q) in enumerate(((s0, q0), (s1, q1), (s2, q2), (s3, q3))):
         s = lax.rem(z + j, RING) * RING + y
@@ -76,23 +76,23 @@
             cur_ref[...] = new
 
 
-def advance(where, counts, parts, states):
+def advance(counts, parts, states):
     vm = pl.BlockSpec(memory_space=pltpu.VMEM)
     sm = pl.BlockSpec(memory_space=pltpu.SMEM)
     *queries, current = pl.pallas_call(
         advance_kernel,
         out_shape=[jax.ShapeDtypeStruct((HALF, 128), BF)] * RING + [jax.ShapeDtypeStruct((HALF, 128), F32)],
-        in_specs=[sm, sm] + [vm] * (2 * RING),
+        in_specs=[sm] + [vm] * (2 * RING),
         out_specs=[vm] * (RING + 1),
         compiler_params=pltpu.CompilerParams(vmem_limit_bytes=4 << 20),
         name="advance",
-    )(where, counts, *parts, *states)
+    )(counts, *parts, *states)
     return queries, current
 
 
-def finish_kernel(where_ref, counts_ref, now_ref, income_ref, g0, g1, g2, g3, cur_ref, con_ref):
+def finish_kernel(counts_ref, now_ref, income_ref, g0, g1, g2, g3, cur_ref, con_ref):
     total = ((g0[...] + g1[...]) + (g2[...] + g3[...]))[:DIM]
-    s = where_ref[0] * RING + where_ref[1]
+    s = counts_ref[16, 0] * RING + counts_ref[16, 1]
     rowsum = counts_ref[s, 0]
     for t in range(1, RING * RING):
         rowsum += counts_ref[s, t]
@@ -104,18 +104,18 @@
     cur_ref[:, 0, :] = (1.0 - damping) * now_ref[0:DIM, :] + damping * share
 
 
-def finish(where, counts, current, income, got):
+def finish(counts, current, income, got):
     vm = pl.BlockSpec(memory_space=pltpu.VMEM)
     sm = pl.BlockSpec(memory_space=pltpu.SMEM)
     flat = jax.ShapeDtypeStruct((DIM, 1, current.shape[1]), F32)
     new, consumption = pl.pallas_call(
         finish_kernel,
         out_shape=[flat, flat],
-        in_specs=[sm, sm] + [vm] * 6,
+        in_specs=[sm] + [vm] * 6,
         out_specs=[vm, vm],
         compiler_params=pltpu.CompilerParams(vmem_limit_bytes=4 << 20),
         name="finish",
-    )(where, counts, current, income, *got)
+    )(counts, current, income, *got)
     return jnp.transpose(new, (1, 0, 2)), jnp.transpose(consumption, (1, 0, 2))
 
 
@@ -147,7 +147,7 @@
 
 
 def kernel(
-    first, where_ref, counts_ref, one, two, q0, q1, q2, q3, *refs
+    first, counts_ref, one, two, q0, q1, q2, q3, *refs
 ):
     if first:
         outs, unit_ref, tab_ref = refs[:1], refs[1], refs[2]
@@ -156,7 +156,7 @@
         outs, unit_ref, tab_ref = refs[:4], one, two
     qt_ref, sel_a, sel_b, basis_a, basis_b, acc_ref = refs[-6:]
     units = unit_ref[39]
-    z, y = where_ref[0], where_ref[1]
+    z, y = counts_ref[16, 0], counts_ref[16, 1]
     for j, q in enumerate((q0, q1, q2, q3)):
         whole = (q[0] if first else q[...]).astype(BF).astype(F32)
         whole = jnp.where(lax.broadcasted_iota(jnp.int32, whole.shape, 0) < DIM, whole * SPLIT, whole)
@@ -233,7 +233,7 @@
             outs[j][...] = total.T[:HALF]
 
 
-def partial_sums(first, where, counts, tables, queries):
+def partial_sums(first, counts, tables, queries):
     vm = pl.BlockSpec(memory_space=pltpu.VMEM)
     sm = pl.BlockSpec(memory_space=pltpu.SMEM)
     if first:
@@ -249,7 +249,7 @@
     return pl.pallas_call(
         functools.partial(kernel, first),
         out_shape=shapes,
-        in_specs=[sm, sm, vm if first else sm] + [vm] * 5,
+        in_specs=[sm, vm if first else sm] + [vm] * 5,
         out_specs=places,
         scratch_shapes=[
             pltpu.VMEM((512, 2 * HALF), F8),
@@ -261,7 +261,7 @@
         ],
         compiler_params=pltpu.CompilerParams(vmem_limit_bytes=40 << 20),
         name="euler_basis",
-    )(where, counts, *tables, *queries)
+    )(counts, *tables, *queries)
 
 
 def shift(dz):
@@ -290,16 +290,17 @@
     ]
     mine = lax.all_to_all(blocks, ("pts", "shk"), 0, 0, tiled=True, axis_index_groups=groups)
     states = spread(savings[0], wealth[0])
-    mine, *states = lax.optimization_barrier((mine, *states))
+    shock = lax.axis_index("shk")
+    place = jnp.where(jnp.arange(16) == 0, shock // RING, shock % RING).astype(jnp.int32)
+    scalars = jnp.concatenate([trans_counts, place[None]], axis=0)
+    mine, scalars, *states = lax.optimization_barrier((mine, scalars, *states))
     tables = (mine, lax.ppermute(mine, "pts", [(i, i ^ 1) for i in range(8)]))
-    shock = lax.axis_index("shk")
-    where = jnp.stack([shock // RING, shock % RING]).astype(jnp.int32)
-    sums, *tables = partial_sums(True, where, trans_counts, tables, states)
+    sums, *tables = partial_sums(True, scalars, tables, states)
     parts = [sums] + trade(-1, lambda k: sums)
-    queries, current = advance(where, trans_counts, parts, states)
-    parts = partial_sums(False, where, trans_counts, tables, queries)
+    queries, current = advance(scalars, parts, states)
+    parts = partial_sums(False, scalars, tables, queries)
     got = [parts[0]] + trade(1, lambda k: parts[k])
-    return finish(where, trans_counts, current, jnp.transpose(wealth, (1, 0, 2)), got)
+    return finish(scalars, current, jnp.transpose(wealth, (1, 0, 2)), got)
 
 
 def solution(mesh):

time: 65.6 us -> 65 us (level)
  local copies, waits for them, and re-layouts: 1.63 us -> 0.93 us
  waiting for transfers between devices: 14.5 us -> 13.8 us
    concatenate x0 -> x1, other arithmetic: none -> 0.7 us  [per_device(): scalars = jnp.concatenate([trans_counts, place[None]], axis=0)]
    unnamed x5 -> x3, local copies, waits for them, and re-layouts: 1.48 us -> 0.78 us
    ppermute x9, waiting for transfers between devices: 11.2 us -> 10.5 us  [trade(): got[k] = lax.ppermute(pick(k), 'shk', shift(sign * k))]
  transfers between devices with their start and end apart: 11 -> 11, of which waited for: 9 -> 9; matrix products, arithmetic and copies ran while one was open for 2% -> 3% of each run, Pallas kernels for 0% -> 0%
where the time goes in v11:
time: 65 us; the launch traced here: 64.6 us
  starting transfers between devices  25.2 us (39%)
  Pallas kernels  22.5 us (35%)
  waiting for transfers between devices  13.8 us (21%)
  between operations  1.33 us (2%)
  local copies, waits for them, and re-layouts  0.93 us (1%)
  other arithmetic  0.79 us (1%)
    pallas_call x2, Pallas kernels, partial_sums(): pl.pallas_call(functools.partial(kernel, first), out_shape=shapes, in_spe...  18.4 us
    ppermute x9, starting transfers between devices, trade(): got[k] = lax.ppermute(pick(k), 'shk', shift(sign * k))  18.1 us
    ppermute x9, waiting for transfers between devices, trade(): got[k] = lax.ppermute(pick(k), 'shk', shift(sign * k))  10.5 us
    all_to_all x1, starting transfers between devices, per_device(): lax.all_to_all(blocks, ('pts', 'shk'), 0, 0, tiled=True, axis_index_group...  7.15 us
    ppermute x1, waiting for transfers between devices, per_device(): tables = (mine, lax.ppermute(mine, 'pts', [(i, i ^ 1) for i in range(8)]))  2 us
    pallas_call x1, Pallas kernels, pack(): pl.pallas_call(pack_kernel, out_shape=jax.ShapeDtypeStruct((16, ROWS, sur...  1.8 us
    pallas_call x1, Pallas kernels, finish(): pl.pallas_call(finish_kernel, out_shape=[flat, flat], in_specs=[sm] + [vm...  1.43 us
    all_to_all x1, waiting for transfers between devices, per_device(): lax.all_to_all(blocks, ('pts', 'shk'), 0, 0, tiled=True, axis_index_group...  1.32 us
  transfers between devices with their start and end apart: 11, of which 9 were waited for; matrix products, arithmetic and copies ran while one was open for 3% of the time, Pallas kernels for 0%

profile of v11, /device:TPU:0, one launch (start us, length us, event | category | flops | bytes accessed | tf_op | source)
XLA Modules:
  0.0 64.6 jit_solution(2218099840330831086)
XLA Ops:
  1.3 1.8 %pack_tables.1 = s16[16,72,256]{2,1,0:T(8,128)(2,1)} custom-call(s32[1,1]{1,0:T(1,128)S(6)} %copy.14.live_ref, bf16[118,256]{1,0:T(8,128)(2,1)} %bitcast.17, s32[3,1,256]{2,1,0:T(1,128)} %bitcast.18, s32[3,1,256]{2,1,0:T(1,128)} %bitcast.19, s32[3,1,256]{2,1,0:T(1,128)} %bitcast.20), custom_call_target="tpu_custom_call" | custom-call | tf_op jit(solution)/shard_map/pack_tables/pallas_call | solution.py:51
  3.1 7.1 %all-to-all-start = ((s16[16,72,256]{2,1,0:T(8,128)(2,1)}), s16[16,72,256]{2,1,0:T(8,128)(2,1)S(1)}, u32[]{:S(2)}, u32[]{:S(2)}) async-start(s16[16,72,256]{2,1,0:T(8,128)(2,1)} %pack_tables.1), calls=%async_computation | async-start | bytes 1179648 | tf_op jit(solution)/shard_map/all_to_all | solution.py:291
  10.4 0.8 %copy_bitcast_fusion = (f32[59,128]{1,0:T(8,128)S(1)}, f32[59,128]{1,0:T(8,128)S(1)}) fusion(f32[1,59,128]{2,0,1:T(1,128)} %param.9, f32[1,59,128]{2,0,1:T(1,128)} %param.8), kind=kLoop, calls=%fused_computation.3 | loop fusion | bytes 120832
  11.3 2.0 %collective-permute-start.2 = (f32[2,64,128]{2,1,0:T(8,128)S(1)}, f32[2,64,128]{2,1,0:T(8,128)S(1)}, u32[]{:S(2)}, u32[]{:S(2)}) collective-permute-start(f32[2,64,128]{2,1,0:T(8,128)S(1)} %pad_maximum_fusion.q0.s0), channel_id=1, source_target_pairs={{0,4},{1,5},{2,6},{3,7},{4,8},{5,9},{6,10},{7,11},{8,12},{9,13},{1... | collective-permute-start | bytes 196616 | tf_op jit(solution)/shard_map/ppermute | solution.py:274
  13.3 3.6 %collective-permute-start.1 = (f32[2,64,128]{2,1,0:T(8,128)S(1)}, f32[2,64,128]{2,1,0:T(8,128)S(1)}, u32[]{:S(2)}, u32[]{:S(2)}) collective-permute-start(f32[2,64,128]{2,1,0:T(8,128)S(1)} %pad_maximum_fusion.q0.s0), channel_id=1, source_target_pairs={{0,8},{1,9},{2,10},{3,11},{4,12},{5,13},{6,14},{7,15},{8,0},{9,1},... | collective-permute-start | bytes 196616 | tf_op jit(solution)/shard_map/ppermute | solution.py:274
  16.8 1.0 %collective-permute-start = (f32[2,64,128]{2,1,0:T(8,128)S(1)}, f32[2,64,128]{2,1,0:T(8,128)S(1)}, u32[]{:S(2)}, u32[]{:S(2)}) collective-permute-start(f32[2,64,128]{2,1,0:T(8,128)S(1)} %pad_maximum_fusion.q0.s0), channel_id=1, source_target_pairs={{0,12},{1,13},{2,14},{3,15},{4,0},{5,1},{6,2},{7,3},{8,4},{9,5},{1... | collective-permute-start | bytes 196616 | tf_op jit(solution)/shard_map/ppermute | solution.py:274
  17.9 0.7 %pad_add_fusion.counts_ref = s32[17,16]{1,0:T(8,128)S(1)} fusion(s32[1,16]{1,0:T(1,128)S(1)} %compare_select_fusion, s32[16,16]{1,0:T(8,128)} %param.15), kind=kLoop, calls=%fused_computation.5 | loop fusion | flops 272 | bytes 2176 | tf_op jit(solution)/shard_map/concatenate | solution.py:295
  18.6 1.2 %collective-permute-done.1.q2.s2 = f32[2,64,128]{2,1,0:T(8,128)S(1)} collective-permute-done((f32[2,64,128]{2,1,0:T(8,128)S(1)}, f32[2,64,128]{2,1,0:T(8,128)S(1)}, u32[]{:S(2)}, u32[]{:S(2)}) %collective-permute-start.1) | collective-permute-done | bytes 65568 | tf_op jit(solution)/shard_map/ppermute | solution.py:274
  19.8 1.3 %collective-permute-done.q1.s1 = f32[2,64,128]{2,1,0:T(8,128)S(1)} collective-permute-done((f32[2,64,128]{2,1,0:T(8,128)S(1)}, f32[2,64,128]{2,1,0:T(8,128)S(1)}, u32[]{:S(2)}, u32[]{:S(2)}) %collective-permute-start) | collective-permute-done | bytes 65568 | tf_op jit(solution)/shard_map/ppermute | solution.py:274
  21.1 1.3 %all-to-all-done.one = s16[16,72,256]{2,1,0:T(8,128)(2,1)S(1)} async-done(((s16[16,72,256]{2,1,0:T(8,128)(2,1)}), s16[16,72,256]{2,1,0:T(8,128)(2,1)S(1)}, u32[]{:S(2)}, u32[]{:S(2)}) %all-to-all-start) | async-done | bytes 589856 | tf_op jit(solution)/shard_map/all_to_all | solution.py:291
  22.4 2.0 %collective-permute-done.3.two = s16[16,72,256]{2,1,0:T(8,128)(2,1)S(1)} collective-permute-done((s16[16,72,256]{2,1,0:T(8,128)(2,1)S(1)}, s16[16,72,256]{2,1,0:T(8,128)(2,1)S(1)}, u32[]{:S(2)}, u32[]{:S(2)}) %collective-permute-start.3) | collective-permute-done | bytes 589856 | tf_op jit(solution)/shard_map/ppermute | solution.py:297
  24.4 9.9 %euler_basis.2 = (f32[4,64,128]{2,1,0:T(8,128)S(1)}, s32[40]{0:T(128)S(1)}, f32[4,72,2560]{2,1,0:T(8,128)S(1)}) custom-call(s32[17,16]{1,0:T(8,128)S(1)} %pad_add_fusion.counts_ref, s16[16,72,256]{2,1,0:T(8,128)(2,1)S(1)} %all-to-all-done.one, s16[16,72,256]{2,1,0:T(8,128)(2,1)S(1)} %collective-permute-done.3.two, f32[2,64,128]{2,1,0:T(8,128)S(1)} %pad_maximum_fusion.q0.s0, ...), custom_call_target="tpu_custom_call" | custom-call | tf_op jit(solution)/shard_map/euler_basis/pallas_call | solution.py:249
  34.3 0.8 %collective-permute-start.6 = (f32[4,64,128]{2,1,0:T(8,128)S(1)}, f32[4,64,128]{2,1,0:T(8,128)S(1)}, u32[]{:S(2)}, u32[]{:S(2)}) collective-permute-start(f32[4,64,128]{2,1,0:T(8,128)S(1)} %get-tuple-element.28.p0), channel_id=1, source_target_pairs={{0,4},{1,5},{2,6},{3,7},{4,8},{5,9},{6,10},{7,11},{8,12},{9,13},{1... | collective-permute-start | bytes 393224 | tf_op jit(solution)/shard_map/ppermute | solution.py:274
  35.2 4.7 %collective-permute-start.5 = (f32[4,64,128]{2,1,0:T(8,128)S(1)}, f32[4,64,128]{2,1,0:T(8,128)S(1)}, u32[]{:S(2)}, u32[]{:S(2)}) collective-permute-start(f32[4,64,128]{2,1,0:T(8,128)S(1)} %get-tuple-element.28.p0), channel_id=1, source_target_pairs={{0,8},{1,9},{2,10},{3,11},{4,12},{5,13},{6,14},{7,15},{8,0},{9,1},... | collective-permute-start | bytes 393224 | tf_op jit(solution)/shard_map/ppermute | solution.py:274
  39.9 1.0 %collective-permute-start.4 = (f32[4,64,128]{2,1,0:T(8,128)S(1)}, f32[4,64,128]{2,1,0:T(8,128)S(1)}, u32[]{:S(2)}, u32[]{:S(2)}) collective-permute-start(f32[4,64,128]{2,1,0:T(8,128)S(1)} %get-tuple-element.28.p0), channel_id=1, source_target_pairs={{0,12},{1,13},{2,14},{3,15},{4,0},{5,1},{6,2},{7,3},{8,4},{9,5},{1... | collective-permute-start | bytes 393224 | tf_op jit(solution)/shard_map/ppermute | solution.py:274
  40.9 1.3 %collective-permute-done.6.p3 = f32[4,64,128]{2,1,0:T(8,128)S(1)} collective-permute-done((f32[4,64,128]{2,1,0:T(8,128)S(1)}, f32[4,64,128]{2,1,0:T(8,128)S(1)}, u32[]{:S(2)}, u32[]{:S(2)}) %collective-permute-start.6) | collective-permute-done | bytes 131104 | tf_op jit(solution)/shard_map/ppermute | solution.py:274
  42.2 4.0 %collective-permute-done.5.p2 = f32[4,64,128]{2,1,0:T(8,128)S(1)} collective-permute-done((f32[4,64,128]{2,1,0:T(8,128)S(1)}, f32[4,64,128]{2,1,0:T(8,128)S(1)}, u32[]{:S(2)}, u32[]{:S(2)}) %collective-permute-start.5) | collective-permute-done | bytes 131104 | tf_op jit(solution)/shard_map/ppermute | solution.py:274
  46.2 0.9 %advance.1 = (bf16[64,128]{1,0:T(8,128)(2,1)S(1)}, bf16[64,128]{1,0:T(8,128)(2,1)S(1)}, bf16[64,128]{1,0:T(8,128)(2,1)S(1)}, bf16[64,128]{1,0:T(8,128)(2,1)S(1)}, f32[64,128]{1,0:T(8,128)S(1)}) custom-call(s32[17,16]{1,0:T(8,128)S(1)} %pad_add_fusion.counts_ref, f32[4,64,128]{2,1,0:T(8,128)S(1)} %get-tuple-element.28.p0, ...), custom_call_target="tpu_custom_call" | custom-call | tf_op jit(solution)/shard_map/advance/pallas_call | solution.py:82
  47.1 8.5 %euler_basis.3 = (f32[64,128]{1,0:T(8,128)S(1)}, f32[64,128]{1,0:T(8,128)S(1)}, f32[64,128]{1,0:T(8,128)S(1)}, f32[64,128]{1,0:T(8,128)S(1)}) custom-call(s32[17,16]{1,0:T(8,128)S(1)} %pad_add_fusion.counts_ref, s32[40]{0:T(128)S(1)} %get-tuple-element.30.one, f32[4,72,2560]{2,1,0:T(8,128)S(1)} %get-tuple-element.31.two, ...), custom_call_target="tpu_custom_call" | custom-call | tf_op jit(solution)/shard_map/euler_basis/pallas_call | solution.py:249
  55.8 3.5 %collective-permute-start.8 = (f32[64,128]{1,0:T(8,128)S(1)}, f32[64,128]{1,0:T(8,128)S(1)}, u32[]{:S(2)}, u32[]{:S(2)}) collective-permute-start(f32[64,128]{1,0:T(8,128)S(1)} %get-tuple-element.38), channel_id=1, source_target_pairs={{0,8},{1,9},{2,10},{3,11},{4,12},{5,13},{6,14},{7,15},{8,0},{9,1},... | collective-permute-start | bytes 98312 | tf_op jit(solution)/shard_map/ppermute | solution.py:274
  59.3 1.2 %collective-permute-start.9 = (f32[64,128]{1,0:T(8,128)S(1)}, f32[64,128]{1,0:T(8,128)S(1)}, u32[]{:S(2)}, u32[]{:S(2)}) collective-permute-start(f32[64,128]{1,0:T(8,128)S(1)} %get-tuple-element.39), channel_id=1, source_target_pairs={{0,12},{1,13},{2,14},{3,15},{4,0},{5,1},{6,2},{7,3},{8,4},{9,5},{1... | collective-permute-start | bytes 98312 | tf_op jit(solution)/shard_map/ppermute | solution.py:274
  60.8 0.7 %collective-permute-done.8.g2 = f32[64,128]{1,0:T(8,128)S(1)} collective-permute-done((f32[64,128]{1,0:T(8,128)S(1)}, f32[64,128]{1,0:T(8,128)S(1)}, u32[]{:S(2)}, u32[]{:S(2)}) %collective-permute-start.8) | collective-permute-done | bytes 32800 | tf_op jit(solution)/shard_map/ppermute | solution.py:274
  61.5 1.7 %collective-permute-done.9.g3 = f32[64,128]{1,0:T(8,128)S(1)} collective-permute-done((f32[64,128]{1,0:T(8,128)S(1)}, f32[64,128]{1,0:T(8,128)S(1)}, u32[]{:S(2)}, u32[]{:S(2)}) %collective-permute-start.9) | collective-permute-done | bytes 32800 | tf_op jit(solution)/shard_map/ppermute | solution.py:274
  63.2 1.4 %finish.1 = (f32[59,1,128]{2,1,0:T(1,128)}, f32[59,1,128]{2,1,0:T(1,128)}) custom-call(s32[17,16]{1,0:T(8,128)S(1)} %pad_add_fusion.counts_ref, f32[64,128]{1,0:T(8,128)S(1)} %get-tuple-element.29.now_ref, f32[59,1,128]{2,1,0:T(1,128)S(1)} %bitcast.16, f32[64,128]{1,0:T(8,128)S(1)} %get-tuple-element.36.g0, f32[64,128]{1,0:T(8,128)S(1)} %collective-permute-done.7.g1, ...), custom_call_target="tpu_custom_call" | custom-call | tf_op jit(solution)/shard_map/finish/pallas_call | solution.py:111
  (13 shorter events, 0.7 us)
Async XLA Ops:
  3.1 19.3 %all-to-all-start = ((s16[16,72,256]{2,1,0:T(8,128)(2,1)}), s16[16,72,256]{2,1,0:T(8,128)(2,1)S(1)}, u32[]{:S(2)}, u32[]{:S(2)}) async-start(s16[16,72,256]{2,1,0:T(8,128)(2,1)} %pack_tables.1), calls=%async_computation | async-start | bytes 1179648 | tf_op jit(solution)/shard_map/all_to_all | solution.py:291
  10.2 53.0 %copy-start = (f32[1,59,128]{2,0,1:T(1,128)S(1)}, f32[1,59,128]{2,0,1:T(1,128)}, u32[]{:S(2)}) copy-start(f32[1,59,128]{2,0,1:T(1,128)} %param.9) | copy-start | bytes 90628
  11.3 7.3 %collective-permute-start.2 = (f32[2,64,128]{2,1,0:T(8,128)S(1)}, f32[2,64,128]{2,1,0:T(8,128)S(1)}, u32[]{:S(2)}, u32[]{:S(2)}) collective-permute-start(f32[2,64,128]{2,1,0:T(8,128)S(1)} %pad_maximum_fusion.q0.s0), channel_id=1, source_target_pairs={{0,4},{1,5},{2,6},{3,7},{4,8},{5,9},{6,10},{7,11},{8,12},{9,13},{1... | collective-permute-start | bytes 196616 | tf_op jit(solution)/shard_map/ppermute | solution.py:274
  13.3 6.5 %collective-permute-start.1 = (f32[2,64,128]{2,1,0:T(8,128)S(1)}, f32[2,64,128]{2,1,0:T(8,128)S(1)}, u32[]{:S(2)}, u32[]{:S(2)}) collective-permute-start(f32[2,64,128]{2,1,0:T(8,128)S(1)} %pad_maximum_fusion.q0.s0), channel_id=1, source_target_pairs={{0,8},{1,9},{2,10},{3,11},{4,12},{5,13},{6,14},{7,15},{8,0},{9,1},... | collective-permute-start | bytes 196616 | tf_op jit(solution)/shard_map/ppermute | solution.py:274
  16.8 4.3 %collective-permute-start = (f32[2,64,128]{2,1,0:T(8,128)S(1)}, f32[2,64,128]{2,1,0:T(8,128)S(1)}, u32[]{:S(2)}, u32[]{:S(2)}) collective-permute-start(f32[2,64,128]{2,1,0:T(8,128)S(1)} %pad_maximum_fusion.q0.s0), channel_id=1, source_target_pairs={{0,12},{1,13},{2,14},{3,15},{4,0},{5,1},{6,2},{7,3},{8,4},{9,5},{1... | collective-permute-start | bytes 196616 | tf_op jit(solution)/shard_map/ppermute | solution.py:274
  22.4 2.0 %collective-permute-start.3 = (s16[16,72,256]{2,1,0:T(8,128)(2,1)S(1)}, s16[16,72,256]{2,1,0:T(8,128)(2,1)S(1)}, u32[]{:S(2)}, u32[]{:S(2)}) collective-permute-start(s16[16,72,256]{2,1,0:T(8,128)(2,1)S(1)} %all-to-all-done.one), channel_id=1, source_target_pairs={{0,16},{16,0},{32,48},{48,32},{64,80},{80,64},{96,112},{112,96},{1... | collective-permute-start | bytes 1769480 | tf_op jit(solution)/shard_map/ppermute | solution.py:297
  34.3 7.9 %collective-permute-start.6 = (f32[4,64,128]{2,1,0:T(8,128)S(1)}, f32[4,64,128]{2,1,0:T(8,128)S(1)}, u32[]{:S(2)}, u32[]{:S(2)}) collective-permute-start(f32[4,64,128]{2,1,0:T(8,128)S(1)} %get-tuple-element.28.p0), channel_id=1, source_target_pairs={{0,4},{1,5},{2,6},{3,7},{4,8},{5,9},{6,10},{7,11},{8,12},{9,13},{1... | collective-permute-start | bytes 393224 | tf_op jit(solution)/shard_map/ppermute | solution.py:274
  35.2 11.0 %collective-permute-start.5 = (f32[4,64,128]{2,1,0:T(8,128)S(1)}, f32[4,64,128]{2,1,0:T(8,128)S(1)}, u32[]{:S(2)}, u32[]{:S(2)}) collective-permute-start(f32[4,64,128]{2,1,0:T(8,128)S(1)} %get-tuple-element.28.p0), channel_id=1, source_target_pairs={{0,8},{1,9},{2,10},{3,11},{4,12},{5,13},{6,14},{7,15},{8,0},{9,1},... | collective-permute-start | bytes 393224 | tf_op jit(solution)/shard_map/ppermute | solution.py:274
  39.9 6.3 %collective-permute-start.4 = (f32[4,64,128]{2,1,0:T(8,128)S(1)}, f32[4,64,128]{2,1,0:T(8,128)S(1)}, u32[]{:S(2)}, u32[]{:S(2)}) collective-permute-start(f32[4,64,128]{2,1,0:T(8,128)S(1)} %get-tuple-element.28.p0), channel_id=1, source_target_pairs={{0,12},{1,13},{2,14},{3,15},{4,0},{5,1},{6,2},{7,3},{8,4},{9,5},{1... | collective-permute-start | bytes 393224 | tf_op jit(solution)/shard_map/ppermute | solution.py:274
  55.6 5.2 %collective-permute-start.7 = (f32[64,128]{1,0:T(8,128)S(1)}, f32[64,128]{1,0:T(8,128)S(1)}, u32[]{:S(2)}, u32[]{:S(2)}) collective-permute-start(f32[64,128]{1,0:T(8,128)S(1)} %get-tuple-element.37), channel_id=1, source_target_pairs={{0,4},{1,5},{2,6},{3,7},{4,8},{5,9},{6,10},{7,11},{8,12},{9,13},{1... | collective-permute-start | bytes 98312 | tf_op jit(solution)/shard_map/ppermute | solution.py:274
  55.8 5.8 %collective-permute-start.8 = (f32[64,128]{1,0:T(8,128)S(1)}, f32[64,128]{1,0:T(8,128)S(1)}, u32[]{:S(2)}, u32[]{:S(2)}) collective-permute-start(f32[64,128]{1,0:T(8,128)S(1)} %get-tuple-element.38), channel_id=1, source_target_pairs={{0,8},{1,9},{2,10},{3,11},{4,12},{5,13},{6,14},{7,15},{8,0},{9,1},... | collective-permute-start | bytes 98312 | tf_op jit(solution)/shard_map/ppermute | solution.py:274
  59.3 3.9 %collective-permute-start.9 = (f32[64,128]{1,0:T(8,128)S(1)}, f32[64,128]{1,0:T(8,128)S(1)}, u32[]{:S(2)}, u32[]{:S(2)}) collective-permute-start(f32[64,128]{1,0:T(8,128)S(1)} %get-tuple-element.39), channel_id=1, source_target_pairs={{0,12},{1,13},{2,14},{3,15},{4,0},{5,1},{6,2},{7,3},{8,4},{9,5},{1... | collective-permute-start | bytes 98312 | tf_op jit(solution)/shard_map/ppermute | solution.py:274
